TPU v7x, 128 devices: a whole 4x4x4 slice. The times are simulated.
128 devices in a mesh: rows: 32 (over y, z, core), rep: 4 (over x).
Axes of the slice: x: 4, y: 4, z: 4, core: 2. Of those that a mesh axis runs over, the one named last changes fastest.
Arguments:
- entity_table: float32 [65536, 400], P(('rows', 'rep')), may hold values from -3 to 3
- entity_state: float32 [65536], P(('rows', 'rep')), may hold values from 0.005 to 1
- relation_table: float32 [7424, 400], replicated, may hold values from -3 to 3
- relation_state: float32 [7424], replicated, may hold values from 0.05 to 2
- end_owner: int32 [131072, 2], P(('rows', 'rep')), may hold values from 0 to 127, all different within a row; in each aligned block of 1024 rows (0 to 1023, 1024 to 2047, ...) at most 40 rows name the same one
- end_row: int32 [131072, 2], P(('rows', 'rep')), may hold values from 0 to 511
- relation_id: int32 [131072], P(('rows', 'rep')), may hold values from 0 to 7423
- negative_owner: int32 [131072, 1], P(('rows', 'rep')), may hold values from 0 to 127; in each aligned block of 1024 rows (0 to 1023, 1024 to 2047, ...) at most 16 rows name the same one
- negative_row: int32 [131072], P(('rows', 'rep')), may hold values from 0 to 511
Outputs:
- new_entity_table: float32 [65536, 400], P(('rows', 'rep'))
- new_entity_state: float32 [65536], P(('rows', 'rep'))
- new_relation_table: float32 [7424, 400], replicated
- new_relation_state: float32 [7424], replicated
Inputs may be any that keep to these rules, and one draw needn't show every extreme that they name: `end_owner`: in each edge the head's and the tail's owners differ. Among the edges of one device no owner is named more than 40 times, heads and tails counted together; in some device some owner is named exactly 40 times. `negative_owner`: among the negatives of one group no owner is named more than 16 times; in some group some owner is named exactly 16 times.
All inputs are finite; a program needn't handle non-finite values.
Results may differ from a plain program's by a relative error of at most 0.0003.
Values sent between devices are 32-bit elements; how exact they have to be, the bound alone decides.
No kernel may reach another device: no remote copies, remote signals or barrier semaphores. Data moves between devices by JAX's collectives and lax.ppermute only.
A program may use at most 256 MiB of HBM per device.

v0:
```python
import jax
import jax.numpy as jnp
from jax import lax
from jax.sharding import PartitionSpec as P

learn_rate = 0.5
adagrad_eps = 1e-10


def adagrad(table, state, grad):
    new_state = state + jnp.mean(grad * grad, axis=1)
    new_table = table - learn_rate * grad / (jnp.sqrt(new_state)[:, None] + adagrad_eps)
    return (new_table, new_state)


def rank_within(owner, device_count):
    onehot = (owner[:, None] == jnp.arange(device_count, dtype=jnp.int32)[None, :]).astype(
        jnp.int32
    )
    earlier = jnp.cumsum(onehot, axis=0) - onehot
    return jnp.sum(earlier * onehot, axis=1)


def per_device(
    entity_table,
    entity_state,
    relation_table,
    relation_state,
    end_owner,
    end_row,
    relation_id,
    negative_owner,
    negative_row,
):
    device_count = lax.axis_size(("rows", "rep"))
    edge_count = end_owner.shape[0]
    negative_count = negative_owner.shape[0]
    feature_width = entity_table.shape[1]
    capacity = 5 * edge_count // device_count
    neg_capacity = max(2, 2 * negative_count // device_count)
    slot_count = capacity + neg_capacity
    high = lax.Precision.HIGHEST
    owners = end_owner.reshape(-1)
    end_slot = owners * slot_count + rank_within(owners, device_count)
    neg_slot = (
        negative_owner[:, 0] * slot_count
        + capacity
        + rank_within(negative_owner[:, 0], device_count)
    )
    request = jnp.zeros((device_count * slot_count,), jnp.int32)
    request = request.at[end_slot].set(end_row.reshape(-1)).at[neg_slot].set(negative_row)
    request = request.reshape(device_count, slot_count)
    wanted = lax.all_to_all(request, ("rows", "rep"), split_axis=0, concat_axis=0, tiled=True)
    looked = jnp.take(entity_table, wanted, axis=0)
    arrived = lax.all_to_all(looked, ("rows", "rep"), split_axis=0, concat_axis=0, tiled=True)
    flat_rows = arrived.reshape(device_count * slot_count, feature_width)
    pair_slot = end_slot.reshape(edge_count, 2)
    head_slot = pair_slot[:, 0]
    tail_slot = pair_slot[:, 1]
    head_rows = flat_rows[head_slot]
    tail_rows = flat_rows[tail_slot]
    neg_rows = flat_rows[neg_slot]
    rel_rows = relation_table[relation_id]
    product = head_rows * rel_rows
    positive = jnp.sum(product * tail_rows, axis=1)
    score = lax.dot_general(
        product,
        neg_rows,
        (((1,), (1,)), ((), ())),
        precision=high,
        preferred_element_type=jnp.float32,
    )
    dpos = -jax.nn.sigmoid(-positive)
    dneg = jax.nn.sigmoid(score) / negative_count
    grad_product = dpos[:, None] * tail_rows + jnp.dot(
        dneg, neg_rows, precision=high, preferred_element_type=jnp.float32
    )
    grad_tail = dpos[:, None] * product
    grad_neg = lax.dot_general(
        dneg, product, (((0,), (0,)), ((), ())), precision=high, preferred_element_type=jnp.float32
    )
    outgoing = jnp.zeros((device_count * slot_count, feature_width), jnp.float32)
    outgoing = outgoing.at[head_slot].set(grad_product * rel_rows)
    outgoing = outgoing.at[tail_slot].set(grad_tail)
    outgoing = outgoing.at[neg_slot].set(grad_neg)
    incoming = lax.all_to_all(
        outgoing.reshape(device_count, slot_count, feature_width),
        ("rows", "rep"),
        split_axis=0,
        concat_axis=0,
        tiled=True,
    )
    entity_grad = jnp.zeros(entity_table.shape, jnp.float32)
    entity_grad = entity_grad.at[wanted.reshape(-1)].add(incoming.reshape(-1, feature_width))
    new_entity_table, new_entity_state = adagrad(entity_table, entity_state, entity_grad)
    relation_grad = (
        jnp.zeros(relation_table.shape, jnp.float32).at[relation_id].add(grad_product * head_rows)
    )
    total_grad = lax.psum(relation_grad, ("rows", "rep"))
    new_relation_table, new_relation_state = adagrad(relation_table, relation_state, total_grad)
    return (new_entity_table, new_entity_state, new_relation_table, new_relation_state)


def solution(mesh):
    return jax.shard_map(
        per_device,
        mesh=mesh,
        in_specs=(
            P(("rows", "rep"), None),
            P(("rows", "rep")),
            P(),
            P(),
            P(("rows", "rep"), None),
            P(("rows", "rep"), None),
            P(("rows", "rep")),
            P(("rows", "rep"), None),
            P(("rows", "rep")),
        ),
        out_specs=(P(("rows", "rep"), None), P(("rows", "rep")), P(), P()),
        check_vma=False,
    )
```

profile of v0, /device:TPU:1, one launch (start us, length us, event | category | flops | bytes accessed | tf_op | source)
XLA Modules:
  0.0 857.8 jit_solution(4273394722346697271)
XLA Ops:
  7.2 0.9 copy.75
  8.7 0.8 copy.80
  9.9 0.4 fusion.9
  10.8 0.3 fusion.6
  11.3 0.3 copy.78
  11.7 0.6 fusion.5
  12.3 0.5 reduce_sum.55
  13.6 8.1 scatter_custom_fusion
  21.7 4.4 scatter_fusion
  26.1 0.7 all_to_all.16
  26.8 11.5 %all-to-all-start = ((s32[128,1,56]{2,1,0:T(1,128)}), s32[128,1,56]{2,1,0:T(1,128)S(1)}, u32[]{:S(2)}, u32[]{:S(2)}) async-start(s32[128,1,56]{2,1,0:T(1,128)} %bitcast.12), calls=%async_computation | async-start | bytes 131072 | tf_op jit(solution)/shard_map/all_to_all | solution.py:53
  38.7 9.5 %all-to-all-done = s32[128,1,56]{2,1,0:T(1,128)S(1)} async-done(((s32[128,1,56]{2,1,0:T(1,128)}), s32[128,1,56]{2,1,0:T(1,128)S(1)}, u32[]{:S(2)}, u32[]{:S(2)}) %all-to-all-start) | async-done | bytes 28704 | tf_op jit(solution)/shard_map/all_to_all | solution.py:53
  48.3 28.7 %gather_fusion = f32[7168,400]{1,0:T(8,128)} fusion(f32[512,400]{1,0:T(8,128)S(1)} %copy.94, s32[7168]{0:T(1024)S(1)} %broadcast_clamp_fusion), kind=kCustom, calls=%fused_computation | custom fusion | bytes 22966272 | tf_op jit(solution)/shard_map/jit(_take)/gather | solution.py:54
  77.0 10.5 %broadcast_select_fusion = f32[128,56,400]{2,1,0:T(8,128)} fusion(f32[128,56,400]{2,1,0:T(8,128)} %bitcast.50, pred[128,56]{1,0:T(8,128)(4,1)S(1)} %compare_and_fusion), kind=kLoop, calls=%fused_computation.16 | loop fusion | flops 2867200 | bytes 22944768 | tf_op jit(solution)/shard_map/jit(_take)/select_n | solution.py:54
  87.5 5.1 all-to-all-start.1
  92.6 14.1 %copy.85 = f32[7424,400]{1,0:T(8,128)} copy(f32[7424,400]{0,1:T(8,128)} %param.11) | data formatting | bytes 23756800 | tf_op args[2]
  106.7 10.6 %gather_fusion.2 = f32[1024,400]{1,0:T(8,128)} fusion(f32[7424,400]{1,0:T(8,128)} %copy.85, s32[1024]{0:T(1024)S(1)} %get-tuple-element.29), kind=kCustom, calls=%fused_computation.2 | custom fusion | bytes 3280896 | tf_op jit(solution)/shard_map/gather | solution.py:63
  117.3 1.8 copy.87
  119.2 167.4 %all-to-all-done.1 = f32[128,56,400]{2,1,0:T(8,128)} async-done(((f32[128,56,400]{2,1,0:T(8,128)}), f32[128,56,400]{2,1,0:T(8,128)}, u32[]{:S(2)}, u32[]{:S(2)}) %all-to-all-start.1) | async-done | bytes 11468832 | tf_op jit(solution)/shard_map/all_to_all | solution.py:55
  286.6 10.5 %gather_fusion.4 = f32[1024,400]{1,0:T(8,128)} fusion(f32[7168,400]{1,0:T(8,128)} %bitcast.18, s32[1024]{0:T(1024)S(1)} %broadcast_clamp_fusion.2), kind=kCustom, calls=%fused_computation.4 | custom fusion | bytes 3280896 | tf_op jit(solution)/shard_map/gather | solution.py:62
  297.1 10.5 %gather_fusion.3 = f32[1024,400]{1,0:T(8,128)} fusion(f32[7168,400]{1,0:T(8,128)} %bitcast.18, s32[1024]{0:T(1024)S(1)} %broadcast_clamp_fusion.3), kind=kCustom, calls=%fused_computation.3 | custom fusion | bytes 3280896 | tf_op jit(solution)/shard_map/gather | solution.py:61
  307.5 10.4 %gather_fusion.1 = f32[1024,400]{1,0:T(8,128)} fusion(f32[7168,400]{1,0:T(8,128)} %bitcast.18, s32[1024]{0:T(1024)S(1)} %broadcast_clamp_fusion.4), kind=kCustom, calls=%fused_computation.1 | custom fusion | bytes 3280896 | tf_op jit(solution)/shard_map/gather | solution.py:60
  318.0 2.8 copy.86
  320.7 2.9 copy.88
  323.7 2.4 multiply_reduce_fusion.1
  326.1 1.5 broadcast_multiply_fusion
  327.5 0.7 copy-done.2
  328.3 13.8 %divide_multiply_fusion = f32[1024,1024]{1,0:T(8,128)S(1)} fusion(f32[1024,400]{0,1:T(8,128)S(1)} %get-tuple-element.21, f32[1024,400]{1,0:T(8,128)S(1)} %copy-done.2), kind=kOutput, calls=%fused_computation.19 | convolution fusion | flops 5037359104 | bytes 7471104 | tf_op jit(solution)/shard_map/dot_general | solution.py:66
  342.1 7.3 fusion.19
  349.3 14.6 %fusion.20 = f32[1024,400]{1,0:T(8,128)} fusion(f32[1024,1024]{1,0:T(8,128)S(1)} %divide_multiply_fusion, f32[1024,400]{0,1:T(8,128)S(1)} %get-tuple-element.21), kind=kOutput, calls=%fused_computation.71 | convolution fusion | flops 5033164800 | bytes 7471104 | tf_op jit(solution)/shard_map/dot_general | solution.py:79
  363.9 1.8 copy.92
  365.8 2.8 copy.91
  368.6 11.7 %scatter_custom_fusion.2 = f32[7168,400]{1,0:T(8,128)} fusion(s32[1024]{0:T(1024)S(1)} %bitcast.64, f32[1024,400]{1,0:T(8,128)} %copy.91, f32[]{:T(128)} %constant.15.clone.1), kind=kCustom, calls=%fused_computation.17 | custom fusion | bytes 11469312 | tf_op jit(solution)/shard_map/scatter | solution.py:83
  380.3 15.0 %scatter_fusion.1 = f32[7168,400]{1,0:T(8,128)} fusion(f32[7168,400]{1,0:T(8,128)} %scatter_custom_fusion.2, s32[1024]{0:T(1024)S(1)} %bitcast.60, f32[1024,400]{1,0:T(8,128)S(1)} %copy.92), kind=kCustom, calls=%fused_computation.8 | custom fusion | bytes 4919296 | tf_op jit(solution)/shard_map/scatter | solution.py:84
  395.3 15.7 %scatter_fusion.2 = f32[7168,400]{1,0:T(8,128)} fusion(f32[7168,400]{1,0:T(8,128)} %scatter_fusion.1, s32[1024]{0:T(1024)S(1)} %bitcast.56, f32[1024,400]{1,0:T(8,128)} %fusion.20), kind=kCustom, calls=%fused_computation.9 | custom fusion | bytes 4919296 | tf_op jit(solution)/shard_map/scatter | solution.py:85
  411.0 16.3 %all-to-all-start.2 = ((f32[128,56,400]{2,1,0:T(8,128)}), f32[128,56,400]{2,1,0:T(8,128)}, u32[]{:S(2)}, u32[]{:S(2)}) async-start(f32[128,56,400]{2,1,0:T(8,128)} %bitcast.49), calls=%async_computation.2 | async-start | bytes 29360128 | tf_op jit(solution)/shard_map/all_to_all | solution.py:86
  427.4 2.0 copy.96
  429.5 13.5 %scatter_custom_fusion.6 = f32[7424,400]{1,0:T(8,128)} fusion(s32[1024]{0:T(1024)S(1)} %get-tuple-element.28, f32[1024,400]{1,0:T(8,128)} %copy.96, f32[]{:T(128)} %constant.15.clone.1), kind=kCustom, calls=%fused_computation.14 | custom fusion | flops 409600 | bytes 11878912 | tf_op jit(solution)/shard_map/scatter-add | solution.py:97
  443.0 0.5 broadcast.191
  443.5 0.8 reduce.3
  444.5 320.7 %all-reduce.2.cloned.1.call-done = f32[7424,400]{1,0:T(8,128)} async-done(((f32[7424,400]{1,0:T(8,128)}), f32[7424,400]{1,0:T(8,128)}) %all-reduce.2.cloned.1.call-update) | async-done | bytes 11878416 | tf_op jit(solution)/shard_map/psum | solution.py:99
  765.2 6.5 multiply_reduce_fusion
  771.7 0.6 sqrt_add_fusion
  772.3 16.1 %divide_subtract_fusion = f32[7424,400]{1,0:T(8,128)} fusion(f32[7424,400]{1,0:T(8,128)} %copy.85, f32[7424,400]{1,0:T(8,128)} %all-reduce.2.cloned.1.call-done, f32[7424]{0:T(1024)S(1)} %get-tuple-element.16), kind=kLoop, calls=%fused_computation.12 | loop fusion | flops 8908800 | bytes 35664896 | tf_op jit(solution)/shard_map/sub | solution.py:12
  788.4 14.2 %copy.99 = f32[7424,400]{0,1:T(8,128)} copy(f32[7424,400]{1,0:T(8,128)} %divide_subtract_fusion) | data formatting | bytes 23756800
  802.6 45.7 %scatter_custom_fusion.5 = f32[512,400]{1,0:T(8,128)S(1)} fusion(s32[7168]{0:T(1024)S(1)} %bitcast.61, f32[7168,400]{1,0:T(8,128)} %bitcast.21, f32[]{:T(128)} %constant.15.clone.1), kind=kCustom, calls=%fused_computation.41 | custom fusion | flops 2867200 | bytes 819712 | tf_op jit(solution)/shard_map/scatter-add | solution.py:94
  848.5 0.6 sqrt_add_fusion.1
  849.3 1.2 copy.98
  (62 shorter events, 3.5 us)
Async XLA Ops:
  7.2 2.7 copy-start.5
  8.4 2.0 copy-start.8
  11.3 1.7 copy-start.6
  11.7 10.0 %copy-start.9 = (s32[1024]{0:T(1024)S(1)}, s32[1024]{0:T(1024)}, u32[]{:S(2)}) copy-start(s32[1024]{0:T(1024)} %param.17) | copy-start | bytes 12292
  21.7 16.6 %copy-start.4 = (f32[512,400]{0,1:T(8,128)S(1)}, f32[512,400]{0,1:T(8,128)}, u32[]{:S(2)}) copy-start(f32[512,400]{0,1:T(8,128)} %param.9) | copy-start | bytes 2457604
  26.8 21.3 %all-to-all-start = ((s32[128,1,56]{2,1,0:T(1,128)}), s32[128,1,56]{2,1,0:T(1,128)S(1)}, u32[]{:S(2)}, u32[]{:S(2)}) async-start(s32[128,1,56]{2,1,0:T(1,128)} %bitcast.12), calls=%async_computation | async-start | bytes 131072 | tf_op jit(solution)/shard_map/all_to_all | solution.py:53
  87.5 199.1 %all-to-all-start.1 = ((f32[128,56,400]{2,1,0:T(8,128)}), f32[128,56,400]{2,1,0:T(8,128)}, u32[]{:S(2)}, u32[]{:S(2)}) async-start(f32[128,56,400]{2,1,0:T(8,128)} %broadcast_select_fusion), calls=%async_computation.1 | async-start | bytes 29360128 | tf_op jit(solution)/shard_map/all_to_all | solution.py:55
  92.6 14.1 %copy-start.10 = (s32[1024]{0:T(1024)S(1)}, s32[1024]{0:T(1024)}, u32[]{:S(2)}) copy-start(s32[1024]{0:T(1024)} %param.15) | copy-start | bytes 12292
  326.1 2.2 copy-start.2
  328.2 13.8 %copy-start = (f32[1024,400]{0,1:T(8,128)S(1)}, f32[1024,400]{0,1:T(8,128)}, u32[]{:S(2)}) copy-start(f32[1024,400]{0,1:T(8,128)} %copy.86) | copy-start | bytes 4915204
  328.3 13.8 %copy-start.1 = (f32[1024,400]{0,1:T(8,128)S(1)}, f32[1024,400]{0,1:T(8,128)}, u32[]{:S(2)}) copy-start(f32[1024,400]{0,1:T(8,128)} %copy.88) | copy-start | bytes 4915204
  411.0 16.4 %copy-start.3 = (f32[1024,400]{0,1:T(8,128)S(1)}, f32[1024,400]{0,1:T(8,128)}, u32[]{:S(2)}) copy-start(f32[1024,400]{0,1:T(8,128)} %get-tuple-element.22) | copy-start | bytes 4915204
  411.0 391.6 %all-to-all-start.2 = ((f32[128,56,400]{2,1,0:T(8,128)}), f32[128,56,400]{2,1,0:T(8,128)}, u32[]{:S(2)}, u32[]{:S(2)}) async-start(f32[128,56,400]{2,1,0:T(8,128)} %bitcast.49), calls=%async_computation.2 | async-start | bytes 29360128 | tf_op jit(solution)/shard_map/all_to_all | solution.py:86
  427.4 337.8 %all-reduce.2.cloned.1.call-start = ((), (), s32[]{:S(2)}) async-start(), calls=%async_computation.3 | async-start | bytes 30408704 | tf_op jit(solution)/shard_map/psum | solution.py:99
  444.5 327.2 %copy-start.7 = (f32[7424]{0:T(1024)S(1)}, f32[7424]{0:T(1024)}, u32[]{:S(2)}) copy-start(f32[7424]{0:T(1024)} %param.12) | copy-start | bytes 89092
  802.6 45.9 %copy-start.11 = (f32[512]{0:T(512)S(1)}, f32[512]{0:T(512)}, u32[]{:S(2)}) copy-start(f32[512]{0:T(512)} %param.10) | copy-start | bytes 6148
Sparse Core Ops, SparseCore 0:
  443.1 322.0 all-reduce.1
where the time goes:
time: 867 us; the launch traced here: 858 us
  waiting for transfers between devices  498 us (57%)
  local copies, waits for them, and re-layouts  176 us (20%)
  other arithmetic  100 us (12%)
  matrix products  35.7 us (4%)
  starting transfers between devices  32.9 us (4%)
  between operations  14.9 us (2%)
    psum x1, waiting for transfers between devices, per_device(): total_grad = lax.psum(relation_grad, ('rows', 'rep'))  321 us
    all_to_all x1, waiting for transfers between devices, per_device(): lax.all_to_all(looked, ('rows', 'rep'), split_axis=0, concat_axis=0, tile...  167 us
    scatter-add x1, other arithmetic, per_device(): entity_grad.at[wanted.reshape(-1)].add(incoming.reshape(-1, feature_width))  45.7 us
    unnamed x30, local copies, waits for them, and re-layouts  31.7 us
    gather x1, local copies, waits for them, and re-layouts, per_device(): looked = jnp.take(entity_table, wanted, axis=0)  28.7 us
  transfers between devices with their start and end apart: 4, of which 3 were waited for; matrix products, arithmetic and copies ran while one was open for 9% of the time, Pallas kernels for 0%

commit v1 on v0

v1 whole, which is shorter than its diff:
```python
import functools
import jax
import jax.numpy as jnp
from jax import lax
from jax.experimental import pallas as pl
from jax.experimental.pallas import tpu as pltpu
from jax.sharding import PartitionSpec as P

learn_rate = 0.5
adagrad_eps = 1e-10

AXES = ("rows", "rep")
F32, BF16, I32 = jnp.float32, jnp.bfloat16, jnp.int32
NDEV = 128
ENT = 512
EDGE = 1024
NEG = 1024
CAP = 40
SLOTS = 56
OCT = SLOTS // 8
TILES = 3 * OCT + 1
REL = 7424
GROUPS = REL // 128
VMEM_LIMIT = 60 * 1024 * 1024


def dot(a, b, dims):
    return lax.dot_general(a, b, (dims, ((), ())), preferred_element_type=F32)


NN = ((1,), (0,))
NT = ((1,), (1,))
TN = ((0,), (0,))


def split(x):
    hi = x.astype(BF16)
    return hi, (x - hi.astype(F32)).astype(BF16)


def prep_kernel(owner_ref, row_ref, request_ref, addr_ref):
    upper = (
        lax.broadcasted_iota(I32, (128, 128), 0) < lax.broadcasted_iota(I32, (128, 128), 1)
    ).astype(BF16)
    device = lax.broadcasted_iota(I32, (NDEV, 128), 0)
    lane = lax.broadcasted_iota(I32, (128, 128), 0)

    def block(i, carry):
        count, low, high = carry
        count = jnp.where(i == 16, 0.0, count)
        first = jnp.where(i >= 16, CAP, 0)
        owner = owner_ref[pl.ds(i, 1), :]
        row = row_ref[pl.ds(i, 1), :]
        onehot = (device == owner).astype(F32)
        onehot_b = onehot.astype(BF16)
        earlier = dot(onehot_b, upper, NN) + count
        rank = jnp.sum(onehot * earlier, axis=0, keepdims=True).astype(I32) + first
        count = count + jnp.sum(onehot, axis=1, keepdims=True)
        at = lane == rank
        low = low + dot(onehot_b, jnp.where(at, (row & 255).astype(F32), 0.0).astype(BF16), NT)
        high = high + dot(onehot_b, jnp.where(at, (row >> 8).astype(F32), 0.0).astype(BF16), NT)
        addr_ref[pl.ds(i, 1), :] = owner * (32 * OCT) + (rank >> 3) * 32 + (rank & 7)
        return count, low, high

    zero = jnp.zeros((NDEV, 128), F32)
    _, low, high = lax.fori_loop(0, 24, block, (jnp.zeros((NDEV, 1), F32), zero, zero))
    request_ref[...] = (low + 256.0 * high).astype(I32)


def prep(owner, row):
    return pl.pallas_call(
        prep_kernel,
        out_shape=(
            jax.ShapeDtypeStruct((NDEV, 128), I32),
            jax.ShapeDtypeStruct((24, 128), I32),
        ),
        name="prep",
    )(owner, row)


def lookup_kernel(wanted_ref, table_ref, out_ref, hi_ref, lo_ref, onehot_ref):
    @pl.when(pl.program_id(0) == 0)
    def _():
        for t in range(4):
            width = 128 if t < 3 else 16
            part = table_ref[t * 128 : t * 128 + width, :]
            if t == 3:
                part = jnp.concatenate([part, jnp.zeros((112, ENT), F32)], axis=0)
            hi, lo = split(part.T)
            hi_ref[:, t * 128 : (t + 1) * 128] = hi
            lo_ref[:, t * 128 : (t + 1) * 128] = lo

    wanted = wanted_ref[...].reshape(16, 128)
    padded = jnp.concatenate([wanted, jnp.zeros((112, 128), I32)], axis=0)
    columns = padded.T
    lane = lax.broadcasted_iota(I32, (2 * SLOTS, ENT), 1)
    for p in range(8):
        column = jnp.concatenate(
            [columns[:SLOTS, 2 * p : 2 * p + 1], columns[:SLOTS, 2 * p + 1 : 2 * p + 2]], axis=0
        )
        onehot_ref[p * 2 * SLOTS : (p + 1) * 2 * SLOTS, :] = (
            (lane == column).astype(F32).astype(BF16)
        )
    onehot = onehot_ref[...]
    for t in range(4):
        lanes = slice(t * 128, (t + 1) * 128)
        rows = dot(onehot, hi_ref[:, lanes], NN) + dot(onehot, lo_ref[:, lanes], NN)
        rows = rows.reshape(16, OCT, 8, 128)
        if t < 3:
            for q in range(OCT):
                out_ref[:, q * 3 + t] = rows[:, q]
        else:
            rest = rows[:, 0]
            for q in range(1, OCT):
                rest = rest + pltpu.roll(rows[:, q], 16 * q, 2)
            out_ref[:, 3 * OCT] = rest


def lookup(wanted, table_t):
    return pl.pallas_call(
        lookup_kernel,
        grid=(8,),
        in_specs=[
            pl.BlockSpec((16, 1, 128), lambda i: (i, 0, 0)),
            pl.BlockSpec((400, ENT), lambda i: (0, 0)),
        ],
        out_specs=pl.BlockSpec((16, TILES, 8, 128), lambda i: (i, 0, 0, 0)),
        out_shape=jax.ShapeDtypeStruct((NDEV, TILES, 8, 128), F32),
        scratch_shapes=[
            pltpu.VMEM((ENT, 512), BF16),
            pltpu.VMEM((ENT, 512), BF16),
            pltpu.VMEM((16 * SLOTS, ENT), BF16),
        ],
        compiler_params=pltpu.CompilerParams(vmem_limit_bytes=VMEM_LIMIT),
        name="lookup",
    )(wanted, table_t)


BLOCK = 256


def math_kernel(
    addr_ref, pay_ref, rel_ref, grad_ref, rel_grad_ref,
    rows, rest, hr_hi, hr_lo, n_hi, n_lo, g_neg, sems,
):
    copies = [
        pltpu.make_async_copy(
            pay_ref.at[:, 3 * q : 3 * q + 3], rows.at[:, q, 0:3], sems.at[q]
        )
        for q in range(OCT)
    ]
    tail_copy = pltpu.make_async_copy(pay_ref.at[:, 3 * OCT], rest, sems.at[OCT])
    tail_copy.start()
    for copy in copies:
        copy.start()
    tail_copy.wait()
    lane = lax.broadcasted_iota(I32, (8, 8, 128), 2)

    def expand(i, _):
        part = rest[pl.ds(i * 8, 8)]
        for q in range(OCT):
            shifted = part if q == 0 else pltpu.roll(part, 128 - 16 * q, 2)
            rows[pl.ds(i * 8, 8), q, 3] = jnp.where(lane < 16, shifted, 0.0)
        return 0

    lax.fori_loop(0, 16, expand, 0)
    for copy in copies:
        copy.wait()
    flat = rows.reshape(NDEV * OCT * 32, 128)
    grad_flat = grad_ref.reshape(384 * 32, 128)

    def gather(i, _):
        for j in range(8):
            a = addr_ref[i >> 4, (i & 15) * 8 + j]
            grad_flat[pl.ds(i * 32 + j, 4, stride=8), :] = flat[pl.ds(a, 4, stride=8), :]
        return 0

    lax.fori_loop(0, 384, gather, 0, unroll=4)

    def prepare(b, _):
        octets = pl.ds(b * 32, 32)
        edges = pl.ds(b * BLOCK, BLOCK)
        for t in range(4):
            lanes = slice(t * 128, (t + 1) * 128)
            hr = grad_ref[octets, t].reshape(BLOCK, 128) * rel_ref[edges, lanes]
            hr_hi[edges, lanes], hr_lo[edges, lanes] = split(hr)
            neg = grad_ref[pl.ds(256 + b * 32, 32), t].reshape(BLOCK, 128)
            n_hi[edges, lanes], n_lo[edges, lanes] = split(neg)
        return 0

    lax.fori_loop(0, EDGE // BLOCK, prepare, 0)
    g_neg[...] = jnp.zeros_like(g_neg)

    def block(b, _):
        edges = pl.ds(b * BLOCK, BLOCK)
        octets = pl.ds(b * 32, 32)
        tails = pl.ds(128 + b * 32, 32)
        a_hi, a_lo = hr_hi[edges, :], hr_lo[edges, :]
        score = dot(a_hi, n_hi[...], NT) + dot(a_hi, n_lo[...], NT) + dot(a_lo, n_hi[...], NT)
        p_hi, p_lo = split(1.0 / (1.0 + jnp.exp(-score)))
        g_hr = dot(p_hi, n_hi[...], NN) + dot(p_hi, n_lo[...], NN) + dot(p_lo, n_hi[...], NN)
        g_neg[...] += dot(p_hi, a_hi, TN) + dot(p_hi, a_lo, TN) + dot(p_lo, a_hi, TN)
        total = jnp.zeros((BLOCK, 128), F32)
        for t in range(4):
            lanes = slice(t * 128, (t + 1) * 128)
            hr = grad_ref[octets, t].reshape(BLOCK, 128) * rel_ref[edges, lanes]
            total = total + hr * grad_ref[tails, t].reshape(BLOCK, 128)
        positive = jnp.sum(total, axis=1, keepdims=True)
        d_pos = -1.0 / (1.0 + jnp.exp(positive))
        for t in range(4):
            lanes = slice(t * 128, (t + 1) * 128)
            head = grad_ref[octets, t].reshape(BLOCK, 128)
            tail = grad_ref[tails, t].reshape(BLOCK, 128)
            rel = rel_ref[edges, lanes]
            g = d_pos * tail + g_hr[:, lanes] * (1.0 / NEG)
            rel_grad_ref[octets, t] = (g * head).reshape(32, 8, 128)
            grad_ref[tails, t] = (d_pos * (head * rel)).reshape(32, 8, 128)
            grad_ref[octets, t] = (g * rel).reshape(32, 8, 128)
        return 0

    lax.fori_loop(0, EDGE // BLOCK, block, 0)
    for t in range(4):
        lanes = slice(t * 128, (t + 1) * 128)
        grad_ref[256:384, t] = (g_neg[:, lanes] * (1.0 / NEG)).reshape(128, 8, 128)


def math(addr, arrived, rel_rows):
    return pl.pallas_call(
        math_kernel,
        in_specs=[
            pl.BlockSpec(memory_space=pltpu.SMEM),
            pl.BlockSpec(memory_space=pl.ANY),
            pl.BlockSpec(memory_space=pltpu.VMEM),
        ],
        out_specs=(
            pl.BlockSpec(memory_space=pltpu.VMEM),
            pl.BlockSpec(memory_space=pltpu.VMEM),
        ),
        out_shape=(
            jax.ShapeDtypeStruct((384, 4, 8, 128), F32),
            jax.ShapeDtypeStruct((128, 4, 8, 128), F32),
        ),
        scratch_shapes=[
            pltpu.VMEM((NDEV, OCT, 4, 8, 128), F32),
            pltpu.VMEM((NDEV, 8, 128), F32),
            pltpu.VMEM((EDGE, 512), BF16),
            pltpu.VMEM((EDGE, 512), BF16),
            pltpu.VMEM((NEG, 512), BF16),
            pltpu.VMEM((NEG, 512), BF16),
            pltpu.VMEM((NEG, 512), F32),
            pltpu.SemaphoreType.DMA((OCT + 1,)),
        ],
        compiler_params=pltpu.CompilerParams(vmem_limit_bytes=VMEM_LIMIT),
        name="math",
    )(addr, arrived, rel_rows)


def relation_kernel(id_ref, grad_ref, out_ref, rows, packed, sems):
    zero = jnp.zeros((16, 4, 8, 128), F32)

    def clear(g, _):
        rows[pl.ds(g * 16, 16)] = zero
        return 0

    lax.fori_loop(0, GROUPS, clear, 0)
    flat = rows.reshape(REL * 4, 128)
    grad_flat = grad_ref.reshape(128 * 32, 128)

    def add(i, _):
        for j in range(8):
            r = id_ref[i >> 4, (i & 15) * 8 + j]
            at = pl.ds((r >> 3) * 32 + (r & 7), 4, stride=8)
            flat[at, :] = flat[at, :] + grad_flat[pl.ds(i * 32 + j, 4, stride=8), :]
        return 0

    lax.fori_loop(0, 128, add, 0, unroll=2)

    def copy(g):
        return pltpu.make_async_copy(
            packed.at[g & 1], out_ref.at[g], sems.at[g & 1]
        )

    def pack(g, _):
        @pl.when(g >= 2)
        def _():
            copy(g - 2).wait()

        for t in range(3):
            packed[g & 1, pl.ds(t * 16, 16)] = rows[pl.ds(g * 16, 16), t]
        for half in range(2):
            rest = rows[g * 16 + half * 8, 3]
            for q in range(1, 8):
                rest = rest + pltpu.roll(rows[g * 16 + half * 8 + q, 3], 16 * q, 1)
            packed[g & 1, 48 + half] = rest
        copy(g).start()
        return 0

    lax.fori_loop(0, GROUPS, pack, 0)
    copy(GROUPS - 2).wait()
    copy(GROUPS - 1).wait()


def relation_sum(ids, grad):
    return pl.pallas_call(
        relation_kernel,
        in_specs=[
            pl.BlockSpec(memory_space=pltpu.SMEM),
            pl.BlockSpec(memory_space=pltpu.VMEM),
        ],
        out_specs=pl.BlockSpec(memory_space=pl.ANY),
        out_shape=jax.ShapeDtypeStruct((GROUPS, 50, 8, 128), F32),
        scratch_shapes=[
            pltpu.VMEM((REL // 8, 4, 8, 128), F32),
            pltpu.VMEM((2, 50, 8, 128), F32),
            pltpu.SemaphoreType.DMA((2,)),
        ],
        compiler_params=pltpu.CompilerParams(vmem_limit_bytes=VMEM_LIMIT),
        name="relation_sum",
    )(ids, grad)


def pack_kernel(addr_ref, grad_ref, out_ref, rows, rest, sems):
    zero = jnp.zeros((8, OCT, 4, 8, 128), F32)

    def clear(i, _):
        rows[pl.ds(i * 8, 8)] = zero
        return 0

    lax.fori_loop(0, 16, clear, 0)
    flat = rows.reshape(NDEV * OCT * 32, 128)
    grad_flat = grad_ref.reshape(384 * 32, 128)

    def scatter(i, _):
        for j in range(8):
            a = addr_ref[i >> 4, (i & 15) * 8 + j]
            flat[pl.ds(a, 4, stride=8), :] = grad_flat[pl.ds(i * 32 + j, 4, stride=8), :]
        return 0

    lax.fori_loop(0, 384, scatter, 0, unroll=4)
    copies = [
        pltpu.make_async_copy(
            rows.at[:, q, 0:3], out_ref.at[:, 3 * q : 3 * q + 3], sems.at[q]
        )
        for q in range(OCT)
    ]
    for copy in copies:
        copy.start()

    def pack(i, _):
        part = rows[pl.ds(i * 8, 8), 0, 3]
        for q in range(1, OCT):
            part = part + pltpu.roll(rows[pl.ds(i * 8, 8), q, 3], 16 * q, 2)
        rest[pl.ds(i * 8, 8)] = part
        return 0

    lax.fori_loop(0, 16, pack, 0)
    last = pltpu.make_async_copy(rest, out_ref.at[:, 3 * OCT], sems.at[OCT])
    last.start()
    for copy in copies:
        copy.wait()
    last.wait()


def pack_grads(addr, grads):
    return pl.pallas_call(
        pack_kernel,
        in_specs=[
            pl.BlockSpec(memory_space=pltpu.SMEM),
            pl.BlockSpec(memory_space=pltpu.VMEM),
        ],
        out_specs=pl.BlockSpec(memory_space=pl.ANY),
        out_shape=jax.ShapeDtypeStruct((NDEV, TILES, 8, 128), F32),
        scratch_shapes=[
            pltpu.VMEM((NDEV, OCT, 4, 8, 128), F32),
            pltpu.VMEM((NDEV, 8, 128), F32),
            pltpu.SemaphoreType.DMA((OCT + 1,)),
        ],
        compiler_params=pltpu.CompilerParams(vmem_limit_bytes=VMEM_LIMIT),
        name="pack_grads",
    )(addr, grads)


def entity_kernel(wanted_ref, pay_ref, table_ref, state_ref, new_table, new_state, hi, lo, total):
    step = pl.program_id(0)

    @pl.when(step == 0)
    def _():
        total[...] = jnp.zeros_like(total)

    for t in range(4):
        lanes = slice(t * 128, (t + 1) * 128)
        parts = []
        for q in range(OCT):
            if t < 3:
                parts.append(pay_ref[:, q * 3 + t])
            else:
                part = pay_ref[:, 3 * OCT]
                if q:
                    part = pltpu.roll(part, 128 - 16 * q, 2)
                lane = lax.broadcasted_iota(I32, (16, 8, 128), 2)
                parts.append(jnp.where(lane < 16, part, 0.0))
        x = jnp.stack(parts, axis=1).reshape(16 * SLOTS, 128)
        hi[:, lanes], lo[:, lanes] = split(x)
    row = lax.broadcasted_iota(I32, (ENT, 16 * SLOTS), 0)
    onehot = (row == wanted_ref[...].reshape(1, 16 * SLOTS)).astype(F32).astype(BF16)
    total[...] += dot(onehot, hi[...], NN) + dot(onehot, lo[...], NN)

    @pl.when(step == pl.num_programs(0) - 1)
    def _():
        grad = total[...].T[:400, :]
        state = state_ref[...] + jnp.sum(grad * grad, axis=0, keepdims=True) / 400.0
        new_state[...] = state
        new_table[...] = table_ref[...] - learn_rate * grad / (jnp.sqrt(state) + adagrad_eps)


def entity_update(wanted, arrived, table_t, state):
    return pl.pallas_call(
        entity_kernel,
        grid=(8,),
        in_specs=[
            pl.BlockSpec((1, 1, 16 * SLOTS), lambda i: (i, 0, 0)),
            pl.BlockSpec((16, TILES, 8, 128), lambda i: (i, 0, 0, 0)),
            pl.BlockSpec((400, ENT), lambda i: (0, 0)),
            pl.BlockSpec((1, ENT), lambda i: (0, 0)),
        ],
        out_specs=(
            pl.BlockSpec((400, ENT), lambda i: (0, 0)),
            pl.BlockSpec((1, ENT), lambda i: (0, 0)),
        ),
        out_shape=(
            jax.ShapeDtypeStruct((400, ENT), F32),
            jax.ShapeDtypeStruct((1, ENT), F32),
        ),
        scratch_shapes=[
            pltpu.VMEM((16 * SLOTS, 512), BF16),
            pltpu.VMEM((16 * SLOTS, 512), BF16),
            pltpu.VMEM((ENT, 512), F32),
        ],
        compiler_params=pltpu.CompilerParams(vmem_limit_bytes=VMEM_LIMIT),
        name="entity_update",
    )(wanted, arrived, table_t, state)


def relation_update_kernel(grad_ref, table_ref, state_ref, new_table, new_state):
    for g in range(2):
        lanes = slice(g * 128, (g + 1) * 128)
        parts = []
        for t in range(3):
            parts.append(grad_ref[g, t * 16 : (t + 1) * 16].reshape(128, 128).T)
        rest = []
        for half in range(2):
            part = grad_ref[g, 48 + half]
            for q in range(8):
                rest.append(part if q == 0 else pltpu.roll(part, 128 - 16 * q, 1))
        parts.append(jnp.concatenate(rest, axis=0).T[:16, :])
        grad = jnp.concatenate(parts, axis=0)
        state = state_ref[:, lanes] + jnp.sum(grad * grad, axis=0, keepdims=True) / 400.0
        new_state[:, lanes] = state
        new_table[:, lanes] = table_ref[:, lanes] - grad * (
            learn_rate / (jnp.sqrt(state) + adagrad_eps)
        )


def relation_update(grad, table_t, state):
    return pl.pallas_call(
        relation_update_kernel,
        grid=(GROUPS // 2,),
        in_specs=[
            pl.BlockSpec((2, 50, 8, 128), lambda i: (i, 0, 0, 0)),
            pl.BlockSpec((400, 256), lambda i: (0, i)),
            pl.BlockSpec((1, 256), lambda i: (0, i)),
        ],
        out_specs=(
            pl.BlockSpec((400, 256), lambda i: (0, i)),
            pl.BlockSpec((1, 256), lambda i: (0, i)),
        ),
        out_shape=(
            jax.ShapeDtypeStruct((400, REL), F32),
            jax.ShapeDtypeStruct((1, REL), F32),
        ),
        compiler_params=pltpu.CompilerParams(vmem_limit_bytes=VMEM_LIMIT),
        name="relation_update",
    )(grad, table_t, state)


def exchange(x):
    return lax.all_to_all(x, AXES, split_axis=0, concat_axis=0, tiled=True)


def per_device(
    entity_table,
    entity_state,
    relation_table,
    relation_state,
    end_owner,
    end_row,
    relation_id,
    negative_owner,
    negative_row,
):
    owner = jnp.concatenate([end_owner.T.reshape(16, 128), negative_owner.reshape(8, 128)])
    row = jnp.concatenate([end_row.T.reshape(16, 128), negative_row.reshape(8, 128)])
    request, addr = prep(owner, row)
    wanted = exchange(request.reshape(NDEV, 1, 128))
    looked = lookup(wanted, entity_table.T)
    arrived = exchange(looked)
    rel_rows = jnp.pad(relation_table[relation_id], ((0, 0), (0, 112)))
    grads, rel_grads = math(addr, arrived, rel_rows)
    relation_grad = relation_sum(relation_id.reshape(8, 128), rel_grads)
    total_grad = lax.psum(relation_grad, AXES)
    outgoing = pack_grads(addr, grads)
    incoming = exchange(outgoing)
    slots = wanted[:, 0, :SLOTS].reshape(8, 1, 16 * SLOTS)
    new_entity_table, new_entity_state = entity_update(
        slots, incoming, entity_table.T, entity_state.reshape(1, ENT)
    )
    new_relation_table, new_relation_state = relation_update(
        total_grad, relation_table.T, relation_state.reshape(1, REL)
    )
    return (
        new_entity_table.T,
        new_entity_state.reshape(ENT),
        new_relation_table.T,
        new_relation_state.reshape(REL),
    )


def solution(mesh):
    return jax.shard_map(
        per_device,
        mesh=mesh,
        in_specs=(
            P(AXES, None),
            P(AXES),
            P(),
            P(),
            P(AXES, None),
            P(AXES, None),
            P(AXES),
            P(AXES, None),
            P(AXES),
        ),
        out_specs=(P(AXES, None), P(AXES), P(), P()),
        check_vma=False,
    )
```

time: 867 us -> 606 us (0.70)
  local copies, waits for them, and re-layouts: 176 us -> 27.9 us
  Pallas kernels: 0 us -> 146 us
  waiting for transfers between devices: 498 us -> 378 us
  other arithmetic: 100 us -> 2.75 us
  matrix products: 35.7 us -> 0 us
  blocking collectives: 0 us -> 21.9 us
  starting transfers between devices: 32.9 us -> 14.2 us
    pallas_call x0 -> x7, Pallas kernels: none -> 146 us  [the longest x1 29.5 us: relation_sum(): pl.pallas_call(relation_kernel, in_specs=[pl.BlockSpec(memory_space=pltpu...]
    gather x8 -> x1, local copies, waits for them, and re-layouts: 78.2 us -> 9.34 us  [per_device(): rel_rows = jnp.pad(relation_table[relation_id], ((0, 0), (0, 112)))]
    psum x1, waiting for transfers between devices: 321 us -> 257 us  [per_device(): total_grad = lax.psum(relation_grad, AXES)]
    scatter-add x2 -> x0, other arithmetic: 59.2 us -> none  [the longest x1 45.7 us: per_device(): entity_grad.at[wanted.reshape(-1)].add(incoming.reshape(-1, feature_width))]
    all_to_all x3 -> x2, waiting for transfers between devices: 177 us -> 121 us  [exchange(): return lax.all_to_all(x, AXES, split_axis=0, concat_axis=0, tiled=True)]
    scatter x5 -> x0, local copies, waits for them, and re-layouts: 54.9 us -> none  [the longest x1 15.7 us: per_device(): outgoing = outgoing.at[neg_slot].set(grad_neg)]
    dot_general x3 -> x0, matrix products: 35.7 us -> none  [the longest x1 14.6 us: per_device(): lax.dot_general(dneg, product, (((0,), (0,)), ((), ())), precision=high,...]
    all_to_all x0 -> x1, blocking collectives: none -> 21.9 us  [exchange(): return lax.all_to_all(x, AXES, split_axis=0, concat_axis=0, tiled=True)]
  transfers between devices with their start and end apart: 4 -> 3, of which waited for: 3 -> 2; matrix products, arithmetic and copies ran while one was open for 9% -> 5% of each run, Pallas kernels for 0% -> 9%
where the time goes in v1:
time: 606 us; the launch traced here: 604 us
  waiting for transfers between devices  378 us (62%)
  Pallas kernels  146 us (24%)
  local copies, waits for them, and re-layouts  27.9 us (5%)
  blocking collectives  21.9 us (4%)
  starting transfers between devices  14.2 us (2%)
  between operations  14.1 us (2%)
    psum x1, waiting for transfers between devices, per_device(): total_grad = lax.psum(relation_grad, AXES)  257 us
    all_to_all x2, waiting for transfers between devices, exchange(): return lax.all_to_all(x, AXES, split_axis=0, concat_axis=0, tiled=True)  121 us
    pallas_call x1, Pallas kernels, relation_sum(): pl.pallas_call(relation_kernel, in_specs=[pl.BlockSpec(memory_space=pltpu...  29.5 us
    pallas_call x1, Pallas kernels, math(): pl.pallas_call(math_kernel, in_specs=[pl.BlockSpec(memory_space=pltpu.SME...  28.2 us
    pallas_call x1, Pallas kernels, relation_update(): pl.pallas_call(relation_update_kernel, grid=(GROUPS // 2,), in_specs=[pl....  25.6 us
    all_to_all x1, blocking collectives, exchange(): return lax.all_to_all(x, AXES, split_axis=0, concat_axis=0, tiled=True)  21.9 us
    pallas_call x1, Pallas kernels, lookup(): pl.pallas_call(lookup_kernel, grid=(8,), in_specs=[pl.BlockSpec((16, 1, 1...  21.3 us
    pallas_call x1, Pallas kernels, pack_grads(): pl.pallas_call(pack_kernel, in_specs=[pl.BlockSpec(memory_space=pltpu.SME...  16.4 us
  transfers between devices with their start and end apart: 3, of which 2 were waited for; matrix products, arithmetic and copies ran while one was open for 5% of the time, Pallas kernels for 9%

profile of v1, /device:TPU:1, one launch (start us, length us, event | category | flops | bytes accessed | tf_op | source)
XLA Modules:
  0.0 604.1 jit_solution(2478452583347353978)
XLA Ops:
  7.2 0.7 reshape.38
  7.9 0.7 reshape.40
  8.6 1.3 pad_add_fusion
  9.9 9.5 %prep.1 = (s32[128,128]{1,0:T(8,128)}, s32[24,128]{1,0:T(8,128)}) custom-call(s32[24,128]{1,0:T(8,128)} %get-tuple-element.20.owner_ref, s32[24,128]{1,0:T(8,128)} %get-tuple-element.21.row_ref), custom_call_target="tpu_custom_call" | custom-call | tf_op jit(solution)/shard_map/prep/pallas_call | solution.py:71
  19.3 21.9 %all_to_all.15.wanted_ref = s32[128,1,128]{2,1,0:T(1,128)} all-to-all(s32[128,1,128]{2,1,0:T(1,128)} %bitcast.15), channel_id=1, replica_groups=mesh['rows'=32,'rep'=4] {'rows','rep'}, dimensions={0} | all-to-all | bytes 131072 | tf_op jit(solution)/shard_map/all_to_all | solution.py:487
  41.2 21.3 %lookup.1 = f32[128,22,8,128]{3,2,1,0:T(8,128)} custom-call(s32[128,1,128]{2,1,0:T(1,128)} %all_to_all.15.wanted_ref, f32[400,512]{1,0:T(8,128)} %bitcast.13), custom_call_target="tpu_custom_call" | custom-call | tf_op jit(solution)/shard_map/lookup/pallas_call | solution.py:120
  62.5 4.9 all-to-all-start.1
  67.4 0.0 copy-start.2
  67.4 14.1 %copy.14 = f32[7424,400]{1,0:T(8,128)} copy(f32[7424,400]{0,1:T(8,128)} %param.11) | data formatting | bytes 23756800 | tf_op args[2]
  81.5 0.0 copy-done.2
  81.5 9.3 %gather_fusion = f32[1024,400]{1,0:T(8,128)S(1)} fusion(f32[7424,400]{1,0:T(8,128)} %copy.14, s32[1024]{0:T(1024)S(1)} %fusion), kind=kCustom, calls=%fused_computation | custom fusion | bytes 3280896 | tf_op jit(solution)/shard_map/gather | solution.py:507
  90.9 1.5 pad.4.rel_ref
  92.4 120.6 %all-to-all-done.1.pay_ref = f32[128,22,8,128]{3,2,1,0:T(8,128)} async-done(((f32[128,22,8,128]{3,2,1,0:T(8,128)}), f32[128,22,8,128]{3,2,1,0:T(8,128)}, u32[]{:S(2)}, u32[]{:S(2)}) %all-to-all-start.1) | async-done | bytes 11534368 | tf_op jit(solution)/shard_map/all_to_all | solution.py:487
  213.0 28.2 %math.1 = (f32[384,4,8,128]{3,2,1,0:T(8,128)}, f32[128,4,8,128]{3,2,1,0:T(8,128)}) custom-call(s32[24,128]{1,0:T(8,128)} %get-tuple-element.13.addr_ref, f32[128,22,8,128]{3,2,1,0:T(8,128)} %all-to-all-done.1.pay_ref, f32[1024,512]{1,0:T(8,128)} %pad.4.rel_ref), custom_call_target="tpu_custom_call" | custom-call | tf_op jit(solution)/shard_map/math/pallas_call | solution.py:228
  241.2 16.4 %pack_grads.1 = f32[128,22,8,128]{3,2,1,0:T(8,128)} custom-call(s32[24,128]{1,0:T(8,128)} %get-tuple-element.13.addr_ref, f32[384,4,8,128]{3,2,1,0:T(8,128)} %get-tuple-element.14.grad_ref), custom_call_target="tpu_custom_call" | custom-call | tf_op jit(solution)/shard_map/pack_grads/pallas_call | solution.py:365
  257.6 9.3 %all-to-all-start.2 = ((f32[128,22,8,128]{3,2,1,0:T(8,128)}), f32[128,22,8,128]{3,2,1,0:T(8,128)}, u32[]{:S(2)}, u32[]{:S(2)}) async-start(f32[128,22,8,128]{3,2,1,0:T(8,128)} %pack_grads.1), calls=%async_computation.2 | async-start | bytes 23068672 | tf_op jit(solution)/shard_map/all_to_all | solution.py:487
  266.9 0.0 all-reduce.3.cloned.1.call-start
  267.0 0.0 copy-start.1
  267.0 0.0 copy-start
  267.0 29.5 %relation_sum.1 = f32[58,50,8,128]{3,2,1,0:T(8,128)} custom-call(s32[8,128]{1,0:T(8,128)} %bitcast.16, f32[128,4,8,128]{3,2,1,0:T(8,128)} %get-tuple-element.17.grad_ref), custom_call_target="tpu_custom_call" | custom-call | tf_op jit(solution)/shard_map/relation_sum/pallas_call | solution.py:304
  296.5 0.0 all-reduce.3.cloned.1.call-update
  296.5 0.0 copy-done.1
  296.5 0.6 reshape.46.state_ref
  297.2 0.0 copy-done
  297.2 0.2 slice_reduce_fusion
  297.4 0.7 reshape_squeeze.4.wanted_ref
  298.1 256.9 %all-reduce.3.cloned.1.call-done.grad_ref = f32[58,50,8,128]{3,2,1,0:T(8,128)} async-done(((f32[58,50,8,128]{3,2,1,0:T(8,128)}), f32[58,50,8,128]{3,2,1,0:T(8,128)}) %all-reduce.3.cloned.1.call-update) | async-done | bytes 11878416 | tf_op jit(solution)/shard_map/psum | solution.py:510
  554.9 25.6 %relation_update.1 = (f32[400,7424]{1,0:T(8,128)}, f32[1,7424]{1,0:T(1,128)}) custom-call(f32[58,50,8,128]{3,2,1,0:T(8,128)} %all-reduce.3.cloned.1.call-done.grad_ref, f32[400,7424]{1,0:T(8,128)} %bitcast.12, f32[1,7424]{1,0:T(1,128)} %reshape.46.state_ref), custom_call_target="tpu_custom_call" | custom-call | tf_op jit(solution)/shard_map/relation_update/pallas_call | solution.py:465
  580.6 1.4 reduce.1
  582.0 0.0 all-to-all-done.2.pay_ref
  582.0 15.2 %entity_update.1 = (f32[400,512]{1,0:T(8,128)}, f32[1,512]{1,0:T(1,128)}) custom-call(s32[8,1,896]{2,1,0:T(1,128)} %reshape_squeeze.4.wanted_ref, f32[128,22,8,128]{3,2,1,0:T(8,128)} %all-to-all-done.2.pay_ref, f32[400,512]{1,0:T(8,128)} %bitcast.14, f32[1,512]{1,0:T(1,128)} %bitcast.21), custom_call_target="tpu_custom_call" | custom-call | tf_op jit(solution)/shard_map/entity_update/pallas_call | solution.py:417
  (1 shorter events, 0.0 us)
Async XLA Ops:
  62.5 150.5 %all-to-all-start.1 = ((f32[128,22,8,128]{3,2,1,0:T(8,128)}), f32[128,22,8,128]{3,2,1,0:T(8,128)}, u32[]{:S(2)}, u32[]{:S(2)}) async-start(f32[128,22,8,128]{3,2,1,0:T(8,128)} %lookup.1), calls=%async_computation.1 | async-start | bytes 23068672 | tf_op jit(solution)/shard_map/all_to_all | solution.py:487
  67.4 14.1 %copy-start.2 = (s32[1024]{0:T(1024)S(1)}, s32[1024]{0:T(1024)}, u32[]{:S(2)}) copy-start(s32[1024]{0:T(1024)} %param.15) | copy-start | bytes 12292
  257.6 324.4 %all-to-all-start.2 = ((f32[128,22,8,128]{3,2,1,0:T(8,128)}), f32[128,22,8,128]{3,2,1,0:T(8,128)}, u32[]{:S(2)}, u32[]{:S(2)}) async-start(f32[128,22,8,128]{3,2,1,0:T(8,128)} %pack_grads.1), calls=%async_computation.2 | async-start | bytes 23068672 | tf_op jit(solution)/shard_map/all_to_all | solution.py:487
  266.9 288.0 %all-reduce.3.cloned.1.call-start = ((), (), s32[]{:S(2)}) async-start(), calls=%async_computation.3 | async-start | bytes 23756800 | tf_op jit(solution)/shard_map/psum | solution.py:510
  267.0 29.6 %copy-start.1 = (f32[7424]{0:T(1024)S(1)}, f32[7424]{0:T(1024)}, u32[]{:S(2)}) copy-start(f32[7424]{0:T(1024)} %param.12) | copy-start | bytes 89092
  267.0 30.2 %copy-start = (s32[128,1,128]{2,1,0:T(1,128)S(1)}, s32[128,1,128]{2,1,0:T(1,128)}, u32[]{:S(2)}) copy-start(s32[128,1,128]{2,1,0:T(1,128)} %all_to_all.15.wanted_ref) | copy-start | bytes 196612
Sparse Core Ops, SparseCore 0:
  296.6 258.2 all-reduce.2

commit v2 on v1

v2 whole, which is shorter than its diff:
```python
import functools
import jax
import jax.numpy as jnp
from jax import lax
from jax.experimental import pallas as pl
from jax.experimental.pallas import tpu as pltpu
from jax.sharding import PartitionSpec as P

learn_rate = 0.5
adagrad_eps = 1e-10

AXES = ("rows", "rep")
F32, BF16, I32 = jnp.float32, jnp.bfloat16, jnp.int32
ENT = 512
WIDTH = 400
EDGE = 1024
NEG = 1024
GROUP = 32
MAIN = 22
OCT = 28
OVER = OCT - MAIN
MAIN_TILES = 3 * MAIN + 3
OVER_TILES = 3 * OVER + 1
REL = 7424
RELGROUPS = REL // 128
VMEM_LIMIT = 60 * 1024 * 1024
FLAG = 127


def dot(a, b, dims):
    return lax.dot_general(a, b, (dims, ((), ())), preferred_element_type=F32)


NN = ((1,), (0,))
NT = ((1,), (1,))
TN = ((0,), (0,))


def split(x):
    hi = x.astype(BF16)
    return hi, (x - hi.astype(F32)).astype(BF16)


def prep_kernel(end_owner, end_row, neg_owner, neg_row, request_ref, addr_ref):
    iota0 = lax.broadcasted_iota(I32, (128, 128), 0)
    upper = (iota0 < lax.broadcasted_iota(I32, (128, 128), 1)).astype(BF16)
    group = lax.broadcasted_iota(I32, (GROUP, 128), 0)
    double = lax.broadcasted_iota(I32, (2 * GROUP, 128), 0)
    count = jnp.zeros((GROUP, 1), F32)
    low = jnp.zeros((2 * GROUP, 128), F32)
    high = jnp.zeros((2 * GROUP, 128), F32)
    for i in range(24):
        lanes = slice((i & 7) * 128, (i & 7) * 128 + 128)
        if i < 16:
            owner = end_owner[i >> 3 : (i >> 3) + 1, lanes]
            row = end_row[i >> 3 : (i >> 3) + 1, lanes]
        else:
            owner = neg_owner[:, lanes]
            row = neg_row[i - 16 : i - 15, :]
        target = owner >> 2
        value = (owner & 3) * ENT + row
        onehot = (group == target).astype(F32)
        earlier = dot(onehot.astype(BF16), upper, NN) + count
        rank = jnp.sum(onehot * earlier, axis=0, keepdims=True).astype(I32)
        count = count + jnp.sum(onehot, axis=1, keepdims=True)
        wide = (double == 2 * target + (rank >> 7)).astype(F32).astype(BF16)
        at = iota0 == (rank & 127)
        low = low + dot(wide, jnp.where(at, (value & 255).astype(F32), 0.0).astype(BF16), NT)
        high = high + dot(wide, jnp.where(at, (value >> 8).astype(F32), 0.0).astype(BF16), NT)
        addr_ref[i : i + 1, :] = (target * OCT + (rank >> 3)) * 32 + (rank & 7)
    most = jnp.max(count, axis=0, keepdims=True)
    flag = (most > 8.0 * MAIN).astype(F32)
    lane = lax.broadcasted_iota(I32, (2 * GROUP, 128), 1)
    mark = (lane == FLAG) & ((double & 1) == 1)
    request_ref[...] = jnp.where(mark, flag, low + 256.0 * high).astype(I32)


def prep(end_owner, end_row, neg_owner, neg_row):
    return pl.pallas_call(
        prep_kernel,
        out_shape=(
            jax.ShapeDtypeStruct((2 * GROUP, 128), I32),
            jax.ShapeDtypeStruct((24, 128), I32),
        ),
        name="prep",
    )(end_owner, end_row, neg_owner, neg_row)


STEP = 4


def lookup_kernel(octets, first, wanted_ref, table_ref, out_ref, table, rows):
    step = pl.program_id(0)

    @pl.when(step == 0)
    def _():
        def turn(i, _):
            for t in range(4):
                width = 128 if t < 3 else 16
                for b in range(4):
                    part = table_ref[i, t * 128 : t * 128 + width, b * 128 : (b + 1) * 128]
                    if t == 3:
                        part = jnp.concatenate([part, jnp.zeros((112, 128), F32)], axis=0)
                    table[pl.ds(i * 64 + b * 16, 16), t] = part.T.reshape(16, 8, 128)
            return 0

        lax.fori_loop(0, 4, turn, 0)

    flat = table.reshape(256 * 32, 128)
    rows_flat = rows.reshape(STEP * octets * 32, 128)
    for d in range(STEP):
        g = step * STEP + d

        def fetch(q, _):
            k = (q + first) * 8
            for j in range(8):
                w = wanted_ref[2 * g + (k >> 7), (k & 127) + j]
                a = (w >> 3) * 32 + (w & 7)
                rows_flat[pl.ds((d * octets + q) * 32 + j, 4, stride=8), :] = flat[
                    pl.ds(a, 4, stride=8), :
                ]
            return 0

        lax.fori_loop(0, octets, fetch, 0, unroll=2)
    for q in range(octets):
        out_ref[:, 3 * q : 3 * q + 3] = rows[:, q, 0:3]
    for tile in range((octets + 7) // 8):
        rest = rows[:, tile * 8, 3]
        for q in range(tile * 8 + 1, min(octets, tile * 8 + 8)):
            rest = rest + pltpu.roll(rows[:, q, 3], 16 * (q & 7), 2)
        out_ref[:, 3 * octets + tile] = rest


def lookup(octets, first, wanted, tables):
    tiles = 3 * octets + (octets + 7) // 8
    return pl.pallas_call(
        functools.partial(lookup_kernel, octets, first),
        grid=(GROUP // STEP,),
        in_specs=[
            pl.BlockSpec(memory_space=pltpu.SMEM),
            pl.BlockSpec((4, WIDTH, ENT), lambda i: (0, 0, 0)),
        ],
        out_specs=pl.BlockSpec((STEP, tiles, 8, 128), lambda i: (i, 0, 0, 0)),
        out_shape=jax.ShapeDtypeStruct((GROUP, tiles, 8, 128), F32),
        scratch_shapes=[
            pltpu.VMEM((256, 4, 8, 128), F32),
            pltpu.VMEM((STEP, octets, 4, 8, 128), F32),
        ],
        compiler_params=pltpu.CompilerParams(vmem_limit_bytes=VMEM_LIMIT),
        name="lookup" if first == 0 else "lookup_over",
    )(wanted, tables)


BLOCK = 256


def math_kernel(
    addr_ref, flag_ref, pay_ref, over_ref, rel_ref, grad_ref, rel_grad_ref,
    rows, rest, hr_hi, hr_lo, n_hi, n_lo, g_neg, sems,
):
    def fill(source, octets, first, tile, sem):
        copies = [
            pltpu.make_async_copy(
                source.at[:, 3 * q : 3 * q + 3], rows.at[:, first + q, 0:3], sems.at[sem + 1 + q]
            )
            for q in range(octets)
        ]
        tiles = (octets + 7) // 8
        last = pltpu.make_async_copy(
            source.at[:, 3 * octets : 3 * octets + tiles],
            rest.at[:, tile : tile + tiles],
            sems.at[sem],
        )
        last.start()
        for copy in copies:
            copy.start()
        last.wait()
        lane = lax.broadcasted_iota(I32, (8, 8, 128), 2)

        def expand(i, _):
            for q in range(octets):
                part = rest[pl.ds(i * 8, 8), tile + (q >> 3)]
                if q & 7:
                    part = pltpu.roll(part, 128 - 16 * (q & 7), 2)
                rows[pl.ds(i * 8, 8), first + q, 3] = jnp.where(lane < 16, part, 0.0)
            return 0

        lax.fori_loop(0, GROUP // 8, expand, 0)
        for copy in copies:
            copy.wait()

    fill(pay_ref, MAIN, 0, 0, 0)

    @pl.when(flag_ref[0] > 0)
    def _():
        fill(over_ref, OVER, MAIN, 3, MAIN + 1)

    flat = rows.reshape(GROUP * OCT * 32, 128)
    grad_flat = grad_ref.reshape(384 * 32, 128)

    def gather(i, _):
        for j in range(8):
            a = addr_ref[i >> 4, (i & 15) * 8 + j]
            grad_flat[pl.ds(i * 32 + j, 4, stride=8), :] = flat[pl.ds(a, 4, stride=8), :]
        return 0

    lax.fori_loop(0, 384, gather, 0, unroll=4)

    def prepare(b, _):
        octets = pl.ds(b * 32, 32)
        edges = pl.ds(b * BLOCK, BLOCK)
        for t in range(4):
            lanes = slice(t * 128, (t + 1) * 128)
            hr = grad_ref[octets, t].reshape(BLOCK, 128) * rel_ref[edges, lanes]
            hr_hi[edges, lanes], hr_lo[edges, lanes] = split(hr)
            neg = grad_ref[pl.ds(256 + b * 32, 32), t].reshape(BLOCK, 128)
            n_hi[edges, lanes], n_lo[edges, lanes] = split(neg)
        return 0

    lax.fori_loop(0, EDGE // BLOCK, prepare, 0)
    g_neg[...] = jnp.zeros_like(g_neg)

    def block(b, _):
        edges = pl.ds(b * BLOCK, BLOCK)
        octets = pl.ds(b * 32, 32)
        tails = pl.ds(128 + b * 32, 32)
        a_hi, a_lo = hr_hi[edges, :], hr_lo[edges, :]
        score = dot(a_hi, n_hi[...], NT) + dot(a_hi, n_lo[...], NT) + dot(a_lo, n_hi[...], NT)
        p_hi, p_lo = split(1.0 / (1.0 + jnp.exp(-score)))
        g_hr = dot(p_hi, n_hi[...], NN) + dot(p_hi, n_lo[...], NN) + dot(p_lo, n_hi[...], NN)
        g_neg[...] += dot(p_hi, a_hi, TN) + dot(p_hi, a_lo, TN) + dot(p_lo, a_hi, TN)
        total = jnp.zeros((BLOCK, 128), F32)
        for t in range(4):
            lanes = slice(t * 128, (t + 1) * 128)
            hr = grad_ref[octets, t].reshape(BLOCK, 128) * rel_ref[edges, lanes]
            total = total + hr * grad_ref[tails, t].reshape(BLOCK, 128)
        positive = jnp.sum(total, axis=1, keepdims=True)
        d_pos = -1.0 / (1.0 + jnp.exp(positive))
        for t in range(4):
            lanes = slice(t * 128, (t + 1) * 128)
            head = grad_ref[octets, t].reshape(BLOCK, 128)
            tail = grad_ref[tails, t].reshape(BLOCK, 128)
            rel = rel_ref[edges, lanes]
            g = d_pos * tail + g_hr[:, lanes] * (1.0 / NEG)
            rel_grad_ref[octets, t] = (g * head).reshape(32, 8, 128)
            grad_ref[tails, t] = (d_pos * (head * rel)).reshape(32, 8, 128)
            grad_ref[octets, t] = (g * rel).reshape(32, 8, 128)
        return 0

    lax.fori_loop(0, EDGE // BLOCK, block, 0)
    for t in range(4):
        lanes = slice(t * 128, (t + 1) * 128)
        grad_ref[256:384, t] = (g_neg[:, lanes] * (1.0 / NEG)).reshape(128, 8, 128)


def math(addr, flag, arrived, over, rel_rows):
    return pl.pallas_call(
        math_kernel,
        in_specs=[
            pl.BlockSpec(memory_space=pltpu.SMEM),
            pl.BlockSpec(memory_space=pltpu.SMEM),
            pl.BlockSpec(memory_space=pl.ANY),
            pl.BlockSpec(memory_space=pl.ANY),
            pl.BlockSpec(memory_space=pltpu.VMEM),
        ],
        out_specs=(
            pl.BlockSpec(memory_space=pltpu.VMEM),
            pl.BlockSpec(memory_space=pltpu.VMEM),
        ),
        out_shape=(
            jax.ShapeDtypeStruct((384, 4, 8, 128), F32),
            jax.ShapeDtypeStruct((128, 4, 8, 128), F32),
        ),
        scratch_shapes=[
            pltpu.VMEM((GROUP, OCT, 4, 8, 128), F32),
            pltpu.VMEM((GROUP, 4, 8, 128), F32),
            pltpu.VMEM((EDGE, 512), BF16),
            pltpu.VMEM((EDGE, 512), BF16),
            pltpu.VMEM((NEG, 512), BF16),
            pltpu.VMEM((NEG, 512), BF16),
            pltpu.VMEM((NEG, 512), F32),
            pltpu.SemaphoreType.DMA((OCT + 2,)),
        ],
        compiler_params=pltpu.CompilerParams(vmem_limit_bytes=VMEM_LIMIT),
        name="math",
    )(addr, flag, arrived, over, rel_rows)


def relation_kernel(id_ref, grad_ref, out_ref, rows, packed, sems):
    zero = jnp.zeros((16, 4, 8, 128), F32)

    def clear(g, _):
        rows[pl.ds(g * 16, 16)] = zero
        return 0

    lax.fori_loop(0, RELGROUPS, clear, 0)
    flat = rows.reshape(REL * 4, 128)
    grad_flat = grad_ref.reshape(128 * 32, 128)

    def add(i, _):
        for j in range(8):
            r = id_ref[i >> 4, (i & 15) * 8 + j]
            at = pl.ds((r >> 3) * 32 + (r & 7), 4, stride=8)
            flat[at, :] = flat[at, :] + grad_flat[pl.ds(i * 32 + j, 4, stride=8), :]
        return 0

    lax.fori_loop(0, 128, add, 0, unroll=2)

    def copy(g):
        return pltpu.make_async_copy(
            packed.at[g & 1], out_ref.at[g], sems.at[g & 1]
        )

    def pack(g, _):
        @pl.when(g >= 2)
        def _():
            copy(g - 2).wait()

        for t in range(4):
            part = rows[pl.ds(g * 16, 16), t].reshape(128, 128).T
            if t < 3:
                packed[g & 1, pl.ds(t * 16, 16)] = part.reshape(16, 8, 128)
            else:
                packed[g & 1, 48:50] = part[:16].reshape(2, 8, 128)
        copy(g).start()
        return 0

    lax.fori_loop(0, RELGROUPS, pack, 0)
    copy(RELGROUPS - 2).wait()
    copy(RELGROUPS - 1).wait()


def relation_sum(ids, grad):
    return pl.pallas_call(
        relation_kernel,
        in_specs=[
            pl.BlockSpec(memory_space=pltpu.SMEM),
            pl.BlockSpec(memory_space=pltpu.VMEM),
        ],
        out_specs=pl.BlockSpec(memory_space=pl.ANY),
        out_shape=jax.ShapeDtypeStruct((RELGROUPS, 50, 8, 128), F32),
        scratch_shapes=[
            pltpu.VMEM((REL // 8, 4, 8, 128), F32),
            pltpu.VMEM((2, 50, 8, 128), F32),
            pltpu.SemaphoreType.DMA((2,)),
        ],
        compiler_params=pltpu.CompilerParams(vmem_limit_bytes=VMEM_LIMIT),
        name="relation_sum",
    )(ids, grad)


def pack_kernel(addr_ref, flag_ref, grad_ref, out_ref, over_ref, rows, rest, sems):
    zero = jnp.zeros((2, OCT, 4, 8, 128), F32)

    def clear(i, _):
        rows[pl.ds(i * 2, 2)] = zero
        return 0

    lax.fori_loop(0, GROUP // 2, clear, 0)
    flat = rows.reshape(GROUP * OCT * 32, 128)
    grad_flat = grad_ref.reshape(384 * 32, 128)

    def scatter(i, _):
        for j in range(8):
            a = addr_ref[i >> 4, (i & 15) * 8 + j]
            flat[pl.ds(a, 4, stride=8), :] = grad_flat[pl.ds(i * 32 + j, 4, stride=8), :]
        return 0

    lax.fori_loop(0, 384, scatter, 0, unroll=4)

    def send(target, octets, first, tile, sem):
        copies = [
            pltpu.make_async_copy(
                rows.at[:, first + q, 0:3], target.at[:, 3 * q : 3 * q + 3], sems.at[sem + 1 + q]
            )
            for q in range(octets)
        ]
        for copy in copies:
            copy.start()
        tiles = (octets + 7) // 8

        def pack(i, _):
            at = pl.ds(i * 8, 8)
            for n in range(tiles):
                part = rows[at, first + n * 8, 3]
                for q in range(n * 8 + 1, min(octets, n * 8 + 8)):
                    part = part + pltpu.roll(rows[at, first + q, 3], 16 * (q & 7), 2)
                rest[at, tile + n] = part
            return 0

        lax.fori_loop(0, GROUP // 8, pack, 0)
        last = pltpu.make_async_copy(
            rest.at[:, tile : tile + tiles],
            target.at[:, 3 * octets : 3 * octets + tiles],
            sems.at[sem],
        )
        last.start()
        for copy in copies:
            copy.wait()
        last.wait()

    send(out_ref, MAIN, 0, 0, 0)

    @pl.when(flag_ref[0] > 0)
    def _():
        send(over_ref, OVER, MAIN, 3, MAIN + 1)


def pack_grads(addr, flag, grads):
    return pl.pallas_call(
        pack_kernel,
        in_specs=[
            pl.BlockSpec(memory_space=pltpu.SMEM),
            pl.BlockSpec(memory_space=pltpu.SMEM),
            pl.BlockSpec(memory_space=pltpu.VMEM),
        ],
        out_specs=(
            pl.BlockSpec(memory_space=pl.ANY),
            pl.BlockSpec(memory_space=pl.ANY),
        ),
        out_shape=(
            jax.ShapeDtypeStruct((GROUP, MAIN_TILES, 8, 128), F32),
            jax.ShapeDtypeStruct((GROUP, OVER_TILES, 8, 128), F32),
        ),
        scratch_shapes=[
            pltpu.VMEM((GROUP, OCT, 4, 8, 128), F32),
            pltpu.VMEM((GROUP, 4, 8, 128), F32),
            pltpu.SemaphoreType.DMA((OCT + 2,)),
        ],
        compiler_params=pltpu.CompilerParams(vmem_limit_bytes=VMEM_LIMIT),
        name="pack_grads",
    )(addr, flag, grads)


SUM_STEP = 8


def row_sum_kernel(octets, wanted_ref, pay_ref, out_ref, hi, lo, total):
    step = pl.program_id(0)
    slots = SUM_STEP * octets * 8

    @pl.when(step == 0)
    def _():
        total[...] = jnp.zeros_like(total)

    lane = lax.broadcasted_iota(I32, (SUM_STEP, 8, 128), 2)
    for t in range(4):
        lanes = slice(t * 128, (t + 1) * 128)
        parts = []
        for q in range(octets):
            if t < 3:
                parts.append(pay_ref[:, q * 3 + t])
            else:
                part = pay_ref[:, 3 * octets + (q >> 3)]
                if q & 7:
                    part = pltpu.roll(part, 128 - 16 * (q & 7), 2)
                parts.append(jnp.where(lane < 16, part, 0.0))
        hi[:, lanes], lo[:, lanes] = split(jnp.stack(parts, axis=1).reshape(slots, 128))
    wanted = wanted_ref[...].reshape(1, slots)

    def add(i, _):
        row = lax.broadcasted_iota(I32, (ENT, slots), 0) + i * ENT
        onehot = (row == wanted).astype(F32).astype(BF16)
        total[i] = total[i] + (dot(onehot, hi[...], NN) + dot(onehot, lo[...], NN))
        return 0

    lax.fori_loop(0, 4, add, 0)

    @pl.when(step == pl.num_programs(0) - 1)
    def _():
        def turn(i, _):
            out_ref[i] = total[i].T[:WIDTH, :]
            return 0

        lax.fori_loop(0, 4, turn, 0)


def row_sum(octets, wanted, arrived):
    tiles = 3 * octets + (octets + 7) // 8
    slots = SUM_STEP * octets * 8
    return pl.pallas_call(
        functools.partial(row_sum_kernel, octets),
        grid=(GROUP // SUM_STEP,),
        in_specs=[
            pl.BlockSpec((1, 1, slots), lambda i: (i, 0, 0)),
            pl.BlockSpec((SUM_STEP, tiles, 8, 128), lambda i: (i, 0, 0, 0)),
        ],
        out_specs=pl.BlockSpec((4, WIDTH, ENT), lambda i: (0, 0, 0)),
        out_shape=jax.ShapeDtypeStruct((4, WIDTH, ENT), F32),
        scratch_shapes=[
            pltpu.VMEM((slots, 512), BF16),
            pltpu.VMEM((slots, 512), BF16),
            pltpu.VMEM((4, ENT, 512), F32),
        ],
        compiler_params=pltpu.CompilerParams(vmem_limit_bytes=VMEM_LIMIT),
        name="row_sum" if octets == MAIN else "row_sum_over",
    )(wanted, arrived)


def entity_kernel(grad_ref, table_ref, state_ref, new_table, new_state):
    grad = (grad_ref[0] + grad_ref[1]) + (grad_ref[2] + grad_ref[3])
    state = state_ref[...] + jnp.sum(grad * grad, axis=0, keepdims=True) / float(WIDTH)
    new_state[...] = state
    new_table[...] = table_ref[...] - learn_rate * grad / (jnp.sqrt(state) + adagrad_eps)


def entity_update(grads, table_t, state):
    return pl.pallas_call(
        entity_kernel,
        out_shape=(
            jax.ShapeDtypeStruct((WIDTH, ENT), F32),
            jax.ShapeDtypeStruct((1, ENT), F32),
        ),
        compiler_params=pltpu.CompilerParams(vmem_limit_bytes=VMEM_LIMIT),
        name="entity_update",
    )(grads, table_t, state)


def relation_update_kernel(grad_ref, table_ref, state_ref, new_table, new_state):
    step = pl.program_id(0)
    for g in range(2):
        lanes = slice(g * 128, (g + 1) * 128)
        at = pl.ds(step * 2 + g, 1)
        grad = grad_ref[g].reshape(WIDTH, 128)
        state = state_ref[at, :] + jnp.sum(grad * grad, axis=0, keepdims=True) / float(WIDTH)
        new_state[at, :] = state
        new_table[:, lanes] = table_ref[:, lanes] - grad * (
            learn_rate / (jnp.sqrt(state) + adagrad_eps)
        )


def relation_update(grad, table_t, state):
    return pl.pallas_call(
        relation_update_kernel,
        grid=(RELGROUPS // 2,),
        in_specs=[
            pl.BlockSpec((2, 50, 8, 128), lambda i: (i, 0, 0, 0)),
            pl.BlockSpec((WIDTH, 256), lambda i: (0, i)),
            pl.BlockSpec((RELGROUPS, 128), lambda i: (0, 0)),
        ],
        out_specs=(
            pl.BlockSpec((WIDTH, 256), lambda i: (0, i)),
            pl.BlockSpec((RELGROUPS, 128), lambda i: (0, 0)),
        ),
        out_shape=(
            jax.ShapeDtypeStruct((WIDTH, REL), F32),
            jax.ShapeDtypeStruct((RELGROUPS, 128), F32),
        ),
        compiler_params=pltpu.CompilerParams(vmem_limit_bytes=VMEM_LIMIT),
        name="relation_update",
    )(grad, table_t, state)


def exchange(x, axis):
    return lax.all_to_all(x, axis, split_axis=0, concat_axis=0, tiled=True)


def any_device(flag):
    largest = flag
    for k in (1, 2, 3):
        moved = lax.ppermute(flag, "rep", [(p, (p + k) % 4) for p in range(4)])
        largest = jnp.maximum(largest, moved)
    return largest


def per_device(
    entity_table,
    entity_state,
    relation_table,
    relation_state,
    end_owner,
    end_row,
    relation_id,
    negative_owner,
    negative_row,
):
    table_t = entity_table.T
    tables = lax.all_gather(table_t, "rep", axis=0, tiled=False)
    request, addr = prep(
        end_owner.T, end_row.T, negative_owner.reshape(1, NEG), negative_row.reshape(8, 128)
    )
    wanted = exchange(request.reshape(GROUP, 2, 128), "rows")
    flag = any_device(jnp.max(wanted[:, 1, FLAG]).reshape(1))
    over_now = flag[0] > 0
    wanted_rows = wanted.reshape(2 * GROUP, 128)
    arrived = exchange(lookup(MAIN, 0, wanted_rows, tables), "rows")
    over = lax.cond(
        over_now,
        lambda: exchange(lookup(OVER, MAIN, wanted_rows, tables), "rows"),
        lambda: jnp.zeros((GROUP, OVER_TILES, 8, 128), F32),
    )
    rel_rows = jnp.pad(relation_table[relation_id], ((0, 0), (0, 112)))
    grads, rel_grads = math(addr, flag, arrived, over, rel_rows)
    outgoing, outgoing_over = pack_grads(addr, flag, grads)
    incoming = exchange(outgoing, "rows")
    relation_grad = relation_sum(relation_id.reshape(8, 128), rel_grads)
    total_grad = lax.psum(relation_grad, AXES)
    slots = wanted.reshape(GROUP, 256)

    def ids(first, octets):
        part = slots[:, first * 8 : (first + octets) * 8]
        return part.reshape(GROUP // SUM_STEP, 1, SUM_STEP * octets * 8)

    summed = row_sum(MAIN, ids(0, MAIN), incoming)
    summed = lax.cond(
        over_now,
        lambda x: x + row_sum(OVER, ids(MAIN, OVER), exchange(outgoing_over, "rows")),
        lambda x: x,
        summed,
    )
    entity_grads = exchange(summed, "rep")
    new_entity_table, new_entity_state = entity_update(
        entity_grads, table_t, entity_state.reshape(1, ENT)
    )
    new_relation_table, new_relation_state = relation_update(
        total_grad, relation_table.T, relation_state.reshape(RELGROUPS, 128)
    )
    return (
        new_entity_table.T,
        new_entity_state.reshape(ENT),
        new_relation_table.T,
        new_relation_state.reshape(REL),
    )


def solution(mesh):
    return jax.shard_map(
        per_device,
        mesh=mesh,
        in_specs=(
            P(AXES, None),
            P(AXES),
            P(),
            P(),
            P(AXES, None),
            P(AXES, None),
            P(AXES),
            P(AXES, None),
            P(AXES),
        ),
        out_specs=(P(AXES, None), P(AXES), P(), P()),
        check_vma=False,
    )
```

time: 606 us -> 589 us (0.972)
  waiting for transfers between devices: 378 us -> 320 us
  starting transfers between devices: 14.2 us -> 50.1 us
  Pallas kernels: 146 us -> 170 us
  blocking collectives: 21.9 us -> 0 us
    psum x1, waiting for transfers between devices: 257 us -> 108 us  [per_device(): total_grad = lax.psum(relation_grad, AXES)]
    all_to_all x2 -> x4, waiting for transfers between devices: 121 us -> 197 us  [exchange(): return lax.all_to_all(x, axis, split_axis=0, concat_axis=0, tiled=True)]
    all_to_all x2 -> x4, starting transfers between devices: 14.2 us -> 45 us  [exchange(): return lax.all_to_all(x, axis, split_axis=0, concat_axis=0, tiled=True)]
    pallas_call x4 -> x5, Pallas kernels: 71.6 us -> 95.2 us  [the longest x1 37.2 us: row_sum(): pl.pallas_call(functools.partial(row_sum_kernel, octets), grid=(GROUP //...]
    all_to_all x1 -> x0, blocking collectives: 21.9 us -> none  [exchange(): return lax.all_to_all(x, AXES, split_axis=0, concat_axis=0, tiled=True)]
    all_gather x0 -> x1, waiting for transfers between devices: none -> 14.4 us  [per_device(): tables = lax.all_gather(table_t, 'rep', axis=0, tiled=False)]
    unnamed x7 -> x8, local copies, waits for them, and re-layouts: 14.1 us -> 15.8 us
  transfers between devices with their start and end apart: 3 -> 9, of which waited for: 2 -> 5; matrix products, arithmetic and copies ran while one was open for 5% -> 5% of each run, Pallas kernels for 9% -> 16%
where the time goes in v2:
time: 589 us; the launch traced here: 587 us
  waiting for transfers between devices  320 us (54%)
  Pallas kernels  170 us (29%)
  starting transfers between devices  50.1 us (9%)
  local copies, waits for them, and re-layouts  30.4 us (5%)
  between operations  16.8 us (3%)
    all_to_all x4, waiting for transfers between devices, exchange(): return lax.all_to_all(x, axis, split_axis=0, concat_axis=0, tiled=True)  197 us
    psum x1, waiting for transfers between devices, per_device(): total_grad = lax.psum(relation_grad, AXES)  108 us
    all_to_all x4, starting transfers between devices, exchange(): return lax.all_to_all(x, axis, split_axis=0, concat_axis=0, tiled=True)  45 us
    pallas_call x1, Pallas kernels, row_sum(): pl.pallas_call(functools.partial(row_sum_kernel, octets), grid=(GROUP //...  37.2 us
    pallas_call x1, Pallas kernels, relation_sum(): pl.pallas_call(relation_kernel, in_specs=[pl.BlockSpec(memory_space=pltpu...  31 us
    pallas_call x1, Pallas kernels, math(): pl.pallas_call(math_kernel, in_specs=[pl.BlockSpec(memory_space=pltpu.SME...  27.6 us
    pallas_call x1, Pallas kernels, lookup(): pl.pallas_call(functools.partial(lookup_kernel, octets, first), grid=(GRO...  25.9 us
    pallas_call x1, Pallas kernels, relation_update(): pl.pallas_call(relation_update_kernel, grid=(RELGROUPS // 2,), in_specs=[...  22.7 us
  transfers between devices with their start and end apart: 9, of which 5 were waited for; matrix products, arithmetic and copies ran while one was open for 5% of the time, Pallas kernels for 16%

profile of v2, /device:TPU:1, one launch (start us, length us, event | category | flops | bytes accessed | tf_op | source)
XLA Modules:
  0.0 587.4 jit_solution(16447882788065611572)
XLA Ops:
  7.2 0.0 all-gather.3.cloned.1.call-start
  7.2 0.7 all-gather.3.cloned.1.call-update
  7.9 5.9 %prep.1 = (s32[64,128]{1,0:T(8,128)}, s32[24,128]{1,0:T(8,128)}) custom-call(s32[2,1024]{1,0:T(2,128)} %bitcast.36, s32[2,1024]{1,0:T(2,128)} %bitcast.37, s32[1,1024]{1,0:T(1,128)} %bitcast.38, s32[8,128]{1,0:T(8,128)} %bitcast.39), custom_call_target="tpu_custom_call" | custom-call | tf_op jit(solution)/shard_map/prep/pallas_call | solution.py:79
  13.8 9.6 %all-to-all-start.2 = ((s32[32,2,128]{2,1,0:T(2,128)}), s32[32,2,128]{2,1,0:T(2,128)S(1)}, u32[]{:S(2)}, u32[]{:S(2)}) async-start(s32[32,2,128]{2,1,0:T(2,128)} %bitcast.34), calls=%async_computation.2 | async-start | bytes 65536 | tf_op jit(solution)/shard_map/all_to_all | solution.py:555
  23.4 7.3 %all-to-all-done.2 = s32[32,2,128]{2,1,0:T(2,128)S(1)} async-done(((s32[32,2,128]{2,1,0:T(2,128)}), s32[32,2,128]{2,1,0:T(2,128)S(1)}, u32[]{:S(2)}, u32[]{:S(2)}) %all-to-all-start.2) | async-done | bytes 32800 | tf_op jit(solution)/shard_map/all_to_all | solution.py:555
  30.7 0.7 slice_reduce_fusion
  31.4 1.2 collective-permute-start
  32.7 2.5 collective-permute-start.1
  35.1 1.2 collective-permute-start.2
  36.3 0.0 collective-permute-done
  37.6 0.0 collective-permute-done.1
  38.2 0.0 collective-permute-done.2
  38.9 14.4 %all-gather.3.cloned.1.call-done = f32[1600,512]{1,0:T(8,128)} async-done(((f32[400,512]{1,0:T(8,128)}), f32[1600,512]{1,0:T(8,128)}) %all-gather.3.cloned.1.call-update) | async-done | bytes 3276816 | tf_op jit(solution)/shard_map/all_gather | solution.py:578
  53.3 0.0 copy-start.1
  53.3 25.9 %lookup.1 = f32[32,69,8,128]{3,2,1,0:T(8,128)} custom-call(s32[64,128]{1,0:T(8,128)S(1)} %bitcast.28, f32[4,400,512]{2,1,0:T(8,128)} %bitcast.24), custom_call_target="tpu_custom_call" | custom-call | tf_op jit(solution)/shard_map/lookup/pallas_call | solution.py:136
  79.2 0.0 copy-done.1
  79.2 0.2 conditional.2
  79.2 0.2 broadcast.2
  79.4 7.9 %all-to-all-start.3 = ((f32[32,69,8,128]{3,2,1,0:T(8,128)}), f32[32,69,8,128]{3,2,1,0:T(8,128)}, u32[]{:S(2)}, u32[]{:S(2)}) async-start(f32[32,69,8,128]{3,2,1,0:T(8,128)} %lookup.1), calls=%async_computation.3 | async-start | bytes 18087936 | tf_op jit(solution)/shard_map/all_to_all | solution.py:555
  87.3 0.0 copy-start.3
  87.3 14.1 %copy.13 = f32[7424,400]{1,0:T(8,128)} copy(f32[7424,400]{0,1:T(8,128)} %param.15) | data formatting | bytes 23756800 | tf_op args[2]
  101.4 0.0 copy-done.3
  101.5 10.7 %gather_fusion = f32[1024,400]{1,0:T(8,128)} fusion(f32[7424,400]{1,0:T(8,128)} %copy.13, s32[1024]{0:T(1024)S(1)} %fusion), kind=kCustom, calls=%fused_computation | custom fusion | bytes 3280896 | tf_op jit(solution)/shard_map/gather | solution.py:592
  112.1 3.1 pad.4.rel_ref
  115.2 91.1 %all-to-all-done.3.pay_ref = f32[32,69,8,128]{3,2,1,0:T(8,128)} async-done(((f32[32,69,8,128]{3,2,1,0:T(8,128)}), f32[32,69,8,128]{3,2,1,0:T(8,128)}, u32[]{:S(2)}, u32[]{:S(2)}) %all-to-all-start.3) | async-done | bytes 9044000 | tf_op jit(solution)/shard_map/all_to_all | solution.py:555
  206.2 27.6 %math.1 = (f32[384,4,8,128]{3,2,1,0:T(8,128)}, f32[128,4,8,128]{3,2,1,0:T(8,128)}) custom-call(s32[24,128]{1,0:T(8,128)} %get-tuple-element.37.addr_ref, s32[1]{0:T(128)S(6)} %max.11.flag_ref, f32[32,69,8,128]{3,2,1,0:T(8,128)} %all-to-all-done.3.pay_ref, f32[32,19,8,128]{3,2,1,0:T(8,128)S(1)} %get-tuple-element.46.over_ref, f32[1024,512]{1,0:T(8,128)} %pad.4.rel_ref), custom_call_target="tpu_custom_call" | custom-call | tf_op jit(solution)/shard_map/math/pallas_call | solution.py:257
  233.8 15.8 %pack_grads.1 = (f32[32,69,8,128]{3,2,1,0:T(8,128)}, f32[32,19,8,128]{3,2,1,0:T(8,128)}) custom-call(s32[24,128]{1,0:T(8,128)} %get-tuple-element.37.addr_ref, s32[1]{0:T(128)S(6)} %max.11.flag_ref, f32[384,4,8,128]{3,2,1,0:T(8,128)} %get-tuple-element.38.grad_ref), custom_call_target="tpu_custom_call" | custom-call | tf_op jit(solution)/shard_map/pack_grads/pallas_call | solution.py:410
  249.6 23.8 %all-to-all-start.4 = ((f32[32,69,8,128]{3,2,1,0:T(8,128)}), f32[32,69,8,128]{3,2,1,0:T(8,128)}, u32[]{:S(2)}, u32[]{:S(2)}) async-start(f32[32,69,8,128]{3,2,1,0:T(8,128)} %get-tuple-element.39), calls=%async_computation.4 | async-start | bytes 18087936 | tf_op jit(solution)/shard_map/all_to_all | solution.py:555
  273.4 0.2 all-reduce.3.cloned.1.call-start
  273.7 31.0 %relation_sum.1 = f32[58,50,8,128]{3,2,1,0:T(8,128)} custom-call(s32[8,128]{1,0:T(8,128)} %bitcast.35, f32[128,4,8,128]{3,2,1,0:T(8,128)} %get-tuple-element.43.grad_ref), custom_call_target="tpu_custom_call" | custom-call | tf_op jit(solution)/shard_map/relation_sum/pallas_call | solution.py:334
  304.7 0.0 all-reduce.3.cloned.1.call-update
  304.7 0.7 reshape.56.wanted_ref
  305.4 98.2 %all-to-all-done.4.pay_ref = f32[32,69,8,128]{3,2,1,0:T(8,128)} async-done(((f32[32,69,8,128]{3,2,1,0:T(8,128)}), f32[32,69,8,128]{3,2,1,0:T(8,128)}, u32[]{:S(2)}, u32[]{:S(2)}) %all-to-all-start.4) | async-done | bytes 9044000 | tf_op jit(solution)/shard_map/all_to_all | solution.py:555
  403.7 37.2 %row_sum.1 = f32[4,400,512]{2,1,0:T(8,128)} custom-call(s32[4,1,1408]{2,1,0:T(1,128)} %reshape.56.wanted_ref, f32[32,69,8,128]{3,2,1,0:T(8,128)} %all-to-all-done.4.pay_ref), custom_call_target="tpu_custom_call" | custom-call | tf_op jit(solution)/shard_map/row_sum/pallas_call | solution.py:481
  440.9 3.7 all-to-all-start.5
  444.6 108.1 %all-reduce.3.cloned.1.call-done.grad_ref = f32[58,50,8,128]{3,2,1,0:T(8,128)} async-done(((f32[58,50,8,128]{3,2,1,0:T(8,128)}), f32[58,50,8,128]{3,2,1,0:T(8,128)}) %all-reduce.3.cloned.1.call-update) | async-done | bytes 11878416 | tf_op jit(solution)/shard_map/psum | solution.py:597
  552.7 22.7 %relation_update.1 = (f32[400,7424]{1,0:T(8,128)}, f32[58,128]{1,0:T(8,128)}) custom-call(f32[58,50,8,128]{3,2,1,0:T(8,128)} %all-reduce.3.cloned.1.call-done.grad_ref, f32[400,7424]{1,0:T(8,128)} %bitcast.23, f32[58,128]{1,0:T(8,128)} %bitcast.33), custom_call_target="tpu_custom_call" | custom-call | tf_op jit(solution)/shard_map/relation_update/pallas_call | solution.py:533
  575.4 0.0 all-to-all-done.5.grad_ref
  575.4 0.0 copy-start
  575.4 1.7 copy-done
  577.1 3.5 entity_update.1
  (3 shorter events, 0.0 us)
Async XLA Ops:
  7.2 46.1 %all-gather.3.cloned.1.call-start = ((), (), s32[]{:S(2)}) async-start(), calls=%async_computation.7 | async-start | bytes 4096000 | tf_op jit(solution)/shard_map/all_gather | solution.py:578
  13.8 16.9 %all-to-all-start.2 = ((s32[32,2,128]{2,1,0:T(2,128)}), s32[32,2,128]{2,1,0:T(2,128)S(1)}, u32[]{:S(2)}, u32[]{:S(2)}) async-start(s32[32,2,128]{2,1,0:T(2,128)} %bitcast.34), calls=%async_computation.2 | async-start | bytes 65536 | tf_op jit(solution)/shard_map/all_to_all | solution.py:555
  31.4 4.8 collective-permute-start
  32.7 4.9 collective-permute-start.1
  35.1 3.1 collective-permute-start.2
  53.3 25.9 %copy-start.1 = (f32[1600,512]{1,0:T(8,128)S(1)}, f32[1600,512]{1,0:T(8,128)}, u32[]{:S(2)}) copy-start(f32[1600,512]{1,0:T(8,128)} %all-gather.3.cloned.1.call-done) | copy-start | bytes 9830404
  79.4 126.9 %all-to-all-start.3 = ((f32[32,69,8,128]{3,2,1,0:T(8,128)}), f32[32,69,8,128]{3,2,1,0:T(8,128)}, u32[]{:S(2)}, u32[]{:S(2)}) async-start(f32[32,69,8,128]{3,2,1,0:T(8,128)} %lookup.1), calls=%async_computation.3 | async-start | bytes 18087936 | tf_op jit(solution)/shard_map/all_to_all | solution.py:555
  87.3 14.1 %copy-start.3 = (s32[1024]{0:T(1024)S(1)}, s32[1024]{0:T(1024)}, u32[]{:S(2)}) copy-start(s32[1024]{0:T(1024)} %param.19) | copy-start | bytes 12292
  249.6 154.0 %all-to-all-start.4 = ((f32[32,69,8,128]{3,2,1,0:T(8,128)}), f32[32,69,8,128]{3,2,1,0:T(8,128)}, u32[]{:S(2)}, u32[]{:S(2)}) async-start(f32[32,69,8,128]{3,2,1,0:T(8,128)} %get-tuple-element.39), calls=%async_computation.4 | async-start | bytes 18087936 | tf_op jit(solution)/shard_map/all_to_all | solution.py:555
  273.4 279.2 %all-reduce.3.cloned.1.call-start = ((), (), s32[]{:S(2)}) async-start(), calls=%async_computation.6 | async-start | bytes 23756800 | tf_op jit(solution)/shard_map/psum | solution.py:597
  440.9 134.5 %all-to-all-start.5 = ((f32[4,400,512]{2,1,0:T(8,128)}), f32[4,400,512]{2,1,0:T(8,128)S(1)}, u32[]{:S(2)}, u32[]{:S(2)}) async-start(f32[4,400,512]{2,1,0:T(8,128)} %get-tuple-element.47), calls=%async_computation.5 | async-start | bytes 6553600 | tf_op jit(solution)/shard_map/all_to_all | solution.py:555
  575.4 1.7 copy-start
Sparse Core Ops, SparseCore 0:
  9.6 43.5 all-gather.2
  304.8 247.7 all-reduce.2

commit v3 on v2

--- a/solution.py
+++ b/solution.py
@@ -16,15 +16,17 @@
 EDGE = 1024
 NEG = 1024
 GROUP = 32
-MAIN = 22
+MAIN = 24
 OCT = 28
 OVER = OCT - MAIN
 MAIN_TILES = 3 * MAIN + 3
 OVER_TILES = 3 * OVER + 1
 REL = 7424
 RELGROUPS = REL // 128
+SHARDS = 128
 VMEM_LIMIT = 60 * 1024 * 1024
 FLAG = 127
+COUNT = 126
 
 
 def dot(a, b, dims):
@@ -41,7 +43,7 @@
     return hi, (x - hi.astype(F32)).astype(BF16)
 
 
-def prep_kernel(end_owner, end_row, neg_owner, neg_row, request_ref, addr_ref):
+def prep_kernel(me_ref, end_owner, end_row, neg_owner, neg_row, request_ref, addr_ref):
     iota0 = lax.broadcasted_iota(I32, (128, 128), 0)
     upper = (iota0 < lax.broadcasted_iota(I32, (128, 128), 1)).astype(BF16)
     group = lax.broadcasted_iota(I32, (GROUP, 128), 0)
@@ -58,7 +60,8 @@
             owner = neg_owner[:, lanes]
             row = neg_row[i - 16 : i - 15, :]
         target = owner >> 2
-        value = (owner & 3) * ENT + row
+        near = (owner - me_ref[0]) & 3
+        value = near * (4 * ENT) + (row >> 3) * 32 + (row & 7)
         onehot = (group == target).astype(F32)
         earlier = dot(onehot.astype(BF16), upper, NN) + count
         rank = jnp.sum(onehot * earlier, axis=0, keepdims=True).astype(I32)
@@ -72,36 +75,54 @@
     flag = (most > 8.0 * MAIN).astype(F32)
     lane = lax.broadcasted_iota(I32, (2 * GROUP, 128), 1)
     mark = (lane == FLAG) & ((double & 1) == 1)
-    request_ref[...] = jnp.where(mark, flag, low + 256.0 * high).astype(I32)
-
-
-def prep(end_owner, end_row, neg_owner, neg_row):
+    pair = lax.broadcasted_iota(I32, (2 * GROUP, GROUP), 0) >> 1
+    same = pair == lax.broadcasted_iota(I32, (2 * GROUP, GROUP), 1)
+    half = (2.0 * jnp.floor(count * 0.5), count)
+    low_count = half[1] - half[0]
+    counts = dot(same.astype(F32).astype(BF16), (half[0] * 0.5).astype(BF16), NN) * 2.0
+    counts = counts + dot(same.astype(F32).astype(BF16), low_count.astype(BF16), NN)
+    request = jnp.where(mark, flag, low + 256.0 * high)
+    mark = (lane == COUNT) & ((double & 1) == 1)
+    request_ref[...] = jnp.where(mark, counts, request).astype(I32)
+
+
+def prep(me, end_owner, end_row, neg_owner, neg_row):
     return pl.pallas_call(
         prep_kernel,
         out_shape=(
             jax.ShapeDtypeStruct((2 * GROUP, 128), I32),
             jax.ShapeDtypeStruct((24, 128), I32),
         ),
+        in_specs=[pl.BlockSpec(memory_space=pltpu.SMEM)]
+        + [pl.BlockSpec(memory_space=pltpu.VMEM)] * 4,
         name="prep",
-    )(end_owner, end_row, neg_owner, neg_row)
+    )(me, end_owner, end_row, neg_owner, neg_row)
 
 
 STEP = 4
 
 
-def lookup_kernel(octets, first, wanted_ref, table_ref, out_ref, table, rows):
+def lookup_kernel(
+    octets, first, wanted_ref, own, right, across_a, across_b, left, out_ref, table, rows
+):
     step = pl.program_id(0)
 
     @pl.when(step == 0)
     def _():
-        def turn(i, _):
-            for t in range(4):
-                width = 128 if t < 3 else 16
-                for b in range(4):
-                    part = table_ref[i, t * 128 : t * 128 + width, b * 128 : (b + 1) * 128]
+        def turn(b, _):
+            lanes = pl.ds(pl.multiple_of(b * 128, 128), 128)
+            for i, parts in enumerate(((own,), (right,), (across_a, across_b), (left,))):
+                height = WIDTH // len(parts)
+                for t in range(4):
+                    pieces, low, high = [], t * 128, min(t * 128 + 128, WIDTH)
+                    for n, part in enumerate(parts):
+                        start, stop = max(low, n * height), min(high, (n + 1) * height)
+                        if start < stop:
+                            pieces.append(part[start - n * height : stop - n * height, lanes])
                     if t == 3:
-                        part = jnp.concatenate([part, jnp.zeros((112, 128), F32)], axis=0)
-                    table[pl.ds(i * 64 + b * 16, 16), t] = part.T.reshape(16, 8, 128)
+                        pieces.append(jnp.zeros((112, 128), F32))
+                    block = pieces[0] if len(pieces) == 1 else jnp.concatenate(pieces, axis=0)
+                    table[pl.ds(i * 64 + b * 16, 16), t] = block.T.reshape(16, 8, 128)
             return 0
 
         lax.fori_loop(0, 4, turn, 0)
@@ -110,18 +131,26 @@
     rows_flat = rows.reshape(STEP * octets * 32, 128)
     for d in range(STEP):
         g = step * STEP + d
+        used = (wanted_ref[2 * g + 1, COUNT] + 7) >> 3
+        used = jnp.clip(used - first, 0, octets)
 
         def fetch(q, _):
             k = (q + first) * 8
+            line, lane = 2 * g + (k >> 7), k & 127
             for j in range(8):
-                w = wanted_ref[2 * g + (k >> 7), (k & 127) + j]
-                a = (w >> 3) * 32 + (w & 7)
+                a = wanted_ref[line, lane + j]
                 rows_flat[pl.ds((d * octets + q) * 32 + j, 4, stride=8), :] = flat[
                     pl.ds(a, 4, stride=8), :
                 ]
             return 0
 
-        lax.fori_loop(0, octets, fetch, 0, unroll=2)
+        lax.fori_loop(0, used, fetch, 0)
+
+        def blank(q, _):
+            rows[d, q, 3] = jnp.zeros((8, 128), F32)
+            return 0
+
+        lax.fori_loop(used, octets, blank, 0)
     for q in range(octets):
         out_ref[:, 3 * q : 3 * q + 3] = rows[:, q, 0:3]
     for tile in range((octets + 7) // 8):
@@ -136,10 +165,8 @@
     return pl.pallas_call(
         functools.partial(lookup_kernel, octets, first),
         grid=(GROUP // STEP,),
-        in_specs=[
-            pl.BlockSpec(memory_space=pltpu.SMEM),
-            pl.BlockSpec((4, WIDTH, ENT), lambda i: (0, 0, 0)),
-        ],
+        in_specs=[pl.BlockSpec(memory_space=pltpu.SMEM)]
+        + [pl.BlockSpec(x.shape, lambda i: (0, 0)) for x in tables],
         out_specs=pl.BlockSpec((STEP, tiles, 8, 128), lambda i: (i, 0, 0, 0)),
         out_shape=jax.ShapeDtypeStruct((GROUP, tiles, 8, 128), F32),
         scratch_shapes=[
@@ -148,7 +175,7 @@
         ],
         compiler_params=pltpu.CompilerParams(vmem_limit_bytes=VMEM_LIMIT),
         name="lookup" if first == 0 else "lookup_over",
-    )(wanted, tables)
+    )(wanted, *tables)
 
 
 BLOCK = 256
@@ -293,8 +320,8 @@
         rows[pl.ds(g * 16, 16)] = zero
         return 0
 
-    lax.fori_loop(0, RELGROUPS, clear, 0)
-    flat = rows.reshape(REL * 4, 128)
+    lax.fori_loop(0, SHARDS // 2, clear, 0)
+    flat = rows.reshape(SHARDS * 256, 128)
     grad_flat = grad_ref.reshape(128 * 32, 128)
 
     def add(i, _):
@@ -304,11 +331,11 @@
             flat[at, :] = flat[at, :] + grad_flat[pl.ds(i * 32 + j, 4, stride=8), :]
         return 0
 
-    lax.fori_loop(0, 128, add, 0, unroll=2)
+    lax.fori_loop(0, 128, add, 0)
 
     def copy(g):
         return pltpu.make_async_copy(
-            packed.at[g & 1], out_ref.at[g], sems.at[g & 1]
+            packed.at[g & 1], out_ref.at[pl.ds(g * 4, 4)], sems.at[g & 1]
         )
 
     def pack(g, _):
@@ -316,18 +343,20 @@
         def _():
             copy(g - 2).wait()
 
-        for t in range(4):
-            part = rows[pl.ds(g * 16, 16), t].reshape(128, 128).T
-            if t < 3:
-                packed[g & 1, pl.ds(t * 16, 16)] = part.reshape(16, 8, 128)
-            else:
-                packed[g & 1, 48:50] = part[:16].reshape(2, 8, 128)
+        for n in range(4):
+            first = g * 32 + n * 8
+            for t in range(3):
+                packed[g & 1, n, t * 8 : t * 8 + 8] = rows[pl.ds(first, 8), t]
+            rest = rows[first, 3]
+            for q in range(1, 8):
+                rest = rest + pltpu.roll(rows[first + q, 3], 16 * q, 1)
+            packed[g & 1, n, 24] = rest
         copy(g).start()
         return 0
 
-    lax.fori_loop(0, RELGROUPS, pack, 0)
-    copy(RELGROUPS - 2).wait()
-    copy(RELGROUPS - 1).wait()
+    lax.fori_loop(0, SHARDS // 4, pack, 0)
+    copy(SHARDS // 4 - 2).wait()
+    copy(SHARDS // 4 - 1).wait()
 
 
 def relation_sum(ids, grad):
@@ -338,10 +367,10 @@
             pl.BlockSpec(memory_space=pltpu.VMEM),
         ],
         out_specs=pl.BlockSpec(memory_space=pl.ANY),
-        out_shape=jax.ShapeDtypeStruct((RELGROUPS, 50, 8, 128), F32),
+        out_shape=jax.ShapeDtypeStruct((SHARDS, 25, 8, 128), F32),
         scratch_shapes=[
-            pltpu.VMEM((REL // 8, 4, 8, 128), F32),
-            pltpu.VMEM((2, 50, 8, 128), F32),
+            pltpu.VMEM((SHARDS * 8, 4, 8, 128), F32),
+            pltpu.VMEM((2, 4, 25, 8, 128), F32),
             pltpu.SemaphoreType.DMA((2,)),
         ],
         compiler_params=pltpu.CompilerParams(vmem_limit_bytes=VMEM_LIMIT),
@@ -459,7 +488,8 @@
     wanted = wanted_ref[...].reshape(1, slots)
 
     def add(i, _):
-        row = lax.broadcasted_iota(I32, (ENT, slots), 0) + i * ENT
+        row = lax.broadcasted_iota(I32, (ENT, slots), 0)
+        row = i * (4 * ENT) + (row >> 3) * 32 + (row & 7)
         onehot = (row == wanted).astype(F32).astype(BF16)
         total[i] = total[i] + (dot(onehot, hi[...], NN) + dot(onehot, lo[...], NN))
         return 0
@@ -516,28 +546,74 @@
     )(grads, table_t, state)
 
 
-def relation_update_kernel(grad_ref, table_ref, state_ref, new_table, new_state):
-    step = pl.program_id(0)
+def relation_update_kernel(shard_ref, grad_ref, table_ref, state_ref, out_ref, table, sem):
+    shard = shard_ref[0]
+    group = jnp.minimum(shard >> 1, RELGROUPS - 1)
+    lanes = pl.ds(pl.multiple_of(group * 128, 128), 128)
+    copy = pltpu.make_async_copy(table_ref.at[:, lanes], table, sem)
+    copy.start()
+    odd = (shard & 1) == 1
+    blank = jnp.zeros((64, 128), F32)
+    parts = []
+    for t in range(4):
+        if t < 3:
+            part = grad_ref[t * 8 : t * 8 + 8].reshape(64, 128)
+        else:
+            rest = grad_ref[24]
+            part = jnp.concatenate(
+                [rest] + [pltpu.roll(rest, 128 - 16 * q, 1) for q in range(1, 8)], axis=0
+            )
+        both = jnp.concatenate(
+            [jnp.where(odd, 0.0, part), jnp.where(odd, part, 0.0)], axis=0
+        ).T
+        parts.append(both if t < 3 else both[:16])
+    grad = jnp.concatenate(parts, axis=0)
+    state = state_ref[pl.ds(group, 1), :]
+    state = state + jnp.sum(grad * grad, axis=0, keepdims=True) / float(WIDTH)
+    copy.wait()
+    new = table[...] - grad * (learn_rate / (jnp.sqrt(state) + adagrad_eps))
+    top, bottom = new[: WIDTH // 2], new[WIDTH // 2 :]
+    low = lax.broadcasted_iota(I32, (WIDTH // 2, 128), 1) < 64
+    even_rows = jnp.where(low, top, pltpu.roll(bottom, 64, 1))
+    odd_rows = jnp.where(low, pltpu.roll(top, 64, 1), bottom)
+    out_ref[0:25] = jnp.where(odd, odd_rows, even_rows).reshape(25, 8, 128)
+    out_ref[25] = jnp.broadcast_to(state, (8, 128))
+
+
+def relation_update(shard, grad, table_t, state):
+    return pl.pallas_call(
+        relation_update_kernel,
+        in_specs=[
+            pl.BlockSpec(memory_space=pltpu.SMEM),
+            pl.BlockSpec(memory_space=pltpu.VMEM),
+            pl.BlockSpec(memory_space=pl.ANY),
+            pl.BlockSpec(memory_space=pltpu.VMEM),
+        ],
+        out_specs=pl.BlockSpec(memory_space=pltpu.VMEM),
+        out_shape=jax.ShapeDtypeStruct((26, 8, 128), F32),
+        scratch_shapes=[pltpu.VMEM((WIDTH, 128), F32), pltpu.SemaphoreType.DMA],
+        compiler_params=pltpu.CompilerParams(vmem_limit_bytes=VMEM_LIMIT),
+        name="relation_update",
+    )(shard, grad, table_t, state)
+
+
+def unpack_kernel(shards_ref, new_table, new_state):
+    low = lax.broadcasted_iota(I32, (WIDTH // 2, 128), 1) < 64
     for g in range(2):
         lanes = slice(g * 128, (g + 1) * 128)
-        at = pl.ds(step * 2 + g, 1)
-        grad = grad_ref[g].reshape(WIDTH, 128)
-        state = state_ref[at, :] + jnp.sum(grad * grad, axis=0, keepdims=True) / float(WIDTH)
-        new_state[at, :] = state
-        new_table[:, lanes] = table_ref[:, lanes] - grad * (
-            learn_rate / (jnp.sqrt(state) + adagrad_eps)
-        )
-
-
-def relation_update(grad, table_t, state):
-    return pl.pallas_call(
-        relation_update_kernel,
+        even = shards_ref[2 * g, 0, 0:25].reshape(WIDTH // 2, 128)
+        odd = shards_ref[2 * g + 1, 0, 0:25].reshape(WIDTH // 2, 128)
+        new_table[: WIDTH // 2, lanes] = jnp.where(low, even, pltpu.roll(odd, 64, 1))
+        new_table[WIDTH // 2 :, lanes] = jnp.where(low, pltpu.roll(even, 64, 1), odd)
+        state = jnp.where(low[:8], shards_ref[2 * g, 0, 25], shards_ref[2 * g + 1, 0, 25])
+        new_state[pl.ds(pl.program_id(0) * 2 + g, 1), :] = state[0:1]
+
+
+def unpack(shards):
+    return pl.pallas_call(
+        unpack_kernel,
         grid=(RELGROUPS // 2,),
-        in_specs=[
-            pl.BlockSpec((2, 50, 8, 128), lambda i: (i, 0, 0, 0)),
-            pl.BlockSpec((WIDTH, 256), lambda i: (0, i)),
-            pl.BlockSpec((RELGROUPS, 128), lambda i: (0, 0)),
-        ],
+        in_specs=[pl.BlockSpec((4, 1, 26, 8, 128), lambda i: (i & 7, i >> 3, 0, 0, 0))],
         out_specs=(
             pl.BlockSpec((WIDTH, 256), lambda i: (0, i)),
             pl.BlockSpec((RELGROUPS, 128), lambda i: (0, 0)),
@@ -547,8 +623,8 @@
             jax.ShapeDtypeStruct((RELGROUPS, 128), F32),
         ),
         compiler_params=pltpu.CompilerParams(vmem_limit_bytes=VMEM_LIMIT),
-        name="relation_update",
-    )(grad, table_t, state)
+        name="unpack",
+    )(shards)
 
 
 def exchange(x, axis):
@@ -575,26 +651,44 @@
     negative_row,
 ):
     table_t = entity_table.T
-    tables = lax.all_gather(table_t, "rep", axis=0, tiled=False)
+    to_right = [(p, (p + 1) % 4) for p in range(4)]
+    to_left = [(p, (p + 3) % 4) for p in range(4)]
+    left = lax.ppermute(table_t, "rep", to_right)
+    right = lax.ppermute(table_t, "rep", to_left)
+    across_a = lax.ppermute(left[: WIDTH // 2], "rep", to_right)
+    across_b = lax.ppermute(right[WIDTH // 2 :], "rep", to_left)
+    tables = (table_t, right, across_a, across_b, left)
+    rows_at, rep_at = lax.axis_index("rows"), lax.axis_index("rep")
     request, addr = prep(
+        rep_at.reshape(1),
         end_owner.T, end_row.T, negative_owner.reshape(1, NEG), negative_row.reshape(8, 128)
     )
     wanted = exchange(request.reshape(GROUP, 2, 128), "rows")
+    wanted_rows = wanted.reshape(2 * GROUP, 128)
+    looked = lookup(MAIN, 0, wanted_rows, tables)
+    arrived = exchange(looked, "rows")
     flag = any_device(jnp.max(wanted[:, 1, FLAG]).reshape(1))
     over_now = flag[0] > 0
-    wanted_rows = wanted.reshape(2 * GROUP, 128)
-    arrived = exchange(lookup(MAIN, 0, wanted_rows, tables), "rows")
-    over = lax.cond(
+    rel_rows = jnp.pad(relation_table[relation_id], ((0, 0), (0, 112)))
+    grads, rel_grads = lax.cond(
         over_now,
-        lambda: exchange(lookup(OVER, MAIN, wanted_rows, tables), "rows"),
-        lambda: jnp.zeros((GROUP, OVER_TILES, 8, 128), F32),
-    )
-    rel_rows = jnp.pad(relation_table[relation_id], ((0, 0), (0, 112)))
-    grads, rel_grads = math(addr, flag, arrived, over, rel_rows)
+        lambda x: math(
+            addr, flag, x, exchange(lookup(OVER, MAIN, wanted_rows, tables), "rows"), rel_rows
+        ),
+        lambda x: math(addr, flag, x, x, rel_rows),
+        arrived,
+    )
+    relation_grad = relation_sum(relation_id.reshape(8, 128), rel_grads)
+    grads, relation_grad = lax.optimization_barrier((grads, relation_grad))
+    part_grad = lax.psum_scatter(
+        relation_grad.reshape(4, GROUP, 25, 8, 128), "rep", scatter_dimension=0, tiled=True
+    )
     outgoing, outgoing_over = pack_grads(addr, flag, grads)
     incoming = exchange(outgoing, "rows")
-    relation_grad = relation_sum(relation_id.reshape(8, 128), rel_grads)
-    total_grad = lax.psum(relation_grad, AXES)
+    incoming, part_grad = lax.optimization_barrier((incoming, part_grad))
+    shard_grad = lax.psum_scatter(
+        part_grad.reshape(GROUP, 25, 8, 128), "rows", scatter_dimension=0, tiled=True
+    )
     slots = wanted.reshape(GROUP, 256)
 
     def ids(first, octets):
@@ -602,19 +696,25 @@
         return part.reshape(GROUP // SUM_STEP, 1, SUM_STEP * octets * 8)
 
     summed = row_sum(MAIN, ids(0, MAIN), incoming)
+    summed, shard_grad = lax.optimization_barrier((summed, shard_grad))
     summed = lax.cond(
         over_now,
         lambda x: x + row_sum(OVER, ids(MAIN, OVER), exchange(outgoing_over, "rows")),
         lambda x: x,
         summed,
     )
-    entity_grads = exchange(summed, "rep")
+    entity_grads = exchange(jnp.roll(summed, rep_at, axis=0), "rep")
     new_entity_table, new_entity_state = entity_update(
         entity_grads, table_t, entity_state.reshape(1, ENT)
     )
-    new_relation_table, new_relation_state = relation_update(
-        total_grad, relation_table.T, relation_state.reshape(RELGROUPS, 128)
-    )
+    new_shard = relation_update(
+        (rep_at * GROUP + rows_at).reshape(1),
+        shard_grad.reshape(25, 8, 128),
+        relation_table.T,
+        relation_state.reshape(RELGROUPS, 128),
+    )
+    shards = lax.all_gather(new_shard, AXES, axis=0, tiled=False)
+    new_relation_table, new_relation_state = unpack(shards.reshape(GROUP, 4, 26, 8, 128))
     return (
         new_entity_table.T,
         new_entity_state.reshape(ENT),

time: 589 us -> 594 us (level)
  blocking collectives: 0 us -> 198 us
  waiting for transfers between devices: 320 us -> 184 us
  starting transfers between devices: 50.1 us -> 16.3 us
  Pallas kernels: 170 us -> 149 us
    all_to_all x0 -> x3, blocking collectives: none -> 198 us  [exchange(): return lax.all_to_all(x, axis, split_axis=0, concat_axis=0, tiled=True)]
    psum x1 -> x0, waiting for transfers between devices: 108 us -> none  [per_device(): total_grad = lax.psum(relation_grad, AXES)]
    all_to_all x4 -> x1, waiting for transfers between devices: 197 us -> 96.2 us  [exchange(): return lax.all_to_all(x, axis, split_axis=0, concat_axis=0, tiled=True)]
    all_to_all x4 -> x1, starting transfers between devices: 45 us -> 8.42 us  [exchange(): return lax.all_to_all(x, axis, split_axis=0, concat_axis=0, tiled=True)]
    optimization_barrier x0 -> x1, waiting for transfers between devices: none -> 34 us  [per_device(): summed, shard_grad = lax.optimization_barrier((summed, shard_grad))]
    ppermute x0 -> x4, waiting for transfers between devices: none -> 17.7 us  [the longest x1 17.7 us: per_device(): left = lax.ppermute(table_t, 'rep', to_right)]
    all_gather x1, waiting for transfers between devices: 14.4 us -> 31.8 us  [per_device(): shards = lax.all_gather(new_shard, AXES, axis=0, tiled=False)]
    pallas_call x1, Pallas kernels: 25.9 us -> 15.7 us  [lookup(): pl.pallas_call(functools.partial(lookup_kernel, octets, first), grid=(GRO...]
  transfers between devices with their start and end apart: 9 -> 11, of which waited for: 5 -> 5; matrix products, arithmetic and copies ran while one was open for 5% -> 5% of each run, Pallas kernels for 16% -> 10%
where the time goes in v3:
time: 594 us; the launch traced here: 593 us
  blocking collectives  198 us (33%)
  waiting for transfers between devices  184 us (31%)
  Pallas kernels  149 us (25%)
  local copies, waits for them, and re-layouts  27.4 us (5%)
  between operations  16.5 us (3%)
  starting transfers between devices  16.3 us (3%)
    all_to_all x3, blocking collectives, exchange(): return lax.all_to_all(x, axis, split_axis=0, concat_axis=0, tiled=True)  198 us
    all_to_all x1, waiting for transfers between devices, exchange(): return lax.all_to_all(x, axis, split_axis=0, concat_axis=0, tiled=True)  96.2 us
    pallas_call x1, Pallas kernels, row_sum(): pl.pallas_call(functools.partial(row_sum_kernel, octets), grid=(GROUP //...  36 us
    optimization_barrier x1, waiting for transfers between devices, per_device(): summed, shard_grad = lax.optimization_barrier((summed, shard_grad))  34 us
    all_gather x1, waiting for transfers between devices, per_device(): shards = lax.all_gather(new_shard, AXES, axis=0, tiled=False)  31.8 us
    pallas_call x1, Pallas kernels, math(): pl.pallas_call(math_kernel, in_specs=[pl.BlockSpec(memory_space=pltpu.SME...  26.9 us
    pallas_call x1, Pallas kernels, relation_sum(): pl.pallas_call(relation_kernel, in_specs=[pl.BlockSpec(memory_space=pltpu...  21.4 us
    pallas_call x1, Pallas kernels, unpack(): pl.pallas_call(unpack_kernel, grid=(RELGROUPS // 2,), in_specs=[pl.BlockS...  21.4 us
  transfers between devices with their start and end apart: 11, of which 5 were waited for; matrix products, arithmetic and copies ran while one was open for 5% of the time, Pallas kernels for 10%

profile of v3, /device:TPU:1, one launch (start us, length us, event | category | flops | bytes accessed | tf_op | source)
XLA Modules:
  0.0 593.2 jit_solution(7368647187052324553)
XLA Ops:
  7.2 2.1 collective-permute-start.4
  9.3 1.4 collective-permute-start.3
  10.6 17.7 %collective-permute-done.4.left = f32[400,512]{1,0:T(8,128)S(1)} collective-permute-done((f32[400,512]{1,0:T(8,128)}, f32[400,512]{1,0:T(8,128)S(1)}, u32[]{:S(2)}, u32[]{:S(2)}) %collective-permute-start.4) | collective-permute-done | bytes 819232 | tf_op jit(solution)/shard_map/ppermute | solution.py:656
  28.4 0.3 collective-permute-start.5
  28.7 0.0 collective-permute-done.3.right
  28.7 2.5 collective-permute-start.6
  31.2 6.0 %prep.1 = (s32[64,128]{1,0:T(8,128)}, s32[24,128]{1,0:T(8,128)S(1)}) custom-call(s32[1]{0:T(128)} %bitcast.me_ref, s32[2,1024]{1,0:T(2,128)} %bitcast.47, s32[2,1024]{1,0:T(2,128)} %bitcast.48, s32[1,1024]{1,0:T(1,128)} %bitcast.49, s32[8,128]{1,0:T(8,128)} %bitcast.50), custom_call_target="tpu_custom_call" | custom-call | tf_op jit(solution)/shard_map/prep/pallas_call | solution.py:90
  37.2 17.7 %all_to_all.29 = s32[32,2,128]{2,1,0:T(2,128)S(1)} all-to-all(s32[32,2,128]{2,1,0:T(2,128)} %bitcast.45), channel_id=1, replica_groups=mesh['rows'=32,'rep'=4] {'rows'}, dimensions={0} | all-to-all | bytes 65536 | tf_op jit(solution)/shard_map/all_to_all | solution.py:631
  55.0 0.0 collective-permute-done.5.across_a
  55.0 0.0 collective-permute-done.6.across_b
  55.0 15.7 %lookup.1 = f32[32,75,8,128]{3,2,1,0:T(8,128)} custom-call(s32[64,128]{1,0:T(8,128)S(1)} %bitcast.38, f32[400,512]{1,0:T(8,128)} %bitcast.34, f32[400,512]{1,0:T(8,128)S(1)} %collective-permute-done.3.right, f32[200,512]{1,0:T(8,128)S(1)} %collective-permute-done.5.across_a, f32[200,512]{1,0:T(8,128)S(1)} %collective-permute-done.6.across_b, ...), custom_call_target="tpu_custom_call" | custom-call | tf_op jit(solution)/shard_map/lookup/pallas_call | solution.py:165
  70.7 0.0 copy-done.4
  70.7 8.4 %all-to-all-start.3 = ((f32[32,75,8,128]{3,2,1,0:T(8,128)}), f32[32,75,8,128]{3,2,1,0:T(8,128)}, u32[]{:S(2)}, u32[]{:S(2)}) async-start(f32[32,75,8,128]{3,2,1,0:T(8,128)} %lookup.1), calls=%async_computation.3 | async-start | bytes 19660800 | tf_op jit(solution)/shard_map/all_to_all | solution.py:631
  79.1 0.0 copy-start.5
  79.1 0.0 reduce-scatter.5.cloned.1.call-start
  79.2 14.2 %copy.14 = f32[7424,400]{1,0:T(8,128)} copy(f32[7424,400]{0,1:T(8,128)} %param.15) | data formatting | bytes 23756800 | tf_op args[2]
  93.4 0.0 copy-done.5
  93.4 10.6 %gather_fusion = f32[1024,400]{1,0:T(8,128)} fusion(f32[7424,400]{1,0:T(8,128)} %copy.14, s32[1024]{0:T(1024)S(1)} %fusion.1), kind=kCustom, calls=%fused_computation | custom fusion | bytes 3280896 | tf_op jit(solution)/shard_map/gather | solution.py:672
  104.0 1.8 pad.4
  105.9 0.7 slice_reduce_fusion
  106.6 0.0 collective-permute-start.2
  106.6 0.6 collective-permute-start.1
  107.2 0.9 collective-permute-start
  108.1 3.9 collective-permute-done
  113.3 0.0 collective-permute-done.1
  113.9 0.0 collective-permute-done.2
  114.6 96.2 %all-to-all-done.3 = f32[32,75,8,128]{3,2,1,0:T(8,128)} async-done(((f32[32,75,8,128]{3,2,1,0:T(8,128)}), f32[32,75,8,128]{3,2,1,0:T(8,128)}, u32[]{:S(2)}, u32[]{:S(2)}) %all-to-all-start.3) | async-done | bytes 9830432 | tf_op jit(solution)/shard_map/all_to_all | solution.py:631
  210.9 0.0 copy-done
  210.9 27.1 %conditional.2 = ((f32[384,4,8,128]{3,2,1,0:T(8,128)}, f32[128,4,8,128]{3,2,1,0:T(8,128)})) conditional(s32[]{:T(128)} %bitcast.7, (s32[24,128]{1,0:T(8,128)S(1)}, s32[1]{0:T(128)}, f32[32,75,8,128]{3,2,1,0:T(8,128)}, f32[1024,512]{1,0:T(8,128)S(1)}) %tuple.23, (s32[64,128]{1,0:T(8,128)S(1)}, f32[400,512]{1,0:T(8,128)S(1)}, f32[400,512]{1,0:T(8,128)}, ...), branch_computations={%region_1.2_spmd, %region_2.3_spmd} | conditional | bytes 3407880 | solution.py:673
  210.9 26.9 %math.2 = (f32[384,4,8,128]{3,2,1,0:T(8,128)}, f32[128,4,8,128]{3,2,1,0:T(8,128)}) custom-call(s32[24,128]{1,0:T(8,128)S(1)} %get-tuple-element.38.addr_ref, s32[1]{0:T(128)} %get-tuple-element.39.flag_ref, f32[32,75,8,128]{3,2,1,0:T(8,128)} %get-tuple-element.40.pay_ref.over_ref, f32[32,75,8,128]{3,2,1,0:T(8,128)} %get-tuple-element.40.pay_ref.over_ref, ...), custom_call_target="tpu_custom_call" | custom-call | tf_op jit(solution)/shard_map/cond/branch_0_fun/math/pallas_call | solution.py:284
  238.0 21.4 %relation_sum.1 = f32[128,25,8,128]{3,2,1,0:T(8,128)} custom-call(s32[8,128]{1,0:T(8,128)} %bitcast.46, f32[128,4,8,128]{3,2,1,0:T(8,128)} %get-tuple-element.78.grad_ref), custom_call_target="tpu_custom_call" | custom-call | tf_op jit(solution)/shard_map/relation_sum/pallas_call | solution.py:363
  259.4 0.0 reduce-scatter.5.cloned.1.call-update
  259.4 0.0 reduce-scatter.7.cloned.1.call-start
  259.5 16.0 %pack_grads.1 = (f32[32,75,8,128]{3,2,1,0:T(8,128)}, f32[32,13,8,128]{3,2,1,0:T(8,128)}) custom-call(s32[24,128]{1,0:T(8,128)S(1)} %get-tuple-element.76.addr_ref, s32[1]{0:T(128)} %max.11.flag_ref, f32[384,4,8,128]{3,2,1,0:T(8,128)} %get-tuple-element.79.grad_ref), custom_call_target="tpu_custom_call" | custom-call | tf_op jit(solution)/shard_map/pack_grads/pallas_call | solution.py:439
  275.5 136.4 %all_to_all.30.pay_ref = f32[32,75,8,128]{3,2,1,0:T(8,128)} all-to-all(f32[32,75,8,128]{3,2,1,0:T(8,128)} %get-tuple-element.80), channel_id=1, replica_groups=mesh['rows'=32,'rep'=4] {'rows'}, dimensions={0} | all-to-all | bytes 19660800 | tf_op jit(solution)/shard_map/all_to_all | solution.py:631
  411.9 0.0 reduce-scatter.7.cloned.1.call-update
  411.9 0.0 all-gather.3.cloned.1.call-start
  411.9 0.7 reshape.75.wanted_ref
  412.6 36.0 %row_sum.1 = f32[4,400,512]{2,1,0:T(8,128)S(1)} custom-call(s32[4,1,1536]{2,1,0:T(1,128)} %reshape.75.wanted_ref, f32[32,75,8,128]{3,2,1,0:T(8,128)} %all_to_all.30.pay_ref), custom_call_target="tpu_custom_call" | custom-call | tf_op jit(solution)/shard_map/row_sum/pallas_call | solution.py:511
  448.7 34.0 %reduce-scatter.7.cloned.1.call-done = f32[1,25,8,128]{3,2,1,0:T(8,128)} async-done(((f32[32,25,8,128]{3,2,1,0:T(8,128)}), f32[1,25,8,128]{3,2,1,0:T(8,128)}) %reduce-scatter.7.cloned.1.call-update) | async-done | bytes 102416 | tf_op jit(solution)/shard_map/optimization_barrier | solution.py:699
  482.7 2.6 relation_update.1
  485.3 0.0 all-gather.3.cloned.1.call-update
  485.4 0.8 fusion
  486.2 0.0 copy-start.1
  486.3 44.0 %all_to_all.31.grad_ref = f32[4,400,512]{2,1,0:T(8,128)} all-to-all(f32[4,400,512]{2,1,0:T(8,128)S(1)} %fusion), channel_id=1, replica_groups=mesh['rows'=32,'rep'=4] {'rep'}, dimensions={0} | all-to-all | bytes 6553600 | tf_op jit(solution)/shard_map/all_to_all | solution.py:631
  530.3 3.2 entity_update.1
  533.5 31.8 %all-gather.3.cloned.1.call-done = f32[3328,8,128]{2,1,0:T(8,128)} async-done(((f32[26,8,128]{2,1,0:T(8,128)}), f32[3328,8,128]{2,1,0:T(8,128)}) %all-gather.3.cloned.1.call-update) | async-done | bytes 13631504 | tf_op jit(solution)/shard_map/all_gather | solution.py:716
  565.3 21.4 %unpack.1 = (f32[400,7424]{1,0:T(8,128)}, f32[58,128]{1,0:T(8,128)}) custom-call(f32[32,4,26,8,128]{4,3,2,1,0:T(8,128)} %bitcast.31), custom_call_target="tpu_custom_call" | custom-call | tf_op jit(solution)/shard_map/unpack/pallas_call | solution.py:613
  (13 shorter events, 0.1 us)
Async XLA Ops:
  7.2 21.2 %collective-permute-start.4 = (f32[400,512]{1,0:T(8,128)}, f32[400,512]{1,0:T(8,128)S(1)}, u32[]{:S(2)}, u32[]{:S(2)}) collective-permute-start(f32[400,512]{1,0:T(8,128)} %bitcast.32), channel_id=1, source_target_pairs={{0,1},{1,2},{2,3},{3,0},{4,5},{5,6},{6,7},{7,4},{8,9},{9,10},{10,1... | collective-permute-start | bytes 2457608 | tf_op jit(solution)/shard_map/ppermute | solution.py:656
  9.3 19.4 %collective-permute-start.3 = (f32[400,512]{1,0:T(8,128)}, f32[400,512]{1,0:T(8,128)S(1)}, u32[]{:S(2)}, u32[]{:S(2)}) collective-permute-start(f32[400,512]{1,0:T(8,128)} %bitcast.33), channel_id=1, source_target_pairs={{0,3},{1,0},{2,1},{3,2},{4,7},{5,4},{6,5},{7,6},{8,11},{9,8},{10,9... | collective-permute-start | bytes 2457608 | tf_op jit(solution)/shard_map/ppermute | solution.py:657
  28.3 42.4 %copy-start.2 = (f32[400,512]{1,0:T(8,128)}, f32[400,512]{1,0:T(8,128)S(1)}, u32[]{:S(2)}) copy-start(f32[400,512]{1,0:T(8,128)S(1)} %collective-permute-done.4.left) | copy-start | bytes 2457604
  28.4 26.6 %collective-permute-start.5 = (f32[200,512]{1,0:T(8,128)S(1)}, f32[200,512]{1,0:T(8,128)S(1)}, u32[]{:S(2)}, u32[]{:S(2)}) collective-permute-start(f32[200,512]{1,0:T(8,128)S(1)} %slice.23), channel_id=1, source_target_pairs={{0,1},{1,2},{2,3},{3,0},{4,5},{5,6},{6,7},{7,4},{8,9},{9,10},{10,1... | collective-permute-start | bytes 1228808 | tf_op jit(solution)/shard_map/ppermute | solution.py:658
  28.7 42.0 %copy-start.3 = (f32[400,512]{1,0:T(8,128)}, f32[400,512]{1,0:T(8,128)S(1)}, u32[]{:S(2)}) copy-start(f32[400,512]{1,0:T(8,128)S(1)} %collective-permute-done.3.right) | copy-start | bytes 2457604
  28.7 26.2 %collective-permute-start.6 = (f32[200,512]{1,0:T(8,128)S(1)}, f32[200,512]{1,0:T(8,128)S(1)}, u32[]{:S(2)}, u32[]{:S(2)}) collective-permute-start(f32[200,512]{1,0:T(8,128)S(1)} %slice.24), channel_id=1, source_target_pairs={{0,3},{1,0},{2,1},{3,2},{4,7},{5,4},{6,5},{7,6},{8,11},{9,8},{10,9... | collective-permute-start | bytes 1228808 | tf_op jit(solution)/shard_map/ppermute | solution.py:659
  55.0 15.7 %copy-start.4 = (f32[200,512]{1,0:T(8,128)}, f32[200,512]{1,0:T(8,128)S(1)}, u32[]{:S(2)}) copy-start(f32[200,512]{1,0:T(8,128)S(1)} %collective-permute-done.6.across_b) | copy-start | bytes 1228804
  70.7 140.2 %all-to-all-start.3 = ((f32[32,75,8,128]{3,2,1,0:T(8,128)}), f32[32,75,8,128]{3,2,1,0:T(8,128)}, u32[]{:S(2)}, u32[]{:S(2)}) async-start(f32[32,75,8,128]{3,2,1,0:T(8,128)} %lookup.1), calls=%async_computation.3 | async-start | bytes 19660800 | tf_op jit(solution)/shard_map/all_to_all | solution.py:631
  79.1 14.3 %copy-start.5 = (s32[1024]{0:T(1024)S(1)}, s32[1024]{0:T(1024)}, u32[]{:S(2)}) copy-start(s32[1024]{0:T(1024)} %param.19) | copy-start | bytes 12292
  79.1 332.7 %reduce-scatter.5.cloned.1.call-start = ((), (), s32[]{:S(2)}) async-start(), calls=%async_computation.8 | async-start | bytes 16384000 | tf_op jit(solution)/shard_map/reduce_scatter | solution.py:683
  104.0 106.8 %copy-start = (f32[512,400]{0,1:T(8,128)S(1)}, f32[512,400]{0,1:T(8,128)}, u32[]{:S(2)}) copy-start(f32[512,400]{0,1:T(8,128)} %param.13) | copy-start | bytes 2457604
  106.6 7.3 %collective-permute-start.2 = (s32[1]{0:T(128)}, s32[1]{0:T(128)}, u32[]{:S(2)}, u32[]{:S(2)}) collective-permute-start(s32[1]{0:T(128)} %bitcast.6), channel_id=1, source_target_pairs={{0,3},{1,0},{2,1},{3,2},{4,7},{5,4},{6,5},{7,6},{8,11},{9,8},{10,9... | collective-permute-start | bytes 20 | tf_op jit(solution)/shard_map/ppermute | solution.py:637
  106.6 6.7 %collective-permute-start.1 = (s32[1]{0:T(128)}, s32[1]{0:T(128)}, u32[]{:S(2)}, u32[]{:S(2)}) collective-permute-start(s32[1]{0:T(128)} %bitcast.6), channel_id=1, source_target_pairs={{0,2},{1,3},{2,0},{3,1},{4,6},{5,7},{6,4},{7,5},{8,10},{9,11},{10,... | collective-permute-start | bytes 20 | tf_op jit(solution)/shard_map/ppermute | solution.py:637
  107.2 4.8 collective-permute-start
  259.4 223.3 %reduce-scatter.7.cloned.1.call-start = ((), (), s32[]{:S(2)}) async-start(), calls=%async_computation.10 | async-start | bytes 3379200
  411.9 153.4 %all-gather.3.cloned.1.call-start = ((), (), s32[]{:S(2)}) async-start(), calls=%async_computation.9 | async-start | bytes 13737984 | tf_op jit(solution)/shard_map/all_gather | solution.py:716
  486.2 44.0 %copy-start.1 = (f32[512,400]{0,1:T(8,128)S(1)}, f32[512,400]{0,1:T(8,128)}, u32[]{:S(2)}) copy-start(f32[512,400]{0,1:T(8,128)} %param.13) | copy-start | bytes 2457604
Sparse Core Ops, SparseCore 0:
  259.5 134.6 reduce-scatter.4
  412.0 70.6 reduce-scatter.6
  485.7 79.5 all-gather.2

commit v4 on v3

--- a/solution.py
+++ b/solution.py
@@ -5,6 +5,7 @@
 from jax.experimental import pallas as pl
 from jax.experimental.pallas import tpu as pltpu
 from jax.sharding import PartitionSpec as P
+
 
 learn_rate = 0.5
 adagrad_eps = 1e-10
@@ -23,7 +24,7 @@
 OVER_TILES = 3 * OVER + 1
 REL = 7424
 RELGROUPS = REL // 128
-SHARDS = 128
+SHARDS = 64
 VMEM_LIMIT = 60 * 1024 * 1024
 FLAG = 127
 COUNT = 126
@@ -313,22 +314,26 @@
     )(addr, flag, arrived, over, rel_rows)
 
 
-def relation_kernel(id_ref, grad_ref, out_ref, rows, packed, sems):
-    zero = jnp.zeros((16, 4, 8, 128), F32)
+def relation_kernel(id_ref, other_id_ref, grad_ref, other_ref, out_ref, mine, others, packed, sems):
+    zero = jnp.zeros((8, 4, 8, 128), F32)
 
     def clear(g, _):
-        rows[pl.ds(g * 16, 16)] = zero
-        return 0
-
-    lax.fori_loop(0, SHARDS // 2, clear, 0)
-    flat = rows.reshape(SHARDS * 256, 128)
-    grad_flat = grad_ref.reshape(128 * 32, 128)
+        mine[pl.ds(g * 8, 8)] = zero
+        others[pl.ds(g * 8, 8)] = zero
+        return 0
+
+    lax.fori_loop(0, SHARDS + 1, clear, 0)
+    height = (SHARDS + 1) * 256
+    sides = (
+        (id_ref, grad_ref.reshape(128 * 32, 128), mine.reshape(height, 128)),
+        (other_id_ref, other_ref.reshape(128 * 32, 128), others.reshape(height, 128)),
+    )
 
     def add(i, _):
         for j in range(8):
-            r = id_ref[i >> 4, (i & 15) * 8 + j]
-            at = pl.ds((r >> 3) * 32 + (r & 7), 4, stride=8)
-            flat[at, :] = flat[at, :] + grad_flat[pl.ds(i * 32 + j, 4, stride=8), :]
+            for ids, grad, flat in sides:
+                at = pl.ds(ids[i >> 4, (i & 15) * 8 + j], 4, stride=8)
+                flat[at, :] = flat[at, :] + grad[pl.ds(i * 32 + j, 4, stride=8), :]
         return 0
 
     lax.fori_loop(0, 128, add, 0)
@@ -346,10 +351,12 @@
         for n in range(4):
             first = g * 32 + n * 8
             for t in range(3):
-                packed[g & 1, n, t * 8 : t * 8 + 8] = rows[pl.ds(first, 8), t]
-            rest = rows[first, 3]
+                packed[g & 1, n, t * 8 : t * 8 + 8] = (
+                    mine[pl.ds(first, 8), t] + others[pl.ds(first, 8), t]
+                )
+            rest = mine[first, 3] + others[first, 3]
             for q in range(1, 8):
-                rest = rest + pltpu.roll(rows[first + q, 3], 16 * q, 1)
+                rest = rest + pltpu.roll(mine[first + q, 3] + others[first + q, 3], 16 * q, 1)
             packed[g & 1, n, 24] = rest
         copy(g).start()
         return 0
@@ -359,23 +366,26 @@
     copy(SHARDS // 4 - 1).wait()
 
 
-def relation_sum(ids, grad):
+def relation_sum(ids, other_ids, grad, other):
     return pl.pallas_call(
         relation_kernel,
         in_specs=[
             pl.BlockSpec(memory_space=pltpu.SMEM),
+            pl.BlockSpec(memory_space=pltpu.SMEM),
+            pl.BlockSpec(memory_space=pltpu.VMEM),
             pl.BlockSpec(memory_space=pltpu.VMEM),
         ],
         out_specs=pl.BlockSpec(memory_space=pl.ANY),
         out_shape=jax.ShapeDtypeStruct((SHARDS, 25, 8, 128), F32),
         scratch_shapes=[
-            pltpu.VMEM((SHARDS * 8, 4, 8, 128), F32),
+            pltpu.VMEM(((SHARDS + 1) * 8, 4, 8, 128), F32),
+            pltpu.VMEM(((SHARDS + 1) * 8, 4, 8, 128), F32),
             pltpu.VMEM((2, 4, 25, 8, 128), F32),
             pltpu.SemaphoreType.DMA((2,)),
         ],
         compiler_params=pltpu.CompilerParams(vmem_limit_bytes=VMEM_LIMIT),
         name="relation_sum",
-    )(ids, grad)
+    )(ids, other_ids, grad, other)
 
 
 def pack_kernel(addr_ref, flag_ref, grad_ref, out_ref, over_ref, rows, rest, sems):
@@ -546,20 +556,25 @@
     )(grads, table_t, state)
 
 
-def relation_update_kernel(shard_ref, grad_ref, table_ref, state_ref, out_ref, table, sem):
+def relation_update_kernel(shard_ref, parts_ref, table_ref, state_ref, out_ref, table, sem):
     shard = shard_ref[0]
     group = jnp.minimum(shard >> 1, RELGROUPS - 1)
     lanes = pl.ds(pl.multiple_of(group * 128, 128), 128)
     copy = pltpu.make_async_copy(table_ref.at[:, lanes], table, sem)
     copy.start()
     odd = (shard & 1) == 1
+
+    def total(i, carry):
+        return carry + parts_ref[i]
+
+    packed = lax.fori_loop(1, 16, total, parts_ref[0])
     blank = jnp.zeros((64, 128), F32)
     parts = []
     for t in range(4):
         if t < 3:
-            part = grad_ref[t * 8 : t * 8 + 8].reshape(64, 128)
+            part = packed[t * 8 : t * 8 + 8].reshape(64, 128)
         else:
-            rest = grad_ref[24]
+            rest = packed[24]
             part = jnp.concatenate(
                 [rest] + [pltpu.roll(rest, 128 - 16 * q, 1) for q in range(1, 8)], axis=0
             )
@@ -599,23 +614,31 @@
 
 def unpack_kernel(shards_ref, new_table, new_state):
     low = lax.broadcasted_iota(I32, (WIDTH // 2, 128), 1) < 64
-    for g in range(2):
+    for g in range(4):
         lanes = slice(g * 128, (g + 1) * 128)
-        even = shards_ref[2 * g, 0, 0:25].reshape(WIDTH // 2, 128)
-        odd = shards_ref[2 * g + 1, 0, 0:25].reshape(WIDTH // 2, 128)
+        even = shards_ref[2 * g, 0, 0, 0:25].reshape(WIDTH // 2, 128)
+        odd = shards_ref[2 * g + 1, 0, 0, 0:25].reshape(WIDTH // 2, 128)
         new_table[: WIDTH // 2, lanes] = jnp.where(low, even, pltpu.roll(odd, 64, 1))
         new_table[WIDTH // 2 :, lanes] = jnp.where(low, pltpu.roll(even, 64, 1), odd)
-        state = jnp.where(low[:8], shards_ref[2 * g, 0, 25], shards_ref[2 * g + 1, 0, 25])
-        new_state[pl.ds(pl.program_id(0) * 2 + g, 1), :] = state[0:1]
+        state = jnp.where(low[:8], shards_ref[2 * g, 0, 0, 25], shards_ref[2 * g + 1, 0, 0, 25])
+        group = pl.program_id(0) * 4 + g
+
+        @pl.when(group < RELGROUPS)
+        def _():
+            new_state[pl.ds(group, 1), :] = state[0:1]
 
 
 def unpack(shards):
     return pl.pallas_call(
         unpack_kernel,
-        grid=(RELGROUPS // 2,),
-        in_specs=[pl.BlockSpec((4, 1, 26, 8, 128), lambda i: (i & 7, i >> 3, 0, 0, 0))],
+        grid=(pl.cdiv(RELGROUPS, 4),),
+        in_specs=[
+            pl.BlockSpec(
+                (8, 1, 1, 26, 8, 128), lambda i: (i & 1, i >> 3, (i >> 1) & 3, 0, 0, 0)
+            )
+        ],
         out_specs=(
-            pl.BlockSpec((WIDTH, 256), lambda i: (0, i)),
+            pl.BlockSpec((WIDTH, 512), lambda i: (0, i)),
             pl.BlockSpec((RELGROUPS, 128), lambda i: (0, 0)),
         ),
         out_shape=(
@@ -627,8 +650,10 @@
     )(shards)
 
 
-def exchange(x, axis):
-    return lax.all_to_all(x, axis, split_axis=0, concat_axis=0, tiled=True)
+def exchange(x, axis, groups=None):
+    return lax.all_to_all(
+        x, axis, split_axis=0, concat_axis=0, tiled=True, axis_index_groups=groups
+    )
 
 
 def any_device(flag):
@@ -655,15 +680,16 @@
     to_left = [(p, (p + 3) % 4) for p in range(4)]
     left = lax.ppermute(table_t, "rep", to_right)
     right = lax.ppermute(table_t, "rep", to_left)
-    across_a = lax.ppermute(left[: WIDTH // 2], "rep", to_right)
-    across_b = lax.ppermute(right[WIDTH // 2 :], "rep", to_left)
-    tables = (table_t, right, across_a, across_b, left)
     rows_at, rep_at = lax.axis_index("rows"), lax.axis_index("rep")
     request, addr = prep(
         rep_at.reshape(1),
         end_owner.T, end_row.T, negative_owner.reshape(1, NEG), negative_row.reshape(8, 128)
     )
     wanted = exchange(request.reshape(GROUP, 2, 128), "rows")
+    left, right, _ = lax.optimization_barrier((left, right, wanted))
+    across_a = lax.ppermute(left[: WIDTH // 2], "rep", to_right)
+    across_b = lax.ppermute(right[WIDTH // 2 :], "rep", to_left)
+    tables = (table_t, right, across_a, across_b, left)
     wanted_rows = wanted.reshape(2 * GROUP, 128)
     looked = lookup(MAIN, 0, wanted_rows, tables)
     arrived = exchange(looked, "rows")
@@ -678,17 +704,27 @@
         lambda x: math(addr, flag, x, x, rel_rows),
         arrived,
     )
-    relation_grad = relation_sum(relation_id.reshape(8, 128), rel_grads)
-    grads, relation_grad = lax.optimization_barrier((grads, relation_grad))
-    part_grad = lax.psum_scatter(
-        relation_grad.reshape(4, GROUP, 25, 8, 128), "rep", scatter_dimension=0, tiled=True
-    )
+    core, twins = rows_at & 1, [[r for r in range(GROUP) if r % 2 == c] for c in (0, 1)]
+    swap = [(r, r ^ 1) for r in range(GROUP)]
+    other_id = lax.ppermute(relation_id, "rows", swap)
+    other_grads = lax.ppermute(rel_grads, "rows", swap)
+
+    def places(ids):
+        near = ids - core * (SHARDS * 64)
+        near = jnp.where((near >= 0) & (near < SHARDS * 64), near, SHARDS * 64)
+        return ((near >> 3) * 32 + (near & 7)).reshape(8, 128)
+
     outgoing, outgoing_over = pack_grads(addr, flag, grads)
     incoming = exchange(outgoing, "rows")
+    rel_grads, other_grads, _ = lax.optimization_barrier((rel_grads, other_grads, outgoing))
+    relation_grad = relation_sum(
+        places(relation_id), places(other_id), rel_grads, other_grads
+    )
+    part_grad = lax.psum_scatter(
+        relation_grad.reshape(4, 16, 25, 8, 128), "rep", scatter_dimension=0, tiled=True
+    )
     incoming, part_grad = lax.optimization_barrier((incoming, part_grad))
-    shard_grad = lax.psum_scatter(
-        part_grad.reshape(GROUP, 25, 8, 128), "rows", scatter_dimension=0, tiled=True
-    )
+    shard_grads = exchange(part_grad.reshape(16, 25, 8, 128), "rows", twins)
     slots = wanted.reshape(GROUP, 256)
 
     def ids(first, octets):
@@ -696,7 +732,7 @@
         return part.reshape(GROUP // SUM_STEP, 1, SUM_STEP * octets * 8)
 
     summed = row_sum(MAIN, ids(0, MAIN), incoming)
-    summed, shard_grad = lax.optimization_barrier((summed, shard_grad))
+    summed, shard_grads = lax.optimization_barrier((summed, shard_grads))
     summed = lax.cond(
         over_now,
         lambda x: x + row_sum(OVER, ids(MAIN, OVER), exchange(outgoing_over, "rows")),
@@ -708,13 +744,13 @@
         entity_grads, table_t, entity_state.reshape(1, ENT)
     )
     new_shard = relation_update(
-        (rep_at * GROUP + rows_at).reshape(1),
-        shard_grad.reshape(25, 8, 128),
+        (core * SHARDS + rep_at * 16 + (rows_at >> 1)).reshape(1),
+        shard_grads,
         relation_table.T,
         relation_state.reshape(RELGROUPS, 128),
     )
     shards = lax.all_gather(new_shard, AXES, axis=0, tiled=False)
-    new_relation_table, new_relation_state = unpack(shards.reshape(GROUP, 4, 26, 8, 128))
+    new_relation_table, new_relation_state = unpack(shards.reshape(16, 2, 4, 26, 8, 128))
     return (
         new_entity_table.T,
         new_entity_state.reshape(ENT),

time: 594 us -> 553 us (0.931)
  waiting for transfers between devices: 184 us -> 138 us
  Pallas kernels: 149 us -> 141 us
  starting transfers between devices: 16.3 us -> 24 us
    optimization_barrier x1 -> x0, waiting for transfers between devices: 34 us -> none  [per_device(): summed, shard_grad = lax.optimization_barrier((summed, shard_grad))]
    ppermute x1, waiting for transfers between devices: 17.7 us -> 0.01 us  [per_device(): left = lax.ppermute(table_t, 'rep', to_right)]
    ppermute x1, waiting for transfers between devices: 0.01 us -> 9.06 us  [per_device(): across_a = lax.ppermute(left[:WIDTH // 2], 'rep', to_right)]
    unnamed x14 -> x16, local copies, waits for them, and re-layouts: 14.2 us -> 16.2 us
    all_to_all x1 -> x2, waiting for transfers between devices: 96.2 us -> 96.1 us  [exchange(): lax.all_to_all(x, axis, split_axis=0, concat_axis=0, tiled=True, axis_ind...]
  transfers between devices with their start and end apart: 11 -> 13, of which waited for: 5 -> 6; matrix products, arithmetic and copies ran while one was open for 5% -> 5% of each run, Pallas kernels for 10% -> 11%
where the time goes in v4:
time: 553 us; the launch traced here: 551 us
  blocking collectives  198 us (36%)
  Pallas kernels  141 us (25%)
  waiting for transfers between devices  138 us (25%)
  local copies, waits for them, and re-layouts  29.4 us (5%)
  starting transfers between devices  24 us (4%)
  between operations  16.8 us (3%)
    all_to_all x3, blocking collectives, exchange(): lax.all_to_all(x, axis, split_axis=0, concat_axis=0, tiled=True, axis_ind...  198 us
    all_to_all x2, waiting for transfers between devices, exchange(): lax.all_to_all(x, axis, split_axis=0, concat_axis=0, tiled=True, axis_ind...  96.1 us
    pallas_call x1, Pallas kernels, row_sum(): pl.pallas_call(functools.partial(row_sum_kernel, octets), grid=(GROUP //...  36 us
    all_gather x1, waiting for transfers between devices, per_device(): shards = lax.all_gather(new_shard, AXES, axis=0, tiled=False)  27.8 us
    pallas_call x1, Pallas kernels, math(): pl.pallas_call(math_kernel, in_specs=[pl.BlockSpec(memory_space=pltpu.SME...  26.9 us
    pallas_call x1, Pallas kernels, lookup(): pl.pallas_call(functools.partial(lookup_kernel, octets, first), grid=(GRO...  17.7 us
    pallas_call x1, Pallas kernels, unpack(): pl.pallas_call(unpack_kernel, grid=(pl.cdiv(RELGROUPS, 4),), in_specs=[pl...  16.3 us
    unnamed x16, local copies, waits for them, and re-layouts  16.2 us
  transfers between devices with their start and end apart: 13, of which 6 were waited for; matrix products, arithmetic and copies ran while one was open for 5% of the time, Pallas kernels for 11%

profile of v4, /device:TPU:1, one launch (start us, length us, event | category | flops | bytes accessed | tf_op | source)
XLA Modules:
  0.0 551.1 jit_solution(11066548238963618468)
XLA Ops:
  7.2 2.1 collective-permute-start.3
  9.3 1.4 collective-permute-start.4
  10.6 6.0 %prep.1 = (s32[64,128]{1,0:T(8,128)}, s32[24,128]{1,0:T(8,128)S(1)}) custom-call(s32[1]{0:T(128)} %bitcast.me_ref, s32[2,1024]{1,0:T(2,128)} %bitcast.46, s32[2,1024]{1,0:T(2,128)} %bitcast.47, s32[1,1024]{1,0:T(1,128)} %bitcast.48, s32[8,128]{1,0:T(8,128)} %bitcast.49), custom_call_target="tpu_custom_call" | custom-call | tf_op jit(solution)/shard_map/prep/pallas_call | solution.py:91
  16.6 16.7 %all_to_all.34 = s32[32,2,128]{2,1,0:T(2,128)S(1)} all-to-all(s32[32,2,128]{2,1,0:T(2,128)} %bitcast.45), channel_id=1, replica_groups=mesh['rows'=32,'rep'=4] {'rows'}, dimensions={0} | all-to-all | bytes 65536 | tf_op jit(solution)/shard_map/all_to_all | solution.py:654
  33.4 0.0 collective-permute-done.3.left
  33.4 0.0 collective-permute-done.4.right
  33.4 0.0 copy-start.3
  33.4 0.1 collective-permute-start.5
  33.5 2.7 collective-permute-start.6
  36.3 9.1 %collective-permute-done.5.across_a = f32[200,512]{1,0:T(8,128)S(1)} collective-permute-done((f32[200,512]{1,0:T(8,128)S(1)}, f32[200,512]{1,0:T(8,128)S(1)}, u32[]{:S(2)}, u32[]{:S(2)}) %collective-permute-start.5) | collective-permute-done | bytes 409632 | tf_op jit(solution)/shard_map/ppermute | solution.py:690
  45.3 0.7 copy-done.5
  46.1 17.7 %lookup.1 = f32[32,75,8,128]{3,2,1,0:T(8,128)} custom-call(s32[64,128]{1,0:T(8,128)S(1)} %bitcast.39, f32[400,512]{1,0:T(8,128)} %bitcast.35, f32[400,512]{1,0:T(8,128)S(1)} %collective-permute-done.4.right, f32[200,512]{1,0:T(8,128)S(1)} %collective-permute-done.5.across_a, f32[200,512]{1,0:T(8,128)S(1)} %collective-permute-done.6.across_b, ...), custom_call_target="tpu_custom_call" | custom-call | tf_op jit(solution)/shard_map/lookup/pallas_call | solution.py:166
  63.8 5.9 %all-to-all-start.3 = ((f32[32,75,8,128]{3,2,1,0:T(8,128)}), f32[32,75,8,128]{3,2,1,0:T(8,128)}, u32[]{:S(2)}, u32[]{:S(2)}) async-start(f32[32,75,8,128]{3,2,1,0:T(8,128)} %lookup.1), calls=%async_computation.3 | async-start | bytes 19660800 | tf_op jit(solution)/shard_map/all_to_all | solution.py:654
  69.7 0.0 reduce-scatter.2.cloned.1.call-start
  69.8 0.0 copy-start.6
  69.8 14.1 %copy.14 = f32[7424,400]{1,0:T(8,128)} copy(f32[7424,400]{0,1:T(8,128)} %param.15) | data formatting | bytes 23756800 | tf_op args[2]
  83.9 0.6 add_bitcast_fusion.1
  84.5 10.6 %gather_fusion = f32[1024,400]{1,0:T(8,128)} fusion(f32[7424,400]{1,0:T(8,128)} %copy.14, s32[1024]{0:T(1024)S(1)} %get-tuple-element.96), kind=kCustom, calls=%fused_computation | custom fusion | bytes 3280896 | tf_op jit(solution)/shard_map/gather | solution.py:698
  95.1 1.8 pad.4
  97.0 0.8 slice_reduce_fusion
  97.8 0.2 collective-permute-start
  98.0 3.7 collective-permute-start.1
  101.7 0.4 collective-permute-done
  104.1 0.7 collective-permute-done.2
  105.4 96.1 %all-to-all-done.3 = f32[32,75,8,128]{3,2,1,0:T(8,128)} async-done(((f32[32,75,8,128]{3,2,1,0:T(8,128)}), f32[32,75,8,128]{3,2,1,0:T(8,128)}, u32[]{:S(2)}, u32[]{:S(2)}) %all-to-all-start.3) | async-done | bytes 9830432 | tf_op jit(solution)/shard_map/all_to_all | solution.py:654
  201.5 27.1 %conditional.2 = ((f32[384,4,8,128]{3,2,1,0:T(8,128)}, f32[128,4,8,128]{3,2,1,0:T(8,128)})) conditional(s32[]{:T(128)} %bitcast.7, (s32[24,128]{1,0:T(8,128)S(1)}, s32[1]{0:T(128)}, f32[32,75,8,128]{3,2,1,0:T(8,128)}, f32[1024,512]{1,0:T(8,128)S(1)}) %tuple.25, (s32[64,128]{1,0:T(8,128)S(1)}, f32[400,512]{1,0:T(8,128)S(1)}, f32[400,512]{1,0:T(8,128)}, ...), branch_computations={%region_1.2_spmd, %region_2.3_spmd} | conditional | bytes 3407880 | solution.py:699
  201.5 26.9 %math.2 = (f32[384,4,8,128]{3,2,1,0:T(8,128)}, f32[128,4,8,128]{3,2,1,0:T(8,128)}) custom-call(s32[24,128]{1,0:T(8,128)S(1)} %get-tuple-element.38.addr_ref, s32[1]{0:T(128)} %get-tuple-element.39.flag_ref, f32[32,75,8,128]{3,2,1,0:T(8,128)} %get-tuple-element.40.pay_ref.over_ref, f32[32,75,8,128]{3,2,1,0:T(8,128)} %get-tuple-element.40.pay_ref.over_ref, ...), custom_call_target="tpu_custom_call" | custom-call | tf_op jit(solution)/shard_map/cond/branch_0_fun/math/pallas_call | solution.py:285
  228.6 3.3 collective-permute-start.8
  231.9 0.1 collective-permute-start.7
  232.0 3.9 collective-permute-done.7
  235.9 0.6 add_bitcast_fusion.other_id_ref
  236.5 16.0 %pack_grads.1 = (f32[32,75,8,128]{3,2,1,0:T(8,128)}, f32[32,13,8,128]{3,2,1,0:T(8,128)}) custom-call(s32[24,128]{1,0:T(8,128)S(1)} %get-tuple-element.78.addr_ref, s32[1]{0:T(128)} %max.11.flag_ref, f32[384,4,8,128]{3,2,1,0:T(8,128)} %get-tuple-element.81.grad_ref), custom_call_target="tpu_custom_call" | custom-call | tf_op jit(solution)/shard_map/pack_grads/pallas_call | solution.py:449
  252.5 1.3 copy-done.4
  253.9 16.1 %relation_sum.1 = f32[64,25,8,128]{3,2,1,0:T(8,128)} custom-call(s32[8,128]{1,0:T(8,128)} %get-tuple-element.95.id_ref, s32[8,128]{1,0:T(8,128)} %add_bitcast_fusion.other_id_ref, f32[128,4,8,128]{3,2,1,0:T(8,128)} %get-tuple-element.84.grad_ref, f32[128,4,8,128]{3,2,1,0:T(8,128)} %copy-done.4), custom_call_target="tpu_custom_call" | custom-call | tf_op jit(solution)/shard_map/relation_sum/pallas_call | solution.py:370
  270.0 0.0 reduce-scatter.2.cloned.1.call-update
  270.0 133.2 %all_to_all.35.pay_ref = f32[32,75,8,128]{3,2,1,0:T(8,128)} all-to-all(f32[32,75,8,128]{3,2,1,0:T(8,128)} %get-tuple-element.82), channel_id=1, replica_groups=mesh['rows'=32,'rep'=4] {'rows'}, dimensions={0} | all-to-all | bytes 19660800 | tf_op jit(solution)/shard_map/all_to_all | solution.py:654
  403.2 4.4 all-to-all-start.5
  407.7 0.0 all-gather.3.cloned.1.call-start
  407.7 0.7 reshape.75.wanted_ref
  408.4 36.0 %row_sum.1 = f32[4,400,512]{2,1,0:T(8,128)S(1)} custom-call(s32[4,1,1536]{2,1,0:T(1,128)} %reshape.75.wanted_ref, f32[32,75,8,128]{3,2,1,0:T(8,128)} %all_to_all.35.pay_ref), custom_call_target="tpu_custom_call" | custom-call | tf_op jit(solution)/shard_map/row_sum/pallas_call | solution.py:521
  444.5 3.2 relation_update.1
  447.6 0.0 all-gather.3.cloned.1.call-update
  447.7 0.8 fusion
  448.5 0.0 copy-start.1
  448.6 48.4 %all_to_all.36.grad_ref = f32[4,400,512]{2,1,0:T(8,128)} all-to-all(f32[4,400,512]{2,1,0:T(8,128)S(1)} %fusion), channel_id=1, replica_groups=mesh['rows'=32,'rep'=4] {'rep'}, dimensions={0} | all-to-all | bytes 6553600 | tf_op jit(solution)/shard_map/all_to_all | solution.py:654
  497.0 3.2 entity_update.1
  500.2 27.8 %all-gather.3.cloned.1.call-done = f32[3328,8,128]{2,1,0:T(8,128)} async-done(((f32[26,8,128]{2,1,0:T(8,128)}), f32[3328,8,128]{2,1,0:T(8,128)}) %all-gather.3.cloned.1.call-update) | async-done | bytes 13631504 | tf_op jit(solution)/shard_map/all_gather | solution.py:752
  528.0 16.3 %unpack.1 = (f32[400,7424]{1,0:T(8,128)}, f32[58,128]{1,0:T(8,128)}) custom-call(f32[16,2,4,26,8,128]{5,4,3,2,1,0:T(8,128)} %bitcast.32), custom_call_target="tpu_custom_call" | custom-call | tf_op jit(solution)/shard_map/unpack/pallas_call | solution.py:632
  (19 shorter events, 0.1 us)
Async XLA Ops:
  7.2 26.2 %collective-permute-start.3 = (f32[400,512]{1,0:T(8,128)}, f32[400,512]{1,0:T(8,128)S(1)}, u32[]{:S(2)}, u32[]{:S(2)}) collective-permute-start(f32[400,512]{1,0:T(8,128)} %bitcast.33), channel_id=1, source_target_pairs={{0,1},{1,2},{2,3},{3,0},{4,5},{5,6},{6,7},{7,4},{8,9},{9,10},{10,1... | collective-permute-start | bytes 2457608 | tf_op jit(solution)/shard_map/ppermute | solution.py:681
  9.3 24.1 %collective-permute-start.4 = (f32[400,512]{1,0:T(8,128)}, f32[400,512]{1,0:T(8,128)S(1)}, u32[]{:S(2)}, u32[]{:S(2)}) collective-permute-start(f32[400,512]{1,0:T(8,128)} %bitcast.34), channel_id=1, source_target_pairs={{0,3},{1,0},{2,1},{3,2},{4,7},{5,4},{6,5},{7,6},{8,11},{9,8},{10,9... | collective-permute-start | bytes 2457608 | tf_op jit(solution)/shard_map/ppermute | solution.py:682
  33.4 30.4 %copy-start.2 = (f32[400,512]{1,0:T(8,128)}, f32[400,512]{1,0:T(8,128)S(1)}, u32[]{:S(2)}) copy-start(f32[400,512]{1,0:T(8,128)S(1)} %collective-permute-done.3.left) | copy-start | bytes 2457604
  33.4 30.4 %copy-start.3 = (f32[400,512]{1,0:T(8,128)}, f32[400,512]{1,0:T(8,128)S(1)}, u32[]{:S(2)}) copy-start(f32[400,512]{1,0:T(8,128)S(1)} %collective-permute-done.4.right) | copy-start | bytes 2457604
  33.4 11.9 %collective-permute-start.5 = (f32[200,512]{1,0:T(8,128)S(1)}, f32[200,512]{1,0:T(8,128)S(1)}, u32[]{:S(2)}, u32[]{:S(2)}) collective-permute-start(f32[200,512]{1,0:T(8,128)S(1)} %slice.17), channel_id=1, source_target_pairs={{0,1},{1,2},{2,3},{3,0},{4,5},{5,6},{6,7},{7,4},{8,9},{9,10},{10,1... | collective-permute-start | bytes 1228808 | tf_op jit(solution)/shard_map/ppermute | solution.py:690
  33.5 11.8 %collective-permute-start.6 = (f32[200,512]{1,0:T(8,128)S(1)}, f32[200,512]{1,0:T(8,128)S(1)}, u32[]{:S(2)}, u32[]{:S(2)}) collective-permute-start(f32[200,512]{1,0:T(8,128)S(1)} %slice.18), channel_id=1, source_target_pairs={{0,3},{1,0},{2,1},{3,2},{4,7},{5,4},{6,5},{7,6},{8,11},{9,8},{10,9... | collective-permute-start | bytes 1228808 | tf_op jit(solution)/shard_map/ppermute | solution.py:691
  45.3 0.8 copy-start.5
  63.8 137.7 %all-to-all-start.3 = ((f32[32,75,8,128]{3,2,1,0:T(8,128)}), f32[32,75,8,128]{3,2,1,0:T(8,128)}, u32[]{:S(2)}, u32[]{:S(2)}) async-start(f32[32,75,8,128]{3,2,1,0:T(8,128)} %lookup.1), calls=%async_computation.3 | async-start | bytes 19660800 | tf_op jit(solution)/shard_map/all_to_all | solution.py:654
  69.7 333.5 %reduce-scatter.2.cloned.1.call-start = ((), (), s32[]{:S(2)}) async-start(), calls=%async_computation.8 | async-start | bytes 8192000 | tf_op jit(solution)/shard_map/reduce_scatter | solution.py:723
  69.8 14.1 %copy-start.6 = (s32[1024]{0:T(1024)S(1)}, s32[1024]{0:T(1024)}, u32[]{:S(2)}) copy-start(s32[1024]{0:T(1024)} %param.19) | copy-start | bytes 12292
  95.1 106.4 %copy-start = (f32[512,400]{0,1:T(8,128)S(1)}, f32[512,400]{0,1:T(8,128)}, u32[]{:S(2)}) copy-start(f32[512,400]{0,1:T(8,128)} %param.13) | copy-start | bytes 2457604
  97.8 4.3 collective-permute-start
  98.0 5.4 collective-permute-start.1
  101.7 3.0 collective-permute-start.2
  228.6 23.9 %collective-permute-start.8 = (f32[128,4,8,128]{3,2,1,0:T(8,128)}, f32[128,4,8,128]{3,2,1,0:T(8,128)S(1)}, u32[]{:S(2)}, u32[]{:S(2)}) collective-permute-start(f32[128,4,8,128]{3,2,1,0:T(8,128)} %get-tuple-element.84.grad_ref), channel_id=1, source_target_pairs={{0,4},{4,0},{8,12},{12,8},{16,20},{20,16},{24,28},{28,24},{32,36},... | collective-permute-start | bytes 6291464 | tf_op jit(solution)/shard_map/ppermute | solution.py:710
  231.9 4.0 collective-permute-start.7
  252.5 1.4 copy-start.4
  403.2 41.2 %all-to-all-start.5 = ((f32[16,25,8,128]{3,2,1,0:T(8,128)}), f32[16,25,8,128]{3,2,1,0:T(8,128)}, u32[]{:S(2)}, u32[]{:S(2)}) async-start(f32[16,25,8,128]{3,2,1,0:T(8,128)} %bitcast.38), calls=%async_computation.6 | async-start | bytes 3276800 | tf_op jit(solution)/shard_map/all_to_all | solution.py:654
  407.7 120.3 %all-gather.3.cloned.1.call-start = ((), (), s32[]{:S(2)}) async-start(), calls=%async_computation.9 | async-start | bytes 13737984 | tf_op jit(solution)/shard_map/all_gather | solution.py:752
  448.5 48.4 %copy-start.1 = (f32[512,400]{0,1:T(8,128)S(1)}, f32[512,400]{0,1:T(8,128)}, u32[]{:S(2)}) copy-start(f32[512,400]{0,1:T(8,128)} %param.13) | copy-start | bytes 2457604
Sparse Core Ops, SparseCore 0:
  270.1 81.2 reduce-scatter.1
  447.8 80.1 all-gather.2

commit v5 on v4

--- a/solution.py
+++ b/solution.py
@@ -17,7 +17,7 @@
 EDGE = 1024
 NEG = 1024
 GROUP = 32
-MAIN = 24
+MAIN = 23
 OCT = 28
 OVER = OCT - MAIN
 MAIN_TILES = 3 * MAIN + 3
@@ -556,7 +556,9 @@
     )(grads, table_t, state)
 
 
-def relation_update_kernel(shard_ref, parts_ref, table_ref, state_ref, out_ref, table, sem):
+def relation_update_kernel(
+    shard_ref, part_0, part_1, part_2, part_3, table_ref, state_ref, out_ref, table, sem
+):
     shard = shard_ref[0]
     group = jnp.minimum(shard >> 1, RELGROUPS - 1)
     lanes = pl.ds(pl.multiple_of(group * 128, 128), 128)
@@ -564,11 +566,7 @@
     copy.start()
     odd = (shard & 1) == 1
 
-    def total(i, carry):
-        return carry + parts_ref[i]
-
-    packed = lax.fori_loop(1, 16, total, parts_ref[0])
-    blank = jnp.zeros((64, 128), F32)
+    packed = (part_0[...] + part_1[...]) + (part_2[...] + part_3[...])
     parts = []
     for t in range(4):
         if t < 3:
@@ -595,12 +593,12 @@
     out_ref[25] = jnp.broadcast_to(state, (8, 128))
 
 
-def relation_update(shard, grad, table_t, state):
+def relation_update(shard, parts, table_t, state):
     return pl.pallas_call(
         relation_update_kernel,
         in_specs=[
             pl.BlockSpec(memory_space=pltpu.SMEM),
-            pl.BlockSpec(memory_space=pltpu.VMEM),
+            *[pl.BlockSpec(memory_space=pltpu.VMEM)] * 4,
             pl.BlockSpec(memory_space=pl.ANY),
             pl.BlockSpec(memory_space=pltpu.VMEM),
         ],
@@ -609,7 +607,7 @@
         scratch_shapes=[pltpu.VMEM((WIDTH, 128), F32), pltpu.SemaphoreType.DMA],
         compiler_params=pltpu.CompilerParams(vmem_limit_bytes=VMEM_LIMIT),
         name="relation_update",
-    )(shard, grad, table_t, state)
+    )(shard, *parts, table_t, state)
 
 
 def unpack_kernel(shards_ref, new_table, new_state):
@@ -650,10 +648,8 @@
     )(shards)
 
 
-def exchange(x, axis, groups=None):
-    return lax.all_to_all(
-        x, axis, split_axis=0, concat_axis=0, tiled=True, axis_index_groups=groups
-    )
+def exchange(x, axis):
+    return lax.all_to_all(x, axis, split_axis=0, concat_axis=0, tiled=True)
 
 
 def any_device(flag):
@@ -695,7 +691,20 @@
     arrived = exchange(looked, "rows")
     flag = any_device(jnp.max(wanted[:, 1, FLAG]).reshape(1))
     over_now = flag[0] > 0
+    core = rows_at & 1
+    swap = [(r, r ^ 1) for r in range(GROUP)]
+    other_id = lax.ppermute(relation_id, "rows", swap)
+
+    def places(ids):
+        near = ids - core * (SHARDS * 64)
+        near = jnp.where((near >= 0) & (near < SHARDS * 64), near, SHARDS * 64)
+        return ((near >> 3) * 32 + (near & 7)).reshape(8, 128)
+
     rel_rows = jnp.pad(relation_table[relation_id], ((0, 0), (0, 112)))
+    my_places, other_places = places(relation_id), places(other_id)
+    rel_rows, my_places, other_places = lax.optimization_barrier(
+        (rel_rows, my_places, other_places)
+    )
     grads, rel_grads = lax.cond(
         over_now,
         lambda x: math(
@@ -704,27 +713,37 @@
         lambda x: math(addr, flag, x, x, rel_rows),
         arrived,
     )
-    core, twins = rows_at & 1, [[r for r in range(GROUP) if r % 2 == c] for c in (0, 1)]
-    swap = [(r, r ^ 1) for r in range(GROUP)]
-    other_id = lax.ppermute(relation_id, "rows", swap)
     other_grads = lax.ppermute(rel_grads, "rows", swap)
-
-    def places(ids):
-        near = ids - core * (SHARDS * 64)
-        near = jnp.where((near >= 0) & (near < SHARDS * 64), near, SHARDS * 64)
-        return ((near >> 3) * 32 + (near & 7)).reshape(8, 128)
-
     outgoing, outgoing_over = pack_grads(addr, flag, grads)
     incoming = exchange(outgoing, "rows")
     rel_grads, other_grads, _ = lax.optimization_barrier((rel_grads, other_grads, outgoing))
-    relation_grad = relation_sum(
-        places(relation_id), places(other_id), rel_grads, other_grads
-    )
+    relation_grad = relation_sum(my_places, other_places, rel_grads, other_grads)
     part_grad = lax.psum_scatter(
         relation_grad.reshape(4, 16, 25, 8, 128), "rep", scatter_dimension=0, tiled=True
     )
-    incoming, part_grad = lax.optimization_barrier((incoming, part_grad))
-    shard_grads = exchange(part_grad.reshape(16, 25, 8, 128), "rows", twins)
+    part = part_grad.reshape(4, 4, 25, 8, 128)
+    y_at, z_at = rows_at >> 3, (rows_at >> 1) & 3
+    pieces = [
+        lax.dynamic_index_in_dim(part, (y_at + k) & 3, 0, keepdims=False) for k in range(4)
+    ]
+    part = pieces[0]
+    for k in range(1, 4):
+        ring = [(r, (r + 8 * k) % GROUP) for r in range(GROUP)]
+        part = part + lax.ppermute(pieces[k], "rows", ring)
+    pieces = [
+        lax.dynamic_index_in_dim(part, (z_at + k) & 3, 0, keepdims=False) for k in range(4)
+    ]
+    parts = [pieces[0]]
+    for k in range(1, 4):
+        ring = [(r, r // 8 * 8 + (r + 2 * k) % 8) for r in range(GROUP)]
+        parts.append(lax.ppermute(pieces[k], "rows", ring))
+    new_shard = relation_update(
+        (core * SHARDS + rep_at * 16 + (rows_at >> 1)).reshape(1),
+        parts,
+        relation_table.T,
+        relation_state.reshape(RELGROUPS, 128),
+    )
+    shards = lax.all_gather(new_shard, AXES, axis=0, tiled=False)
     slots = wanted.reshape(GROUP, 256)
 
     def ids(first, octets):
@@ -732,7 +751,6 @@
         return part.reshape(GROUP // SUM_STEP, 1, SUM_STEP * octets * 8)
 
     summed = row_sum(MAIN, ids(0, MAIN), incoming)
-    summed, shard_grads = lax.optimization_barrier((summed, shard_grads))
     summed = lax.cond(
         over_now,
         lambda x: x + row_sum(OVER, ids(MAIN, OVER), exchange(outgoing_over, "rows")),
@@ -743,13 +761,6 @@
     new_entity_table, new_entity_state = entity_update(
         entity_grads, table_t, entity_state.reshape(1, ENT)
     )
-    new_shard = relation_update(
-        (core * SHARDS + rep_at * 16 + (rows_at >> 1)).reshape(1),
-        shard_grads,
-        relation_table.T,
-        relation_state.reshape(RELGROUPS, 128),
-    )
-    shards = lax.all_gather(new_shard, AXES, axis=0, tiled=False)
     new_relation_table, new_relation_state = unpack(shards.reshape(16, 2, 4, 26, 8, 128))
     return (
         new_entity_table.T,

time: 553 us -> 653 us (1.18)
  the two profiles are of different devices: /device:TPU:1 before, /device:TPU:48 now
where the time goes in v5:
time: 653 us; the launch traced here: 652 us
  waiting for transfers between devices  369 us (57%)
  Pallas kernels  137 us (21%)
  blocking collectives  54.9 us (8%)
  starting transfers between devices  38.6 us (6%)
  local copies, waits for them, and re-layouts  32.2 us (5%)
  between operations  16.6 us (3%)
    all_to_all x2, waiting for transfers between devices, exchange(): return lax.all_to_all(x, axis, split_axis=0, concat_axis=0, tiled=True)  268 us
    reduce_scatter x1, waiting for transfers between devices, per_device(): lax.psum_scatter(relation_grad.reshape(4, 16, 25, 8, 128), 'rep', scatter...  66.4 us
    all_to_all x2, blocking collectives, exchange(): return lax.all_to_all(x, axis, split_axis=0, concat_axis=0, tiled=True)  54.9 us
    pallas_call x1, Pallas kernels, row_sum(): pl.pallas_call(functools.partial(row_sum_kernel, octets), grid=(GROUP //...  35.8 us
    pallas_call x1, Pallas kernels, math(): pl.pallas_call(math_kernel, in_specs=[pl.BlockSpec(memory_space=pltpu.SME...  26.8 us
    all_to_all x2, starting transfers between devices, exchange(): return lax.all_to_all(x, axis, split_axis=0, concat_axis=0, tiled=True)  18.9 us
    ppermute x3, waiting for transfers between devices, per_device(): part = part + lax.ppermute(pieces[k], 'rows', ring)  18.4 us
    unnamed x22, local copies, waits for them, and re-layouts  16.9 us
  transfers between devices with their start and end apart: 19, of which 12 were waited for; matrix products, arithmetic and copies ran while one was open for 5% of the time, Pallas kernels for 9%

profile of v5, /device:TPU:48, one launch (start us, length us, event | category | flops | bytes accessed | tf_op | source)
XLA Modules:
  0.0 652.0 jit_solution(11517028291653097623)
XLA Ops:
  7.2 1.6 collective-permute-start.3
  8.7 1.7 collective-permute-start.4
  10.5 6.0 prep.1
  16.5 12.5 %all_to_all.29 = s32[32,2,128]{2,1,0:T(2,128)S(1)} all-to-all(s32[32,2,128]{2,1,0:T(2,128)} %bitcast.66), channel_id=1, replica_groups=mesh['rows'=32,'rep'=4] {'rows'}, dimensions={0} | all-to-all | bytes 65536 | tf_op jit(solution)/shard_map/all_to_all | solution.py:652
  29.0 1.2 collective-permute-start.5
  30.3 2.2 collective-permute-start.6
  32.4 9.4 %collective-permute-done.5.across_a = f32[200,512]{1,0:T(8,128)S(1)} collective-permute-done((f32[200,512]{1,0:T(8,128)S(1)}, f32[200,512]{1,0:T(8,128)S(1)}, u32[]{:S(2)}, u32[]{:S(2)}) %collective-permute-start.5) | collective-permute-done | bytes 409632 | tf_op jit(solution)/shard_map/ppermute | solution.py:686
  41.8 0.8 copy-done.5
  42.5 14.3 %lookup.1 = f32[32,72,8,128]{3,2,1,0:T(8,128)} custom-call(s32[64,128]{1,0:T(8,128)S(1)} %bitcast.60, f32[400,512]{1,0:T(8,128)} %bitcast.55, f32[400,512]{1,0:T(8,128)S(1)} %collective-permute-done.4.right, f32[200,512]{1,0:T(8,128)S(1)} %collective-permute-done.5.across_a, f32[200,512]{1,0:T(8,128)S(1)} %collective-permute-done.6.across_b, ...), custom_call_target="tpu_custom_call" | custom-call | tf_op jit(solution)/shard_map/lookup/pallas_call | solution.py:166
  56.8 11.1 %all-to-all-start.3 = ((f32[32,72,8,128]{3,2,1,0:T(8,128)}), f32[32,72,8,128]{3,2,1,0:T(8,128)}, u32[]{:S(2)}, u32[]{:S(2)}) async-start(f32[32,72,8,128]{3,2,1,0:T(8,128)} %lookup.1), calls=%async_computation.3 | async-start | bytes 18874368 | tf_op jit(solution)/shard_map/all_to_all | solution.py:652
  68.2 0.6 add_bitcast_fusion.1
  68.8 14.1 %copy.14 = f32[7424,400]{1,0:T(8,128)} copy(f32[7424,400]{0,1:T(8,128)} %param.15) | data formatting | bytes 23756800 | tf_op args[2]
  82.9 10.7 %gather_fusion = f32[1024,400]{1,0:T(8,128)} fusion(f32[7424,400]{1,0:T(8,128)} %copy.14, s32[1024]{0:T(1024)S(1)} %get-tuple-element.101), kind=kCustom, calls=%fused_computation | custom fusion | bytes 3280896 | tf_op jit(solution)/shard_map/gather | solution.py:703
  93.6 1.8 pad.4
  95.5 0.6 add_bitcast_fusion.other_id_ref
  96.0 0.7 slice_reduce_fusion
  96.8 0.5 collective-permute-start
  97.3 4.0 collective-permute-start.1
  101.3 0.4 collective-permute-done
  103.8 1.4 collective-permute-done.2
  105.8 107.2 %all-to-all-done.3 = f32[32,72,8,128]{3,2,1,0:T(8,128)} async-done(((f32[32,72,8,128]{3,2,1,0:T(8,128)}), f32[32,72,8,128]{3,2,1,0:T(8,128)}, u32[]{:S(2)}, u32[]{:S(2)}) %all-to-all-start.3) | async-done | bytes 9437216 | tf_op jit(solution)/shard_map/all_to_all | solution.py:652
  212.9 27.0 %conditional.2 = ((f32[384,4,8,128]{3,2,1,0:T(8,128)}, f32[128,4,8,128]{3,2,1,0:T(8,128)})) conditional(s32[]{:T(128)} %bitcast.7, (s32[24,128]{1,0:T(8,128)S(1)}, s32[1]{0:T(128)}, f32[32,72,8,128]{3,2,1,0:T(8,128)}, f32[1024,512]{1,0:T(8,128)S(1)}) %tuple.25, (s32[64,128]{1,0:T(8,128)S(1)}, f32[400,512]{1,0:T(8,128)S(1)}, f32[400,512]{1,0:T(8,128)}, ...), branch_computations={%region_1.2_spmd, %region_2.3_spmd} | conditional | bytes 4194312 | solution.py:708
  212.9 26.8 %math.2 = (f32[384,4,8,128]{3,2,1,0:T(8,128)}, f32[128,4,8,128]{3,2,1,0:T(8,128)}) custom-call(s32[24,128]{1,0:T(8,128)S(1)} %get-tuple-element.38.addr_ref, s32[1]{0:T(128)} %get-tuple-element.39.flag_ref, f32[32,72,8,128]{3,2,1,0:T(8,128)} %get-tuple-element.40.pay_ref.over_ref, f32[32,72,8,128]{3,2,1,0:T(8,128)} %get-tuple-element.40.pay_ref.over_ref, ...), custom_call_target="tpu_custom_call" | custom-call | tf_op jit(solution)/shard_map/cond/branch_0_fun/math/pallas_call | solution.py:285
  240.1 15.9 %pack_grads.1 = (f32[32,72,8,128]{3,2,1,0:T(8,128)}, f32[32,16,8,128]{3,2,1,0:T(8,128)}) custom-call(s32[24,128]{1,0:T(8,128)S(1)} %get-tuple-element.77.addr_ref, s32[1]{0:T(128)} %max.11.flag_ref, f32[384,4,8,128]{3,2,1,0:T(8,128)} %get-tuple-element.81.grad_ref), custom_call_target="tpu_custom_call" | custom-call | tf_op jit(solution)/shard_map/pack_grads/pallas_call | solution.py:449
  256.0 1.4 copy-done.4
  257.3 15.5 %relation_sum.1 = f32[64,25,8,128]{3,2,1,0:T(8,128)} custom-call(s32[8,128]{1,0:T(8,128)} %get-tuple-element.86.id_ref, s32[8,128]{1,0:T(8,128)} %add_bitcast_fusion.other_id_ref, f32[128,4,8,128]{3,2,1,0:T(8,128)} %get-tuple-element.89.grad_ref, f32[128,4,8,128]{3,2,1,0:T(8,128)} %copy-done.4), custom_call_target="tpu_custom_call" | custom-call | tf_op jit(solution)/shard_map/relation_sum/pallas_call | solution.py:370
  272.9 66.4 %reduce-scatter.2.cloned.1.call-done = f32[1,16,25,8,128]{4,3,2,1,0:T(8,128)} async-done(((f32[4,16,25,8,128]{4,3,2,1,0:T(8,128)}), f32[1,16,25,8,128]{4,3,2,1,0:T(8,128)}) %reduce-scatter.2.cloned.1.call-update) | async-done | bytes 1638416 | tf_op jit(solution)/shard_map/reduce_scatter | solution.py:721
  339.3 1.3 dynamic-slice_bitcast_fusion.2
  340.7 0.6 collective-permute-start.11
  341.3 2.7 collective-permute-start.10
  344.0 9.1 %collective-permute-done.11 = f32[4,25,8,128]{3,2,1,0:T(8,128)S(1)} collective-permute-done((f32[4,25,8,128]{3,2,1,0:T(8,128)S(1)}, f32[4,25,8,128]{3,2,1,0:T(8,128)S(1)}, u32[]{:S(2)}, u32[]{:S(2)}) %collective-permute-start.11) | collective-permute-done | bytes 409632 | tf_op jit(solution)/shard_map/ppermute | solution.py:732
  353.1 2.1 collective-permute-done.10
  355.2 7.3 %collective-permute-done.9 = f32[4,25,8,128]{3,2,1,0:T(8,128)S(1)} collective-permute-done((f32[4,25,8,128]{3,2,1,0:T(8,128)S(1)}, f32[4,25,8,128]{3,2,1,0:T(8,128)S(1)}, u32[]{:S(2)}, u32[]{:S(2)}) %collective-permute-start.9) | collective-permute-done | bytes 409632 | tf_op jit(solution)/shard_map/ppermute | solution.py:732
  362.4 1.1 fusion.2
  363.5 0.7 dynamic-slice_bitcast_fusion.3
  364.2 1.5 collective-permute-start.12
  365.7 1.0 collective-permute-start.13
  366.7 2.3 collective-permute-start.14
  369.1 3.8 collective-permute-done.13.part_2
  373.8 2.8 relation_update.1
  376.6 7.8 %all-to-all-start.4 = ((f32[32,72,8,128]{3,2,1,0:T(8,128)}), f32[32,72,8,128]{3,2,1,0:T(8,128)}, u32[]{:S(2)}, u32[]{:S(2)}) async-start(f32[32,72,8,128]{3,2,1,0:T(8,128)} %get-tuple-element.82), calls=%async_computation.4 | async-start | bytes 18874368 | tf_op jit(solution)/shard_map/all_to_all | solution.py:652
  384.4 0.7 reshape.75.wanted_ref
  385.2 161.3 %all-to-all-done.4.pay_ref = f32[32,72,8,128]{3,2,1,0:T(8,128)} async-done(((f32[32,72,8,128]{3,2,1,0:T(8,128)}), f32[32,72,8,128]{3,2,1,0:T(8,128)}, u32[]{:S(2)}, u32[]{:S(2)}) %all-to-all-start.4) | async-done | bytes 9437216 | tf_op jit(solution)/shard_map/all_to_all | solution.py:652
  546.4 35.8 %row_sum.1 = f32[4,400,512]{2,1,0:T(8,128)S(1)} custom-call(s32[4,1,1472]{2,1,0:T(1,128)} %reshape.75.wanted_ref, f32[32,72,8,128]{3,2,1,0:T(8,128)} %all-to-all-done.4.pay_ref), custom_call_target="tpu_custom_call" | custom-call | tf_op jit(solution)/shard_map/row_sum/pallas_call | solution.py:521
  582.3 0.8 fusion
  583.1 42.4 %all_to_all.30.grad_ref = f32[4,400,512]{2,1,0:T(8,128)} all-to-all(f32[4,400,512]{2,1,0:T(8,128)S(1)} %fusion), channel_id=1, replica_groups=mesh['rows'=32,'rep'=4] {'rep'}, dimensions={0} | all-to-all | bytes 6553600 | tf_op jit(solution)/shard_map/all_to_all | solution.py:652
  625.6 3.2 entity_update.1
  628.8 16.3 %unpack.1 = (f32[400,7424]{1,0:T(8,128)}, f32[58,128]{1,0:T(8,128)}) custom-call(f32[16,2,4,26,8,128]{5,4,3,2,1,0:T(8,128)} %bitcast.52), custom_call_target="tpu_custom_call" | custom-call | tf_op jit(solution)/shard_map/unpack/pallas_call | solution.py:630
  (39 shorter events, 1.7 us)
Async XLA Ops:
  7.2 21.8 %collective-permute-start.3 = (f32[400,512]{1,0:T(8,128)}, f32[400,512]{1,0:T(8,128)S(1)}, u32[]{:S(2)}, u32[]{:S(2)}) collective-permute-start(f32[400,512]{1,0:T(8,128)} %bitcast.53), channel_id=1, source_target_pairs={{0,1},{1,2},{2,3},{3,0},{4,5},{5,6},{6,7},{7,4},{8,9},{9,10},{10,1... | collective-permute-start | bytes 2457608 | tf_op jit(solution)/shard_map/ppermute | solution.py:677
  8.7 20.2 %collective-permute-start.4 = (f32[400,512]{1,0:T(8,128)}, f32[400,512]{1,0:T(8,128)S(1)}, u32[]{:S(2)}, u32[]{:S(2)}) collective-permute-start(f32[400,512]{1,0:T(8,128)} %bitcast.54), channel_id=1, source_target_pairs={{0,3},{1,0},{2,1},{3,2},{4,7},{5,4},{6,5},{7,6},{8,11},{9,8},{10,9... | collective-permute-start | bytes 2457608 | tf_op jit(solution)/shard_map/ppermute | solution.py:678
  29.0 27.8 %copy-start.2 = (f32[400,512]{1,0:T(8,128)}, f32[400,512]{1,0:T(8,128)S(1)}, u32[]{:S(2)}) copy-start(f32[400,512]{1,0:T(8,128)S(1)} %collective-permute-done.3.left) | copy-start | bytes 2457604
  29.0 27.8 %copy-start.3 = (f32[400,512]{1,0:T(8,128)}, f32[400,512]{1,0:T(8,128)S(1)}, u32[]{:S(2)}) copy-start(f32[400,512]{1,0:T(8,128)S(1)} %collective-permute-done.4.right) | copy-start | bytes 2457604
  29.0 12.8 %collective-permute-start.5 = (f32[200,512]{1,0:T(8,128)S(1)}, f32[200,512]{1,0:T(8,128)S(1)}, u32[]{:S(2)}, u32[]{:S(2)}) collective-permute-start(f32[200,512]{1,0:T(8,128)S(1)} %slice.17), channel_id=1, source_target_pairs={{0,1},{1,2},{2,3},{3,0},{4,5},{5,6},{6,7},{7,4},{8,9},{9,10},{10,1... | collective-permute-start | bytes 1228808 | tf_op jit(solution)/shard_map/ppermute | solution.py:686
  30.3 11.5 %collective-permute-start.6 = (f32[200,512]{1,0:T(8,128)S(1)}, f32[200,512]{1,0:T(8,128)S(1)}, u32[]{:S(2)}, u32[]{:S(2)}) collective-permute-start(f32[200,512]{1,0:T(8,128)S(1)} %slice.18), channel_id=1, source_target_pairs={{0,3},{1,0},{2,1},{3,2},{4,7},{5,4},{6,5},{7,6},{8,11},{9,8},{10,9... | collective-permute-start | bytes 1228808 | tf_op jit(solution)/shard_map/ppermute | solution.py:687
  41.8 0.8 copy-start.5
  56.8 11.2 %copy-start.9 = (s32[1024]{0:T(1024)S(1)}, s32[1024]{0:T(1024)}, u32[]{:S(2)}) copy-start(s32[1024]{0:T(1024)} %param.19) | copy-start | bytes 12292
  56.8 156.1 %all-to-all-start.3 = ((f32[32,72,8,128]{3,2,1,0:T(8,128)}), f32[32,72,8,128]{3,2,1,0:T(8,128)}, u32[]{:S(2)}, u32[]{:S(2)}) async-start(f32[32,72,8,128]{3,2,1,0:T(8,128)} %lookup.1), calls=%async_computation.3 | async-start | bytes 18874368 | tf_op jit(solution)/shard_map/all_to_all | solution.py:652
  67.9 271.4 %reduce-scatter.2.cloned.1.call-start = ((), (), s32[]{:S(2)}) async-start(), calls=%async_computation.7 | async-start | bytes 8192000 | tf_op jit(solution)/shard_map/reduce_scatter | solution.py:721
  68.0 27.4 %collective-permute-start.7 = (s32[1024]{0:T(1024)S(1)}, s32[1024]{0:T(1024)S(1)}, u32[]{:S(2)}, u32[]{:S(2)}) collective-permute-start(s32[1024]{0:T(1024)S(1)} %copy-done.9), channel_id=1, source_target_pairs={{0,4},{4,0},{8,12},{12,8},{16,20},{20,16},{24,28},{28,24},{32,36},... | collective-permute-start | bytes 12296 | tf_op jit(solution)/shard_map/ppermute | solution.py:696
  93.6 119.3 %copy-start = (f32[512,400]{0,1:T(8,128)S(1)}, f32[512,400]{0,1:T(8,128)}, u32[]{:S(2)}) copy-start(f32[512,400]{0,1:T(8,128)} %param.13) | copy-start | bytes 2457604
  96.8 4.9 collective-permute-start
  97.3 5.9 collective-permute-start.1
  101.3 3.9 collective-permute-start.2
  240.0 16.0 %collective-permute-start.8 = (f32[128,4,8,128]{3,2,1,0:T(8,128)}, f32[128,4,8,128]{3,2,1,0:T(8,128)S(1)}, u32[]{:S(2)}, u32[]{:S(2)}) collective-permute-start(f32[128,4,8,128]{3,2,1,0:T(8,128)} %get-tuple-element.89.grad_ref), channel_id=1, source_target_pairs={{0,4},{4,0},{8,12},{12,8},{16,20},{20,16},{24,28},{28,24},{32,36},... | collective-permute-start | bytes 6291464 | tf_op jit(solution)/shard_map/ppermute | solution.py:716
  256.0 1.4 copy-start.4
  272.9 355.9 %all-gather.3.cloned.1.call-start = ((), (), s32[]{:S(2)}) async-start(), calls=%async_computation.8 | async-start | bytes 13737984 | tf_op jit(solution)/shard_map/all_gather | solution.py:746
  340.7 12.4 %collective-permute-start.11 = (f32[4,25,8,128]{3,2,1,0:T(8,128)S(1)}, f32[4,25,8,128]{3,2,1,0:T(8,128)S(1)}, u32[]{:S(2)}, u32[]{:S(2)}) collective-permute-start(f32[4,25,8,128]{3,2,1,0:T(8,128)S(1)} %get-tuple-element.94), channel_id=1, source_target_pairs={{0,96},{4,100},{8,104},{12,108},{16,112},{20,116},{24,120},{28,124... | collective-permute-start | bytes 1228808 | tf_op jit(solution)/shard_map/ppermute | solution.py:732
  341.3 13.9 %collective-permute-start.10 = (f32[4,25,8,128]{3,2,1,0:T(8,128)S(1)}, f32[4,25,8,128]{3,2,1,0:T(8,128)S(1)}, u32[]{:S(2)}, u32[]{:S(2)}) collective-permute-start(f32[4,25,8,128]{3,2,1,0:T(8,128)S(1)} %get-tuple-element.95), channel_id=1, source_target_pairs={{0,64},{4,68},{8,72},{12,76},{16,80},{20,84},{24,88},{28,92},{32,9... | collective-permute-start | bytes 1228808 | tf_op jit(solution)/shard_map/ppermute | solution.py:732
  344.0 18.4 %collective-permute-start.9 = (f32[4,25,8,128]{3,2,1,0:T(8,128)S(1)}, f32[4,25,8,128]{3,2,1,0:T(8,128)S(1)}, u32[]{:S(2)}, u32[]{:S(2)}) collective-permute-start(f32[4,25,8,128]{3,2,1,0:T(8,128)S(1)} %get-tuple-element.93), channel_id=1, source_target_pairs={{0,32},{4,36},{8,40},{12,44},{16,48},{20,52},{24,56},{28,60},{32,6... | collective-permute-start | bytes 1228808 | tf_op jit(solution)/shard_map/ppermute | solution.py:732
  364.2 4.9 collective-permute-start.12
  365.7 7.2 %collective-permute-start.13 = (f32[25,8,128]{2,1,0:T(8,128)S(1)}, f32[25,8,128]{2,1,0:T(8,128)S(1)}, u32[]{:S(2)}, u32[]{:S(2)}) collective-permute-start(f32[25,8,128]{2,1,0:T(8,128)S(1)} %get-tuple-element.97), channel_id=1, source_target_pairs={{0,16},{4,20},{8,24},{12,28},{16,0},{20,4},{24,8},{28,12},{32,48},... | collective-permute-start | bytes 307208 | tf_op jit(solution)/shard_map/ppermute | solution.py:739
  366.7 6.4 collective-permute-start.14
  369.1 4.1 copy-start.6
  372.9 0.6 copy-start.7
  373.2 0.7 copy-start.8
  376.6 169.8 %all-to-all-start.4 = ((f32[32,72,8,128]{3,2,1,0:T(8,128)}), f32[32,72,8,128]{3,2,1,0:T(8,128)}, u32[]{:S(2)}, u32[]{:S(2)}) async-start(f32[32,72,8,128]{3,2,1,0:T(8,128)} %get-tuple-element.82), calls=%async_computation.4 | async-start | bytes 18874368 | tf_op jit(solution)/shard_map/all_to_all | solution.py:652
  583.1 42.5 %copy-start.1 = (f32[512,400]{0,1:T(8,128)S(1)}, f32[512,400]{0,1:T(8,128)}, u32[]{:S(2)}) copy-start(f32[512,400]{0,1:T(8,128)} %param.13) | copy-start | bytes 2457604
Sparse Core Ops, SparseCore 0:
  273.0 66.3 reduce-scatter.1
  376.7 163.2 all-gather.2

commit v6 on v5

--- a/solution.py
+++ b/solution.py
@@ -682,15 +682,14 @@
         end_owner.T, end_row.T, negative_owner.reshape(1, NEG), negative_row.reshape(8, 128)
     )
     wanted = exchange(request.reshape(GROUP, 2, 128), "rows")
-    left, right, _ = lax.optimization_barrier((left, right, wanted))
+    rel_rows = relation_table[relation_id]
+    left, right, _, rel_rows = lax.optimization_barrier((left, right, wanted, rel_rows))
     across_a = lax.ppermute(left[: WIDTH // 2], "rep", to_right)
     across_b = lax.ppermute(right[WIDTH // 2 :], "rep", to_left)
     tables = (table_t, right, across_a, across_b, left)
     wanted_rows = wanted.reshape(2 * GROUP, 128)
     looked = lookup(MAIN, 0, wanted_rows, tables)
-    arrived = exchange(looked, "rows")
     flag = any_device(jnp.max(wanted[:, 1, FLAG]).reshape(1))
-    over_now = flag[0] > 0
     core = rows_at & 1
     swap = [(r, r ^ 1) for r in range(GROUP)]
     other_id = lax.ppermute(relation_id, "rows", swap)
@@ -700,11 +699,16 @@
         near = jnp.where((near >= 0) & (near < SHARDS * 64), near, SHARDS * 64)
         return ((near >> 3) * 32 + (near & 7)).reshape(8, 128)
 
-    rel_rows = jnp.pad(relation_table[relation_id], ((0, 0), (0, 112)))
+    rel_rows = jnp.pad(rel_rows, ((0, 0), (0, 112)))
     my_places, other_places = places(relation_id), places(other_id)
     rel_rows, my_places, other_places = lax.optimization_barrier(
         (rel_rows, my_places, other_places)
     )
+    over_now = flag[0] > 0
+    looked, rel_rows, flag, over_now = lax.optimization_barrier(
+        (looked, rel_rows, flag, over_now)
+    )
+    arrived = exchange(looked, "rows")
     grads, rel_grads = lax.cond(
         over_now,
         lambda x: math(
@@ -726,10 +730,11 @@
     pieces = [
         lax.dynamic_index_in_dim(part, (y_at + k) & 3, 0, keepdims=False) for k in range(4)
     ]
-    part = pieces[0]
+    parts = [pieces[0]]
     for k in range(1, 4):
         ring = [(r, (r + 8 * k) % GROUP) for r in range(GROUP)]
-        part = part + lax.ppermute(pieces[k], "rows", ring)
+        parts.append(lax.ppermute(pieces[k], "rows", ring))
+    part = (parts[0] + parts[1]) + (parts[2] + parts[3])
     pieces = [
         lax.dynamic_index_in_dim(part, (z_at + k) & 3, 0, keepdims=False) for k in range(4)
     ]
@@ -737,6 +742,14 @@
     for k in range(1, 4):
         ring = [(r, r // 8 * 8 + (r + 2 * k) % 8) for r in range(GROUP)]
         parts.append(lax.ppermute(pieces[k], "rows", ring))
+    slots = wanted.reshape(GROUP, 256)
+
+    def ids(first, octets):
+        part = slots[:, first * 8 : (first + octets) * 8]
+        return part.reshape(GROUP // SUM_STEP, 1, SUM_STEP * octets * 8)
+
+    summed = row_sum(MAIN, ids(0, MAIN), incoming)
+    summed, parts = lax.optimization_barrier((summed, parts))
     new_shard = relation_update(
         (core * SHARDS + rep_at * 16 + (rows_at >> 1)).reshape(1),
         parts,
@@ -744,13 +757,6 @@
         relation_state.reshape(RELGROUPS, 128),
     )
     shards = lax.all_gather(new_shard, AXES, axis=0, tiled=False)
-    slots = wanted.reshape(GROUP, 256)
-
-    def ids(first, octets):
-        part = slots[:, first * 8 : (first + octets) * 8]
-        return part.reshape(GROUP // SUM_STEP, 1, SUM_STEP * octets * 8)
-
-    summed = row_sum(MAIN, ids(0, MAIN), incoming)
     summed = lax.cond(
         over_now,
         lambda x: x + row_sum(OVER, ids(MAIN, OVER), exchange(outgoing_over, "rows")),

time: 653 us -> 616 us (0.943)
  the two profiles are of different devices: /device:TPU:48 before, /device:TPU:1 now
where the time goes in v6:
time: 616 us; the launch traced here: 615 us
  waiting for transfers between devices  295 us (48%)
  Pallas kernels  141 us (23%)
  starting transfers between devices  80.3 us (13%)
  blocking collectives  46.2 us (8%)
  local copies, waits for them, and re-layouts  30.7 us (5%)
  between operations  16.9 us (3%)
    all_to_all x3, waiting for transfers between devices, exchange(): return lax.all_to_all(x, axis, split_axis=0, concat_axis=0, tiled=True)  125 us
    ppermute x6, waiting for transfers between devices, per_device(): parts.append(lax.ppermute(pieces[k], 'rows', ring))  78.7 us
    reduce_scatter x1, waiting for transfers between devices, per_device(): lax.psum_scatter(relation_grad.reshape(4, 16, 25, 8, 128), 'rep', scatter...  57.6 us
    all_to_all x1, blocking collectives, exchange(): return lax.all_to_all(x, axis, split_axis=0, concat_axis=0, tiled=True)  46.2 us
    all_to_all x3, starting transfers between devices, exchange(): return lax.all_to_all(x, axis, split_axis=0, concat_axis=0, tiled=True)  39.2 us
    pallas_call x1, Pallas kernels, row_sum(): pl.pallas_call(functools.partial(row_sum_kernel, octets), grid=(GROUP //...  35.8 us
    all_gather x1, waiting for transfers between devices, per_device(): shards = lax.all_gather(new_shard, AXES, axis=0, tiled=False)  29.2 us
    ppermute x6, starting transfers between devices, per_device(): parts.append(lax.ppermute(pieces[k], 'rows', ring))  27.2 us
  transfers between devices with their start and end apart: 20, of which 7 were waited for; matrix products, arithmetic and copies ran while one was open for 6% of the time, Pallas kernels for 10%

profile of v6, /device:TPU:1, one launch (start us, length us, event | category | flops | bytes accessed | tf_op | source)
XLA Modules:
  0.0 614.6 jit_solution(10277881427016847662)
XLA Ops:
  7.2 2.1 collective-permute-start
  9.3 1.4 collective-permute-start.1
  10.6 6.0 prep.1
  16.6 9.4 %all-to-all-start.2 = ((s32[32,2,128]{2,1,0:T(2,128)}), s32[32,2,128]{2,1,0:T(2,128)S(1)}, u32[]{:S(2)}, u32[]{:S(2)}) async-start(s32[32,2,128]{2,1,0:T(2,128)} %bitcast.64), calls=%async_computation.2 | async-start | bytes 65536 | tf_op jit(solution)/shard_map/all_to_all | solution.py:652
  26.1 1.3 add_bitcast_fusion.1
  27.4 14.1 %copy.14 = f32[7424,400]{1,0:T(8,128)} copy(f32[7424,400]{0,1:T(8,128)} %param.15) | data formatting | bytes 23756800 | tf_op args[2]
  41.5 10.6 %gather_fusion = f32[1024,400]{1,0:T(8,128)} fusion(f32[7424,400]{1,0:T(8,128)} %copy.14, s32[1024]{0:T(1024)S(1)} %get-tuple-element.121), kind=kCustom, calls=%fused_computation | custom fusion | bytes 3280896 | tf_op jit(solution)/shard_map/gather | solution.py:685
  52.1 0.1 collective-permute-start.2
  52.3 2.7 collective-permute-start.3
  55.0 0.8 collective-permute-start.4
  55.8 0.8 collective-permute-done.4
  56.6 0.6 add_bitcast_fusion.other_id_ref
  57.2 0.8 slice_reduce_fusion
  58.0 1.2 collective-permute-start.6
  59.3 1.4 collective-permute-start.7
  60.7 3.5 collective-permute-done.5
  66.8 1.8 pad.4
  68.7 17.9 %lookup.1 = f32[32,72,8,128]{3,2,1,0:T(8,128)} custom-call(s32[64,128]{1,0:T(8,128)S(1)} %bitcast.58, f32[400,512]{1,0:T(8,128)S(1)} %bitcast.53, f32[400,512]{1,0:T(8,128)} %copy-done.3, f32[200,512]{1,0:T(8,128)S(1)} %collective-permute-done.2.across_a, f32[200,512]{1,0:T(8,128)S(1)} %collective-permute-done.3.across_b, f32[400,512]{1,0:T(8,128)} %copy-done.2), custom_call_target="tpu_custom_call" | custom-call | tf_op jit(solution)/shard_map/lookup/pallas_call | solution.py:166
  86.6 8.0 %all-to-all-start.3 = ((f32[32,72,8,128]{3,2,1,0:T(8,128)}), f32[32,72,8,128]{3,2,1,0:T(8,128)}, u32[]{:S(2)}, u32[]{:S(2)}) async-start(f32[32,72,8,128]{3,2,1,0:T(8,128)} %lookup.1), calls=%async_computation.3 | async-start | bytes 18874368 | tf_op jit(solution)/shard_map/all_to_all | solution.py:652
  94.6 0.0 reduce-scatter.2.cloned.1.call-start
  94.7 125.1 %all-to-all-done.3 = f32[32,72,8,128]{3,2,1,0:T(8,128)} async-done(((f32[32,72,8,128]{3,2,1,0:T(8,128)}), f32[32,72,8,128]{3,2,1,0:T(8,128)}, u32[]{:S(2)}, u32[]{:S(2)}) %all-to-all-start.3) | async-done | bytes 9437216 | tf_op jit(solution)/shard_map/all_to_all | solution.py:652
  219.8 26.9 %conditional.2 = ((f32[384,4,8,128]{3,2,1,0:T(8,128)}, f32[128,4,8,128]{3,2,1,0:T(8,128)})) conditional(s32[]{:T(128)} %convert_element_type.6, (s32[24,128]{1,0:T(8,128)S(1)}, s32[1]{0:T(128)}, f32[32,72,8,128]{3,2,1,0:T(8,128)}, f32[1024,512]{1,0:T(8,128)S(1)}) %tuple.28, (s32[64,128]{1,0:T(8,128)S(1)}, f32[400,512]{1,0:T(8,128)S(1)}, ...), branch_computations={%region_1.2_spmd, %region_2.3_spmd} | conditional | bytes 4194312 | solution.py:712
  219.8 26.7 %math.2 = (f32[384,4,8,128]{3,2,1,0:T(8,128)}, f32[128,4,8,128]{3,2,1,0:T(8,128)}) custom-call(s32[24,128]{1,0:T(8,128)S(1)} %get-tuple-element.38.addr_ref, s32[1]{0:T(128)} %get-tuple-element.39.flag_ref, f32[32,72,8,128]{3,2,1,0:T(8,128)} %get-tuple-element.40.pay_ref.over_ref, f32[32,72,8,128]{3,2,1,0:T(8,128)} %get-tuple-element.40.pay_ref.over_ref, ...), custom_call_target="tpu_custom_call" | custom-call | tf_op jit(solution)/shard_map/cond/branch_0_fun/math/pallas_call | solution.py:285
  246.7 4.1 collective-permute-start.8
  250.9 15.9 %pack_grads.1 = (f32[32,72,8,128]{3,2,1,0:T(8,128)}, f32[32,16,8,128]{3,2,1,0:T(8,128)}) custom-call(s32[24,128]{1,0:T(8,128)S(1)} %get-tuple-element.92.addr_ref, s32[1]{0:T(128)} %max.11.flag_ref, f32[384,4,8,128]{3,2,1,0:T(8,128)} %get-tuple-element.96.grad_ref), custom_call_target="tpu_custom_call" | custom-call | tf_op jit(solution)/shard_map/pack_grads/pallas_call | solution.py:449
  266.8 1.4 copy-done.4
  268.1 16.1 %relation_sum.1 = f32[64,25,8,128]{3,2,1,0:T(8,128)} custom-call(s32[8,128]{1,0:T(8,128)} %get-tuple-element.98.id_ref, s32[8,128]{1,0:T(8,128)} %add_bitcast_fusion.other_id_ref, f32[128,4,8,128]{3,2,1,0:T(8,128)} %get-tuple-element.101.grad_ref, f32[128,4,8,128]{3,2,1,0:T(8,128)} %copy-done.4), custom_call_target="tpu_custom_call" | custom-call | tf_op jit(solution)/shard_map/relation_sum/pallas_call | solution.py:370
  284.2 21.8 %all-to-all-start.4 = ((f32[32,72,8,128]{3,2,1,0:T(8,128)}), f32[32,72,8,128]{3,2,1,0:T(8,128)}, u32[]{:S(2)}, u32[]{:S(2)}) async-start(f32[32,72,8,128]{3,2,1,0:T(8,128)} %get-tuple-element.97), calls=%async_computation.4 | async-start | bytes 18874368 | tf_op jit(solution)/shard_map/all_to_all | solution.py:652
  306.0 0.0 all-gather.3.cloned.1.call-start
  306.1 57.6 %reduce-scatter.2.cloned.1.call-done = f32[1,16,25,8,128]{4,3,2,1,0:T(8,128)} async-done(((f32[4,16,25,8,128]{4,3,2,1,0:T(8,128)}), f32[1,16,25,8,128]{4,3,2,1,0:T(8,128)}) %reduce-scatter.2.cloned.1.call-update) | async-done | bytes 1638416 | tf_op jit(solution)/shard_map/reduce_scatter | solution.py:725
  363.6 1.3 dynamic-slice_bitcast_fusion
  365.0 1.3 collective-permute-start.9
  366.2 2.5 collective-permute-start.10
  368.7 1.1 collective-permute-start.11
  369.8 69.9 %collective-permute-done.9 = f32[4,25,8,128]{3,2,1,0:T(8,128)S(1)} collective-permute-done((f32[4,25,8,128]{3,2,1,0:T(8,128)S(1)}, f32[4,25,8,128]{3,2,1,0:T(8,128)S(1)}, u32[]{:S(2)}, u32[]{:S(2)}) %collective-permute-start.9) | collective-permute-done | bytes 409632 | tf_op jit(solution)/shard_map/ppermute | solution.py:736
  439.7 8.8 %collective-permute-done.10 = f32[4,25,8,128]{3,2,1,0:T(8,128)S(1)} collective-permute-done((f32[4,25,8,128]{3,2,1,0:T(8,128)S(1)}, f32[4,25,8,128]{3,2,1,0:T(8,128)S(1)}, u32[]{:S(2)}, u32[]{:S(2)}) %collective-permute-start.10) | collective-permute-done | bytes 409632 | tf_op jit(solution)/shard_map/ppermute | solution.py:736
  448.5 1.1 fusion.1
  449.6 0.7 dynamic-slice_bitcast_fusion.3
  450.3 19.9 %collective-permute-start.12 = (f32[25,8,128]{2,1,0:T(8,128)}, f32[25,8,128]{2,1,0:T(8,128)}, u32[]{:S(2)}, u32[]{:S(2)}) collective-permute-start(f32[25,8,128]{2,1,0:T(8,128)} %get-tuple-element.118), channel_id=1, source_target_pairs={{0,8},{4,12},{8,16},{12,20},{16,24},{20,28},{24,0},{28,4},{32,40},... | collective-permute-start | bytes 307208 | tf_op jit(solution)/shard_map/ppermute | solution.py:744
  470.2 2.4 collective-permute-start.14
  472.6 0.7 reshape.76.wanted_ref
  473.3 35.8 %row_sum.1 = f32[4,400,512]{2,1,0:T(8,128)S(1)} custom-call(s32[4,1,1472]{2,1,0:T(1,128)} %reshape.76.wanted_ref, f32[32,72,8,128]{3,2,1,0:T(8,128)} %all-to-all-done.4.pay_ref), custom_call_target="tpu_custom_call" | custom-call | tf_op jit(solution)/shard_map/row_sum/pallas_call | solution.py:521
  509.2 2.8 relation_update.1
  512.0 0.8 fusion
  512.9 46.2 %all_to_all.29.grad_ref = f32[4,400,512]{2,1,0:T(8,128)} all-to-all(f32[4,400,512]{2,1,0:T(8,128)S(1)} %fusion), channel_id=1, replica_groups=mesh['rows'=32,'rep'=4] {'rep'}, dimensions={0} | all-to-all | bytes 6553600 | tf_op jit(solution)/shard_map/all_to_all | solution.py:652
  559.0 3.2 entity_update.1
  562.2 29.2 %all-gather.3.cloned.1.call-done = f32[3328,8,128]{2,1,0:T(8,128)} async-done(((f32[26,8,128]{2,1,0:T(8,128)}), f32[3328,8,128]{2,1,0:T(8,128)}) %all-gather.3.cloned.1.call-update) | async-done | bytes 13631504 | tf_op jit(solution)/shard_map/all_gather | solution.py:759
  591.5 16.3 %unpack.1 = (f32[400,7424]{1,0:T(8,128)}, f32[58,128]{1,0:T(8,128)}) custom-call(f32[16,2,4,26,8,128]{5,4,3,2,1,0:T(8,128)} %bitcast.50), custom_call_target="tpu_custom_call" | custom-call | tf_op jit(solution)/shard_map/unpack/pallas_call | solution.py:630
  (34 shorter events, 0.2 us)
Async XLA Ops:
  7.2 44.9 %collective-permute-start = (f32[400,512]{1,0:T(8,128)}, f32[400,512]{1,0:T(8,128)S(1)}, u32[]{:S(2)}, u32[]{:S(2)}) collective-permute-start(f32[400,512]{1,0:T(8,128)} %bitcast.51), channel_id=1, source_target_pairs={{0,1},{1,2},{2,3},{3,0},{4,5},{5,6},{6,7},{7,4},{8,9},{9,10},{10,1... | collective-permute-start | bytes 2457608 | tf_op jit(solution)/shard_map/ppermute | solution.py:677
  9.3 42.8 %collective-permute-start.1 = (f32[400,512]{1,0:T(8,128)}, f32[400,512]{1,0:T(8,128)S(1)}, u32[]{:S(2)}, u32[]{:S(2)}) collective-permute-start(f32[400,512]{1,0:T(8,128)} %bitcast.52), channel_id=1, source_target_pairs={{0,3},{1,0},{2,1},{3,2},{4,7},{5,4},{6,5},{7,6},{8,11},{9,8},{10,9... | collective-permute-start | bytes 2457608 | tf_op jit(solution)/shard_map/ppermute | solution.py:678
  16.6 35.4 %all-to-all-start.2 = ((s32[32,2,128]{2,1,0:T(2,128)}), s32[32,2,128]{2,1,0:T(2,128)S(1)}, u32[]{:S(2)}, u32[]{:S(2)}) async-start(s32[32,2,128]{2,1,0:T(2,128)} %bitcast.64), calls=%async_computation.2 | async-start | bytes 65536 | tf_op jit(solution)/shard_map/all_to_all | solution.py:652
  41.5 13.5 %copy-start.6 = (s32[1024]{0:T(1024)S(1)}, s32[1024]{0:T(1024)}, u32[]{:S(2)}) copy-start(s32[1024]{0:T(1024)} %param.19) | copy-start | bytes 12292
  52.1 16.6 %copy-start = (f32[512,400]{0,1:T(8,128)S(1)}, f32[512,400]{0,1:T(8,128)}, u32[]{:S(2)}) copy-start(f32[512,400]{0,1:T(8,128)} %param.13) | copy-start | bytes 2457604
  52.1 14.7 %copy-start.2 = (f32[400,512]{1,0:T(8,128)}, f32[400,512]{1,0:T(8,128)S(1)}, u32[]{:S(2)}) copy-start(f32[400,512]{1,0:T(8,128)S(1)} %collective-permute-done.left) | copy-start | bytes 2457604
  52.1 14.7 %copy-start.3 = (f32[400,512]{1,0:T(8,128)}, f32[400,512]{1,0:T(8,128)S(1)}, u32[]{:S(2)}) copy-start(f32[400,512]{1,0:T(8,128)S(1)} %collective-permute-done.1.right) | copy-start | bytes 2457604
  52.1 16.5 %collective-permute-start.2 = (f32[200,512]{1,0:T(8,128)S(1)}, f32[200,512]{1,0:T(8,128)S(1)}, u32[]{:S(2)}, u32[]{:S(2)}) collective-permute-start(f32[200,512]{1,0:T(8,128)S(1)} %slice.15), channel_id=1, source_target_pairs={{0,1},{1,2},{2,3},{3,0},{4,5},{5,6},{6,7},{7,4},{8,9},{9,10},{10,1... | collective-permute-start | bytes 1228808 | tf_op jit(solution)/shard_map/ppermute | solution.py:687
  52.3 16.4 %collective-permute-start.3 = (f32[200,512]{1,0:T(8,128)S(1)}, f32[200,512]{1,0:T(8,128)S(1)}, u32[]{:S(2)}, u32[]{:S(2)}) collective-permute-start(f32[200,512]{1,0:T(8,128)S(1)} %slice.16), channel_id=1, source_target_pairs={{0,3},{1,0},{2,1},{3,2},{4,7},{5,4},{6,5},{7,6},{8,11},{9,8},{10,9... | collective-permute-start | bytes 1228808 | tf_op jit(solution)/shard_map/ppermute | solution.py:688
  55.0 1.6 collective-permute-start.4
  58.0 6.2 %collective-permute-start.5 = (s32[1]{0:T(128)}, s32[1]{0:T(128)}, u32[]{:S(2)}, u32[]{:S(2)}) collective-permute-start(s32[1]{0:T(128)} %bitcast.10), channel_id=1, source_target_pairs={{0,1},{1,2},{2,3},{3,0},{4,5},{5,6},{6,7},{7,4},{8,9},{9,10},{10,1... | collective-permute-start | bytes 20 | tf_op jit(solution)/shard_map/ppermute | solution.py:658
  58.0 7.5 %collective-permute-start.6 = (s32[1]{0:T(128)}, s32[1]{0:T(128)}, u32[]{:S(2)}, u32[]{:S(2)}) collective-permute-start(s32[1]{0:T(128)} %bitcast.10), channel_id=1, source_target_pairs={{0,2},{1,3},{2,0},{3,1},{4,6},{5,7},{6,4},{7,5},{8,10},{9,11},{10,... | collective-permute-start | bytes 20 | tf_op jit(solution)/shard_map/ppermute | solution.py:658
  59.3 6.9 %collective-permute-start.7 = (s32[1]{0:T(128)}, s32[1]{0:T(128)}, u32[]{:S(2)}, u32[]{:S(2)}) collective-permute-start(s32[1]{0:T(128)} %bitcast.10), channel_id=1, source_target_pairs={{0,3},{1,0},{2,1},{3,2},{4,7},{5,4},{6,5},{7,6},{8,11},{9,8},{10,9... | collective-permute-start | bytes 20 | tf_op jit(solution)/shard_map/ppermute | solution.py:658
  68.6 17.9 %copy-start.5 = (f32[200,512]{1,0:T(8,128)}, f32[200,512]{1,0:T(8,128)S(1)}, u32[]{:S(2)}) copy-start(f32[200,512]{1,0:T(8,128)S(1)} %collective-permute-done.3.across_b) | copy-start | bytes 1228804
  86.6 133.2 %all-to-all-start.3 = ((f32[32,72,8,128]{3,2,1,0:T(8,128)}), f32[32,72,8,128]{3,2,1,0:T(8,128)}, u32[]{:S(2)}, u32[]{:S(2)}) async-start(f32[32,72,8,128]{3,2,1,0:T(8,128)} %lookup.1), calls=%async_computation.3 | async-start | bytes 18874368 | tf_op jit(solution)/shard_map/all_to_all | solution.py:652
  94.6 269.0 %reduce-scatter.2.cloned.1.call-start = ((), (), s32[]{:S(2)}) async-start(), calls=%async_computation.7 | async-start | bytes 8192000 | tf_op jit(solution)/shard_map/reduce_scatter | solution.py:725
  246.7 20.1 %collective-permute-start.8 = (f32[128,4,8,128]{3,2,1,0:T(8,128)}, f32[128,4,8,128]{3,2,1,0:T(8,128)S(1)}, u32[]{:S(2)}, u32[]{:S(2)}) collective-permute-start(f32[128,4,8,128]{3,2,1,0:T(8,128)} %get-tuple-element.101.grad_ref), channel_id=1, source_target_pairs={{0,4},{4,0},{8,12},{12,8},{16,20},{20,16},{24,28},{28,24},{32,36},... | collective-permute-start | bytes 6291464 | tf_op jit(solution)/shard_map/ppermute | solution.py:720
  266.8 1.4 copy-start.4
  284.2 189.1 %all-to-all-start.4 = ((f32[32,72,8,128]{3,2,1,0:T(8,128)}), f32[32,72,8,128]{3,2,1,0:T(8,128)}, u32[]{:S(2)}, u32[]{:S(2)}) async-start(f32[32,72,8,128]{3,2,1,0:T(8,128)} %get-tuple-element.97), calls=%async_computation.4 | async-start | bytes 18874368 | tf_op jit(solution)/shard_map/all_to_all | solution.py:652
  306.0 285.5 %all-gather.3.cloned.1.call-start = ((), (), s32[]{:S(2)}) async-start(), calls=%async_computation.8 | async-start | bytes 13737984 | tf_op jit(solution)/shard_map/all_gather | solution.py:759
  365.0 74.8 %collective-permute-start.9 = (f32[4,25,8,128]{3,2,1,0:T(8,128)S(1)}, f32[4,25,8,128]{3,2,1,0:T(8,128)S(1)}, u32[]{:S(2)}, u32[]{:S(2)}) collective-permute-start(f32[4,25,8,128]{3,2,1,0:T(8,128)S(1)} %get-tuple-element.115), channel_id=1, source_target_pairs={{0,32},{4,36},{8,40},{12,44},{16,48},{20,52},{24,56},{28,60},{32,6... | collective-permute-start | bytes 1228808 | tf_op jit(solution)/shard_map/ppermute | solution.py:736
  366.2 82.3 %collective-permute-start.10 = (f32[4,25,8,128]{3,2,1,0:T(8,128)S(1)}, f32[4,25,8,128]{3,2,1,0:T(8,128)S(1)}, u32[]{:S(2)}, u32[]{:S(2)}) collective-permute-start(f32[4,25,8,128]{3,2,1,0:T(8,128)S(1)} %get-tuple-element.114), channel_id=1, source_target_pairs={{0,64},{4,68},{8,72},{12,76},{16,80},{20,84},{24,88},{28,92},{32,9... | collective-permute-start | bytes 1228808 | tf_op jit(solution)/shard_map/ppermute | solution.py:736
  368.7 79.8 %collective-permute-start.11 = (f32[4,25,8,128]{3,2,1,0:T(8,128)S(1)}, f32[4,25,8,128]{3,2,1,0:T(8,128)S(1)}, u32[]{:S(2)}, u32[]{:S(2)}) collective-permute-start(f32[4,25,8,128]{3,2,1,0:T(8,128)S(1)} %get-tuple-element.113), channel_id=1, source_target_pairs={{0,96},{4,100},{8,104},{12,108},{16,112},{20,116},{24,120},{28,124... | collective-permute-start | bytes 1228808 | tf_op jit(solution)/shard_map/ppermute | solution.py:736
  450.3 58.9 %collective-permute-start.12 = (f32[25,8,128]{2,1,0:T(8,128)}, f32[25,8,128]{2,1,0:T(8,128)}, u32[]{:S(2)}, u32[]{:S(2)}) collective-permute-start(f32[25,8,128]{2,1,0:T(8,128)} %get-tuple-element.118), channel_id=1, source_target_pairs={{0,8},{4,12},{8,16},{12,20},{16,24},{20,28},{24,0},{28,4},{32,40},... | collective-permute-start | bytes 307208 | tf_op jit(solution)/shard_map/ppermute | solution.py:744
  470.2 39.0 %collective-permute-start.13 = (f32[25,8,128]{2,1,0:T(8,128)}, f32[25,8,128]{2,1,0:T(8,128)}, u32[]{:S(2)}, u32[]{:S(2)}) collective-permute-start(f32[25,8,128]{2,1,0:T(8,128)} %get-tuple-element.117), channel_id=1, source_target_pairs={{0,16},{4,20},{8,24},{12,28},{16,0},{20,4},{24,8},{28,12},{32,48},... | collective-permute-start | bytes 307208 | tf_op jit(solution)/shard_map/ppermute | solution.py:744
  470.2 39.0 %collective-permute-start.14 = (f32[25,8,128]{2,1,0:T(8,128)S(1)}, f32[25,8,128]{2,1,0:T(8,128)}, u32[]{:S(2)}, u32[]{:S(2)}) collective-permute-start(f32[25,8,128]{2,1,0:T(8,128)S(1)} %get-tuple-element.116), channel_id=1, source_target_pairs={{0,24},{4,28},{8,0},{12,4},{16,8},{20,12},{24,16},{28,20},{32,56},... | collective-permute-start | bytes 307208 | tf_op jit(solution)/shard_map/ppermute | solution.py:744
  512.9 46.2 %copy-start.1 = (f32[512,400]{0,1:T(8,128)S(1)}, f32[512,400]{0,1:T(8,128)}, u32[]{:S(2)}) copy-start(f32[512,400]{0,1:T(8,128)} %param.13) | copy-start | bytes 2457604
Sparse Core Ops, SparseCore 0:
  284.4 79.2 reduce-scatter.1
  512.1 79.3 all-gather.2
